TPU v7x, 32 devices: a whole 2x2x4 slice. The times are simulated.
32 devices in a mesh: dp: 8 (over z, y), mp: 4 (over x, core).
Axes of the slice: x: 2, y: 2, z: 4, core: 2. Of those that a mesh axis runs over, the one named last changes fastest.
Arguments:
- tokens: bfloat16 [8192, 2048], P('dp'), may hold values from -6 to 6
- out_cot: bfloat16 [8192, 2048], P('dp'), may hold values from -23 to 23
- lengths: int32 [8], P('dp'), may hold values from 1 to 1024, 6144 in all
- seq_family: int32 [8, 1], P('dp'), may hold values from 0 to 3
- family_tokens: int32 [4], replicated, may hold values from 100000 to 3999999
- norm_master: float32 [2048, 6], P('dp'), may hold values from -0.5 to 2.4, as said below
- attn_bias_master: float32 [2, 2048], P(None, 'mp'), may hold values from -2 to 2
- qkv_master: float32 [2048, 3, 2048], P('dp', None, 'mp'), may hold values from -0.125 to 0.125
- proj_master: float32 [2048, 2048], P('dp', 'mp'), may hold values from -1.5 to 1.5
- fc_bias_master: float32 [8192], P('mp'), may hold values from -1.5 to 1.5
- fc_master: float32 [2048, 8192], P('dp', 'mp'), may hold values from -0.125 to 0.125
- down_master: float32 [2048, 8192], P('dp', 'mp'), may hold values from -0.0625 to 0.0625
- norm_moment: float32 [2048, 6], P('dp'), may hold values from -0.0008544922 to 0.0008544922
- attn_bias_moment: float32 [2, 2048], P(None, 'mp'), may hold values from -0.0008544922 to 0.0008544922
- qkv_moment: float32 [2048, 3, 2048], P('dp', None, 'mp'), may hold values from -0.0008544922 to 0.0008544922
- proj_moment: float32 [2048, 2048], P('dp', 'mp'), may hold values from -0.0008544922 to 0.0008544922
- fc_bias_moment: float32 [8192], P('mp'), may hold values from -0.0008544922 to 0.0008544922
- fc_moment: float32 [2048, 8192], P('dp', 'mp'), may hold values from -0.0008544922 to 0.0008544922
- down_moment: float32 [2048, 8192], P('dp', 'mp'), may hold values from -0.0008544922 to 0.0008544922
- norm_average: float32 [2048, 6], P('dp'), may hold values from 0.5 to 1.5
- attn_bias_average: float32 [2, 2048], P(None, 'mp'), may hold values from -2 to 2
- qkv_average: float32 [2048, 3, 2048], P('dp', None, 'mp'), may hold values from -0.125 to 0.125
- proj_average: float32 [2048, 2048], P('dp', 'mp'), may hold values from -1.5 to 1.5
- fc_bias_average: float32 [8192], P('mp'), may hold values from -1.5 to 1.5
- fc_average: float32 [2048, 8192], P('dp', 'mp'), may hold values from -0.125 to 0.125
- down_average: float32 [2048, 8192], P('dp', 'mp'), may hold values from -0.0625 to 0.0625
Outputs:
- block_out: bfloat16 [8192, 2048], P('dp')
- input_grad: float32 [8192, 2048], P('dp')
- norm_grad: float32 [2048, 6], P('dp')
- attn_bias_grad: float32 [2, 2048], P(None, 'mp')
- qkv_grad: float32 [2048, 3, 2048], P('dp', None, 'mp')
- proj_grad: float32 [2048, 2048], P('dp', 'mp')
- fc_bias_grad: float32 [8192], P('mp')
- fc_grad: float32 [2048, 8192], P('dp', 'mp')
- down_grad: float32 [2048, 8192], P('dp', 'mp')
- norm_momentum: float32 [2048, 6], P('dp')
- attn_bias_momentum: float32 [2, 2048], P(None, 'mp')
- qkv_momentum: float32 [2048, 3, 2048], P('dp', None, 'mp')
- proj_momentum: float32 [2048, 2048], P('dp', 'mp')
- fc_bias_momentum: float32 [8192], P('mp')
- fc_momentum: float32 [2048, 8192], P('dp', 'mp')
- down_momentum: float32 [2048, 8192], P('dp', 'mp')
- norm_averaged: float32 [2048, 6], P('dp')
- attn_bias_averaged: float32 [2, 2048], P(None, 'mp')
- qkv_averaged: float32 [2048, 3, 2048], P('dp', None, 'mp')
- proj_averaged: float32 [2048, 2048], P('dp', 'mp')
- fc_bias_averaged: float32 [8192], P('mp')
- fc_averaged: float32 [2048, 8192], P('dp', 'mp')
- down_averaged: float32 [2048, 8192], P('dp', 'mp')
- norm_updated: float32 [2048, 6], P('dp')
- attn_bias_updated: float32 [2, 2048], P(None, 'mp')
- qkv_updated: float32 [2048, 3, 2048], P('dp', None, 'mp')
- proj_updated: float32 [2048, 2048], P('dp', 'mp')
- fc_bias_updated: float32 [8192], P('mp')
- fc_updated: float32 [2048, 8192], P('dp', 'mp')
- down_updated: float32 [2048, 8192], P('dp', 'mp')
- norm_copy: bfloat16 [2048, 6], P('dp')
- attn_bias_copy: bfloat16 [2, 2048], P(None, 'mp')
- qkv_copy: bfloat16 [2048, 3, 2048], P('dp', None, 'mp')
- proj_copy: bfloat16 [2048, 2048], P('dp', 'mp')
- fc_bias_copy: bfloat16 [8192], P('mp')
- fc_copy: bfloat16 [2048, 8192], P('dp', 'mp')
- down_copy: bfloat16 [2048, 8192], P('dp', 'mp')
- grad_norm: float32 [], replicated
Inputs may be any that keep to these rules, and one draw needn't show every extreme that they name: `lengths`: they sum to 6144; the longest is 1024. `seq_family`: every family has a sequence. `norm_master`: gains positive, biases of either sign.
All inputs are finite; a program needn't handle non-finite values. No bound on the sum of `lengths` on one device may be relied on, other than what follows from the above.
Results may differ from a plain program's by a relative error of at most 0.012.
The roundings to bfloat16 on the way count: a program that leaves them out, or rounds other values in their place, can miss the bound.
Values may be sent and summed in bfloat16 or wider, within the bound.
A program may use at most 256 MiB of HBM per device.

v0:
```python
import math

import jax
import jax.numpy as jnp
from jax import lax
from jax.sharding import PartitionSpec as P

HEAD_DIM = 128
LEN = 1024


EPS = 1e-05
MOMENTUM = 0.9
RATE = 192.0
KEEP = 0.9
NEG = -1e30


def layer_norm(value, gain, shift):
    centre = jnp.mean(value, axis=-1, keepdims=True)
    centred = value - centre
    spread = jnp.mean(centred * centred, axis=-1, keepdims=True)
    return centred * lax.rsqrt(spread + EPS) * gain + shift


def gelu_tanh(value):
    return (
        0.5
        * value
        * (1.0 + jnp.tanh(0.7978845608028654 * (value + 0.044715 * value * value * value)))
    )


def local(
    tokens,
    out_cot,
    lengths,
    seq_family,
    family_tokens,
    norm_master,
    attn_bias_master,
    qkv_master,
    proj_master,
    fc_bias_master,
    fc_master,
    down_master,
    norm_moment,
    attn_bias_moment,
    qkv_moment,
    proj_moment,
    fc_bias_moment,
    fc_moment,
    down_moment,
    norm_average,
    attn_bias_average,
    qkv_average,
    proj_average,
    fc_bias_average,
    fc_average,
    down_average,
):
    seq_count = lengths.shape[0]
    row_count = tokens.shape[0]
    seq_len = row_count // seq_count
    family_count = family_tokens.shape[0]
    local_heads = qkv_master.shape[2] // HEAD_DIM
    head_width = qkv_master.shape[2]
    scale = 1.0 / math.sqrt(HEAD_DIM)
    mp_count = lax.axis_size("mp")
    dp_count = lax.axis_size("dp")

    def sum_over_mp(term_fn):
        summed = lax.psum(term_fn(0, row_count), "mp")
        return summed

    family_ids = jnp.arange(family_count, dtype=jnp.int32)
    member = seq_family == family_ids[None, :]
    local_counts = jnp.sum(jnp.where(member, lengths[:, None], 0), axis=0).astype(jnp.float32)
    counts = lax.psum(local_counts, "dp")
    valid_total = jnp.sum(counts)
    share = family_tokens.astype(jnp.float32) / jnp.sum(family_tokens).astype(jnp.float32)
    family_weight = share * valid_total / jnp.maximum(counts, float(LEN // 2))
    seq_weight = jnp.sum(jnp.where(member, family_weight[None, :], 0.0), axis=1)
    places = jnp.arange(seq_len, dtype=jnp.int32)
    token_weight = jnp.where(places[None, :] < lengths[:, None], seq_weight[:, None], 0.0).reshape(
        row_count
    )
    causal = places[:, None] >= places[None, :]
    low_norm = norm_master.astype(jnp.bfloat16)
    low_qkv = qkv_master.astype(jnp.bfloat16)
    low_proj = proj_master.astype(jnp.bfloat16)
    low_fc = fc_master.astype(jnp.bfloat16)
    low_down = down_master.astype(jnp.bfloat16)
    w_qkv, w_proj, w_fc, w_down, w_norm = (
        lax.all_gather(low_qkv, "dp", axis=0, tiled=True),
        lax.all_gather(low_proj, "dp", axis=0, tiled=True),
        lax.all_gather(low_fc, "dp", axis=0, tiled=True),
        lax.all_gather(low_down, "dp", axis=0, tiled=True),
        lax.all_gather(low_norm, "dp", axis=0, tiled=True),
    )
    norm_full = w_norm.astype(jnp.float32)
    bias_rows = jnp.stack(
        [attn_bias_master[0], jnp.zeros_like(attn_bias_master[0]), attn_bias_master[1]], axis=0
    )
    x_in = tokens.astype(jnp.float32)
    ln1_low = layer_norm(x_in, norm_full[:, 0], norm_full[:, 1]).astype(jnp.bfloat16)
    qkv = (
        jnp.einsum("td,dce->tce", ln1_low, w_qkv, preferred_element_type=jnp.float32)
        + bias_rows[None]
    )
    qkv = qkv.astype(jnp.bfloat16)
    heads = qkv.reshape(seq_count, seq_len, 3, local_heads, HEAD_DIM)

    def attend(one_seq):
        query_rows = one_seq[:, 0]
        key_rows = one_seq[:, 1]
        value_rows = one_seq[:, 2]
        scores = (
            jnp.einsum("qhd,khd->hqk", query_rows, key_rows, preferred_element_type=jnp.float32)
            * scale
        )
        scores = jnp.where(causal[None], scores, NEG)
        row_top = jnp.max(scores, axis=-1, keepdims=True)
        log_total = row_top + jnp.log(jnp.sum(jnp.exp(scores - row_top), axis=-1, keepdims=True))
        attn_prob = jnp.exp(scores - log_total).astype(jnp.bfloat16)
        mixed = jnp.einsum(
            "hqk,khd->qhd", attn_prob, value_rows, preferred_element_type=jnp.float32
        )
        return (mixed.astype(jnp.bfloat16), log_total)

    mixed_low, log_kept = lax.map(attend, heads)
    mixed_low = mixed_low.reshape(row_count, head_width)

    def attn_term(start, count):
        return jnp.einsum("te,de->td", mixed_low, w_proj, preferred_element_type=jnp.float32)

    residual_part = x_in + sum_over_mp(attn_term) + norm_full[:, 4]
    ln2_part, ln2_back = jax.vjp(layer_norm, residual_part, norm_full[:, 2], norm_full[:, 3])
    ln2_low = ln2_part.astype(jnp.bfloat16)
    pre_act = (
        jnp.einsum("td,df->tf", ln2_low, w_fc, preferred_element_type=jnp.float32)
        + fc_bias_master[None]
    )
    hidden_act, gelu_back = jax.vjp(gelu_tanh, pre_act)
    hidden_low = hidden_act.astype(jnp.bfloat16)

    def mlp_term(start, count):
        return jnp.einsum("tf,df->td", hidden_low, w_down, preferred_element_type=jnp.float32)

    block_part = (residual_part + sum_over_mp(mlp_term) + norm_full[:, 5]).astype(jnp.bfloat16)
    upstream = token_weight[:, None] * out_cot.astype(jnp.float32)
    upstream_low = upstream.astype(jnp.bfloat16)
    down_sum = jnp.einsum("td,tf->df", upstream_low, hidden_low, preferred_element_type=jnp.float32)
    back_act = jnp.einsum("td,df->tf", upstream_low, w_down, preferred_element_type=jnp.float32)
    back_pre = gelu_back(back_act)[0].astype(jnp.bfloat16)
    fc_bias_sum = jnp.sum(back_pre, axis=0, dtype=jnp.float32)
    fc_sum = jnp.einsum("td,tf->df", ln2_low, back_pre, preferred_element_type=jnp.float32)

    def fc_back_term(start, count):
        return jnp.einsum("tf,df->td", back_pre, w_fc, preferred_element_type=jnp.float32)

    back_ln2 = sum_over_mp(fc_back_term)
    back_resid_part, gain2_sum, shift2_sum = ln2_back(back_ln2)
    back_resid_part = upstream + back_resid_part
    back_attn_low = back_resid_part.astype(jnp.bfloat16)
    proj_sum = jnp.einsum("td,te->de", back_attn_low, mixed_low, preferred_element_type=jnp.float32)
    back_mixed = jnp.einsum(
        "td,de->te", back_attn_low, w_proj, preferred_element_type=jnp.float32
    ).astype(jnp.bfloat16)
    back_mixed = back_mixed.reshape(seq_count, seq_len, local_heads, HEAD_DIM)

    def attend_back(items):
        one_seq, log_total, back_seq = items
        query_rows = one_seq[:, 0]
        key_rows = one_seq[:, 1]
        value_rows = one_seq[:, 2]
        scores = (
            jnp.einsum("qhd,khd->hqk", query_rows, key_rows, preferred_element_type=jnp.float32)
            * scale
        )
        scores = jnp.where(causal[None], scores, NEG)
        attn_prob = jnp.exp(scores - log_total)
        prob_low = attn_prob.astype(jnp.bfloat16)
        back_value = jnp.einsum(
            "hqk,qhd->khd", prob_low, back_seq, preferred_element_type=jnp.float32
        )
        back_prob = jnp.einsum(
            "qhd,khd->hqk", back_seq, value_rows, preferred_element_type=jnp.float32
        )
        back_score = attn_prob * (
            back_prob - jnp.sum(attn_prob * back_prob, axis=-1, keepdims=True)
        )
        back_score = back_score.astype(jnp.bfloat16)
        back_query = (
            jnp.einsum("hqk,khd->qhd", back_score, key_rows, preferred_element_type=jnp.float32)
            * scale
        )
        back_key = (
            jnp.einsum("hqk,qhd->khd", back_score, query_rows, preferred_element_type=jnp.float32)
            * scale
        )
        return jnp.stack([back_query, back_key, back_value], axis=1).astype(jnp.bfloat16)

    back_heads = lax.map(attend_back, (heads, log_kept, back_mixed))
    back_qkv = back_heads.reshape(row_count, 3, head_width)
    attn_bias_sum = jnp.sum(back_qkv[:, 0::2], axis=0, dtype=jnp.float32)
    qkv_sum = jnp.einsum("td,tce->dce", ln1_low, back_qkv, preferred_element_type=jnp.float32)

    def qkv_back_term(start, count):
        return jnp.einsum("tce,dce->td", back_qkv, w_qkv, preferred_element_type=jnp.float32)

    back_ln1 = sum_over_mp(qkv_back_term)
    ln1_again, ln1_back = jax.vjp(layer_norm, x_in, norm_full[:, 0], norm_full[:, 1])
    back_input, gain1_sum, shift1_sum = ln1_back(back_ln1)
    whole = back_resid_part + back_input
    norm_part = jnp.stack(
        [
            gain1_sum,
            shift1_sum,
            gain2_sum,
            shift2_sum,
            jnp.sum(back_resid_part, axis=0),
            jnp.sum(upstream, axis=0),
        ],
        axis=1,
    )
    qkv_reduced, proj_reduced, fc_reduced, down_reduced, norm_reduced = (
        lax.psum_scatter(qkv_sum, "dp", scatter_dimension=0, tiled=True),
        lax.psum_scatter(proj_sum, "dp", scatter_dimension=0, tiled=True),
        lax.psum_scatter(fc_sum, "dp", scatter_dimension=0, tiled=True),
        lax.psum_scatter(down_sum, "dp", scatter_dimension=0, tiled=True),
        lax.psum_scatter(norm_part, "dp", scatter_dimension=0, tiled=True),
    )
    attn_bias_reduced, fc_bias_reduced = lax.psum((attn_bias_sum, fc_bias_sum), "dp")
    raw_grads = [
        reduced / valid_total
        for reduced in (
            norm_reduced,
            attn_bias_reduced,
            qkv_reduced,
            proj_reduced,
            fc_bias_reduced,
            fc_reduced,
            down_reduced,
        )
    ]
    local_squares = jnp.sum(raw_grads[0] * raw_grads[0]) / float(mp_count)
    local_squares = local_squares + jnp.sum(raw_grads[1] * raw_grads[1]) / float(dp_count)
    local_squares = local_squares + jnp.sum(raw_grads[4] * raw_grads[4]) / float(dp_count)
    for grad_raw in (raw_grads[2], raw_grads[3], raw_grads[5], raw_grads[6]):
        local_squares = local_squares + jnp.sum(grad_raw * grad_raw)
    squares = lax.psum(local_squares, ("dp", "mp"))
    grad_norm = jnp.sqrt(squares)
    clip_factor = jnp.minimum(1.0, 1.0 / (grad_norm + 1e-06))
    masters = (
        norm_master,
        attn_bias_master,
        qkv_master,
        proj_master,
        fc_bias_master,
        fc_master,
        down_master,
    )
    moments = (
        norm_moment,
        attn_bias_moment,
        qkv_moment,
        proj_moment,
        fc_bias_moment,
        fc_moment,
        down_moment,
    )
    averages = (
        norm_average,
        attn_bias_average,
        qkv_average,
        proj_average,
        fc_bias_average,
        fc_average,
        down_average,
    )
    grads_out = []
    momenta_out = []
    averaged_out = []
    updated_out = []
    copies_out = []
    for master, moment, average, grad_raw in zip(masters, moments, averages, raw_grads):
        clipped = grad_raw * clip_factor
        momentum = MOMENTUM * moment + clipped
        updated = master - RATE * (clipped + MOMENTUM * momentum)
        averaged = KEEP * average + (1.0 - KEEP) * updated
        grads_out.append(clipped)
        momenta_out.append(momentum)
        averaged_out.append(averaged)
        updated_out.append(updated)
        copies_out.append(updated.astype(jnp.bfloat16))
    return (
        block_part,
        whole,
        grads_out[0],
        grads_out[1],
        grads_out[2],
        grads_out[3],
        grads_out[4],
        grads_out[5],
        grads_out[6],
        momenta_out[0],
        momenta_out[1],
        momenta_out[2],
        momenta_out[3],
        momenta_out[4],
        momenta_out[5],
        momenta_out[6],
        averaged_out[0],
        averaged_out[1],
        averaged_out[2],
        averaged_out[3],
        averaged_out[4],
        averaged_out[5],
        averaged_out[6],
        updated_out[0],
        updated_out[1],
        updated_out[2],
        updated_out[3],
        updated_out[4],
        updated_out[5],
        updated_out[6],
        copies_out[0],
        copies_out[1],
        copies_out[2],
        copies_out[3],
        copies_out[4],
        copies_out[5],
        copies_out[6],
        grad_norm,
    )


def solution(mesh):
    placed = (
        P("dp", None),
        P("dp", None),
        P("dp"),
        P("dp", None),
        P(),
        P("dp", None),
        P(None, "mp"),
        P("dp", None, "mp"),
        P("dp", "mp"),
        P("mp"),
        P("dp", "mp"),
        P("dp", "mp"),
        P("dp", None),
        P(None, "mp"),
        P("dp", None, "mp"),
        P("dp", "mp"),
        P("mp"),
        P("dp", "mp"),
        P("dp", "mp"),
        P("dp", None),
        P(None, "mp"),
        P("dp", None, "mp"),
        P("dp", "mp"),
        P("mp"),
        P("dp", "mp"),
        P("dp", "mp"),
    )
    return jax.shard_map(
        local,
        mesh=mesh,
        in_specs=placed,
        out_specs=(
            P("dp", None),
            P("dp", None),
            P("dp", None),
            P(None, "mp"),
            P("dp", None, "mp"),
            P("dp", "mp"),
            P("mp"),
            P("dp", "mp"),
            P("dp", "mp"),
            P("dp", None),
            P(None, "mp"),
            P("dp", None, "mp"),
            P("dp", "mp"),
            P("mp"),
            P("dp", "mp"),
            P("dp", "mp"),
            P("dp", None),
            P(None, "mp"),
            P("dp", None, "mp"),
            P("dp", "mp"),
            P("mp"),
            P("dp", "mp"),
            P("dp", "mp"),
            P("dp", None),
            P(None, "mp"),
            P("dp", None, "mp"),
            P("dp", "mp"),
            P("mp"),
            P("dp", "mp"),
            P("dp", "mp"),
            P("dp", None),
            P(None, "mp"),
            P("dp", None, "mp"),
            P("dp", "mp"),
            P("mp"),
            P("dp", "mp"),
            P("dp", "mp"),
            P(),
        ),
        check_vma=False,
    )
```

profile of v0, /device:TPU:0, one launch (start us, length us, event | category | flops | bytes accessed | tf_op | source)
XLA Modules:
  0.0 2152.3 jit_solution(12280135592228971859)
XLA Ops:
  15.6 3.4 fusion.15
  19.1 32.9 %all_gather.15 = bf16[2048,6]{0,1:T(8,128)(2,1)S(1)} all-gather(bf16[256,6]{0,1:T(8,128)(2,1)S(1)} %convert_element_type.108), channel_id=1, replica_groups=mesh['dp'=8,'mp'=4] {'dp'}, dimensions={0}, use_global_device_ids=true | all-gather | bytes 27648 | tf_op jit(solution)/shard_map/all_gather | solution.py:99
  52.7 61.0 %all-gather.5.cloned.1.call-done = bf16[2048,3,512]{0,2,1:T(8,128)(2,1)} async-done(((bf16[256,3,512]{0,2,1:T(8,128)(2,1)}), bf16[2048,3,512]{0,2,1:T(8,128)(2,1)}) %all-gather.5.cloned.1.call-update) | async-done | bytes 6291472 | tf_op jit(solution)/shard_map/all_gather | solution.py:95
  113.7 11.1 add_convert_fusion.2
  124.9 3.3 fusion
  128.3 3.7 exponential_reduce_fusion
  134.0 6.5 convolution_convert_fusion.1
  140.5 23.5 %all-gather.7.cloned.1.call-done = bf16[2048,512]{1,0:T(8,128)(2,1)} async-done(((bf16[256,512]{1,0:T(8,128)(2,1)}), bf16[2048,512]{1,0:T(8,128)(2,1)}) %all-gather.7.cloned.1.call-update) | async-done | bytes 2097168 | tf_op jit(solution)/shard_map/all_gather | solution.py:96
  164.0 7.4 fusion.66
  174.3 3.2 convert_element_type.120
  178.8 18.5 psum.58
  201.1 121.8 %all-reduce.6.cloned.1.call-done = f32[1024,2048]{1,0:T(8,128)} async-done(((f32[1024,2048]{1,0:T(8,128)}), f32[1024,2048]{1,0:T(8,128)}) %all-reduce.6.cloned.1.call-update) | async-done | bytes 8388624 | tf_op jit(solution)/shard_map/psum | solution.py:73
  322.9 5.8 fusion.62
  328.7 3.3 copy-done
  333.0 117.6 %all-gather.9.cloned.1.call-done = bf16[2048,2048]{1,0:T(8,128)(2,1)} async-done(((bf16[256,2048]{1,0:T(8,128)(2,1)}), bf16[2048,2048]{1,0:T(8,128)(2,1)}) %all-gather.9.cloned.1.call-update) | async-done | bytes 8388624 | tf_op jit(solution)/shard_map/all_gather | solution.py:97
  450.6 15.9 fusion.51
  466.5 109.8 %all-gather.11.cloned.1.call-done = bf16[2048,2048]{1,0:T(8,128)(2,1)} async-done(((bf16[256,2048]{1,0:T(8,128)(2,1)}), bf16[2048,2048]{1,0:T(8,128)(2,1)}) %all-gather.11.cloned.1.call-update) | async-done | bytes 8388624 | tf_op jit(solution)/shard_map/all_gather | solution.py:98
  576.3 21.0 convert_reduce_fusion.1
  599.2 11.1 fusion.67
  610.3 18.3 fusion.49
  628.6 132.9 %all-reduce.8.cloned.1.call-done = f32[1024,2048]{1,0:T(8,128)} async-done(((f32[1024,2048]{1,0:T(8,128)}), f32[1024,2048]{1,0:T(8,128)}) %all-reduce.8.cloned.1.call-update) | async-done | bytes 8388624 | tf_op jit(solution)/shard_map/psum | solution.py:73
  761.5 7.5 multiply_reduce_fusion.1
  769.7 5.0 fusion.61
  774.7 6.3 fusion.33
  781.1 9.7 convolution_convert_fusion
  790.7 12.6 multiply_reduce_fusion
  803.3 12.1 multiply_convert_fusion
  823.1 11.0 convolution_bitcast_fusion
  835.3 9.5 fusion.23
  844.9 278.3 %all-reduce.10.cloned.1.call-done = (f32[1024,2048]{1,0:T(8,128)}, f32[1024,2048]{1,0:T(8,128)}) async-done(((f32[1024,2048]{1,0:T(8,128)}, f32[1024,2048]{1,0:T(8,128)}), (f32[1024,2048]{1,0:T(8,128)}, f32[1024,2048]{1,0:T(8,128)})) %all-reduce.10.cloned.1.call-update) | async-done | bytes 16777232 | tf_op jit(solution)/shard_map/psum | solution.py:73
  1123.3 6.4 fusion.53
  1131.6 3.9 fusion.10
  1135.5 10.2 fusion.20
  1146.7 13.6 fusion.36
  1161.0 16.4 fusion.50
  1177.7 17.1 fusion.27
  1195.5 37.8 %all-reduce = (f32[2,512]{1,0:T(2,128)S(1)}, f32[2048]{0:T(1024)S(1)}) all-reduce(f32[2,512]{1,0:T(2,128)S(1)} %convert_reduce_fusion.2, f32[2048]{0:T(1024)S(1)} %copy-done.48), channel_id=1, replica_groups=mesh['dp'=8,'mp'=4] {'dp'}, use_global_device_ids=true, to_apply=%region_28.29 | all-reduce | flops 3072 | bytes 24576 | tf_op jit(solution)/shard_map/psum | solution.py:234
  1239.6 41.7 %reduce-scatter.6.cloned.1.call-done = f32[256,6]{0,1:T(8,128)} async-done(((f32[2048,6]{0,1:T(8,128)}), f32[256,6]{0,1:T(8,128)}) %reduce-scatter.6.cloned.1.call-update) | async-done | bytes 6160 | tf_op jit(solution)/shard_map/reduce_scatter | solution.py:232
  1283.9 208.1 %reduce-scatter.8.cloned.1.call-done = f32[256,3,512]{2,0,1:T(8,128)} async-done(((f32[2048,3,512]{2,0,1:T(8,128)}), f32[256,3,512]{2,0,1:T(8,128)}) %reduce-scatter.8.cloned.1.call-update) | async-done | bytes 1572880 | tf_op jit(solution)/shard_map/reduce_scatter | solution.py:228
  1496.3 280.9 %reduce-scatter.12.cloned.1.call-done = f32[256,2048]{1,0:T(8,128)} async-done(((f32[2048,2048]{1,0:T(8,128)}), f32[256,2048]{1,0:T(8,128)}) %reduce-scatter.12.cloned.1.call-update) | async-done | bytes 2097168 | tf_op jit(solution)/shard_map/reduce_scatter | solution.py:230
  1777.2 3.4 multiply_reduce_fusion.5
  1781.3 281.4 %reduce-scatter.14.cloned.1.call-done = f32[256,2048]{1,0:T(8,128)} async-done(((f32[2048,2048]{1,0:T(8,128)}), f32[256,2048]{1,0:T(8,128)}) %reduce-scatter.14.cloned.1.call-update) | async-done | bytes 2097168 | tf_op jit(solution)/shard_map/reduce_scatter | solution.py:231
  2062.7 3.4 multiply_reduce_fusion.4
  2066.9 10.2 add_convert_fusion
  2077.0 39.2 %psum.63 = f32[]{:T(128)} all-reduce(f32[]{:T(128)S(6)} %add.249), channel_id=1, replica_groups=mesh['dp'=8,'mp'=4] {'dp','mp'}, use_global_device_ids=true, to_apply=%region_41.42 | all-reduce | flops 1 | bytes 8 | tf_op jit(solution)/shard_map/psum | solution.py:252
  2122.0 3.2 fusion.57
  2127.5 5.9 fusion.58
  2135.1 5.1 fusion.54
  (190 shorter events, 57.0 us)
Async XLA Ops:
  7.2 11.8 copy-start.40
  7.2 106.5 %all-gather.5.cloned.1.call-start = ((), (), s32[]{:S(2)}) async-start(), calls=%async_computation.5 | async-start | bytes 7077888 | tf_op jit(solution)/shard_map/all_gather | solution.py:95
  9.9 154.1 %all-gather.7.cloned.1.call-start = ((), (), s32[]{:S(2)}) async-start(), calls=%async_computation.6 | async-start | bytes 2359296 | tf_op jit(solution)/shard_map/all_gather | solution.py:96
  11.7 311.2 %all-reduce.6.cloned.1.call-start = ((), (), s32[]{:S(2)}) async-start(), calls=%async_computation.7 | async-start | bytes 16777216 | tf_op jit(solution)/shard_map/psum | solution.py:73
  15.6 109.2 %copy-start.28 = (f32[1024]{0:T(1024)}, f32[1024]{0:T(1024)S(1)}, u32[]{:S(2)}) copy-start(f32[1024]{0:T(1024)S(1)} %broadcast_multiply_fusion.8) | copy-start | bytes 12292
  19.0 105.8 %copy-start.32 = (f32[1024]{0:T(1024)}, f32[1024]{0:T(1024)S(1)}, u32[]{:S(2)}) copy-start(f32[1024]{0:T(1024)S(1)} %fusion.15) | copy-start | bytes 12292
  19.1 105.8 %copy-start.30 = (f32[1024]{0:T(1024)}, f32[1024]{0:T(1024)S(1)}, u32[]{:S(2)}) copy-start(f32[1024]{0:T(1024)S(1)} %fusion.42) | copy-start | bytes 12292
  52.6 72.3 %copy-start.26 = (f32[2048,1]{0,1:T(1,128)}, f32[2048,1]{0,1:T(1,128)S(1)}, u32[]{:S(2)}) copy-start(f32[2048,1]{0,1:T(1,128)S(1)} %get-tuple-element.123) | copy-start | bytes 24580
  52.6 72.3 %copy-start.46 = (f32[2048,1]{0,1:T(1,128)}, f32[2048,1]{0,1:T(1,128)S(1)}, u32[]{:S(2)}) copy-start(f32[2048,1]{0,1:T(1,128)S(1)} %get-tuple-element.124) | copy-start | bytes 24580
  52.6 398.0 %copy-start.44 = (f32[2048,1]{0,1:T(1,128)}, f32[2048,1]{0,1:T(1,128)S(1)}, u32[]{:S(2)}) copy-start(f32[2048,1]{0,1:T(1,128)S(1)} %get-tuple-element.121) | copy-start | bytes 24580
  140.4 31.0 %copy-start.56 = (bf16[4,128,1024]{2,1,0:T(8,128)(2,1)}, bf16[4,128,1024]{2,1,0:T(8,128)(2,1)S(1)}, u32[]{:S(2)}) copy-start(bf16[4,128,1024]{2,1,0:T(8,128)(2,1)S(1)} %convolution_convert_fusion.1) | copy-start | bytes 3145732
  171.4 25.9 %copy-start.54 = (s32[4]{0:T(128)S(1)}, s32[4]{0:T(128)}, u32[]{:S(2)}) copy-start(s32[4]{0:T(128)} %param.30) | copy-start | bytes 52
  171.4 279.2 %all-gather.9.cloned.1.call-start = ((), (), s32[]{:S(2)}) async-start(), calls=%async_computation.8 | async-start | bytes 9437184 | tf_op jit(solution)/shard_map/all_gather | solution.py:97
  174.2 402.1 %all-gather.11.cloned.1.call-start = ((), (), s32[]{:S(2)}) async-start(), calls=%async_computation.9 | async-start | bytes 9437184 | tf_op jit(solution)/shard_map/all_gather | solution.py:98
  177.5 584.0 %all-reduce.8.cloned.1.call-start = ((), (), s32[]{:S(2)}) async-start(), calls=%async_computation.10 | async-start | bytes 16777216 | tf_op jit(solution)/shard_map/psum | solution.py:73
  450.6 125.7 %copy-start.49 = (f32[2048]{0:T(1024)S(1)}, f32[2048]{0:T(1024)}, u32[]{:S(2)}) copy-start(f32[2048]{0:T(1024)} %param.35) | copy-start | bytes 24580
  576.3 22.9 %copy-start.55 = (bf16[2048,2048]{1,0:T(8,128)(2,1)S(1)}, bf16[2048,2048]{1,0:T(8,128)(2,1)}, u32[]{:S(2)}) copy-start(bf16[2048,2048]{1,0:T(8,128)(2,1)} %all-gather.9.cloned.1.call-done) | copy-start | bytes 25165828
  610.3 513.0 %all-reduce.10.cloned.1.call-start = ((), (), s32[]{:S(2)}) async-start(), calls=%async_computation.16 | async-start | bytes 33554432 | tf_op jit(solution)/shard_map/psum | solution.py:73
  834.1 289.2 %copy-start.27 = (f32[2048,1]{0,1:T(1,128)S(1)}, f32[2048,1]{0,1:T(1,128)}, u32[]{:S(2)}) copy-start(f32[2048,1]{0,1:T(1,128)} %copy-done.26) | copy-start | bytes 24580
  834.1 289.1 %copy-start.29 = (f32[1024]{0:T(1024)S(1)}, f32[1024]{0:T(1024)}, u32[]{:S(2)}) copy-start(f32[1024]{0:T(1024)} %copy-done.28) | copy-start | bytes 12292
  834.1 403.0 %reduce-scatter.10.cloned.1.call-start = ((), (), s32[]{:S(2)}) async-start(), calls=%async_computation.13 | async-start | bytes 4718592 | tf_op jit(solution)/shard_map/reduce_scatter | solution.py:229
  844.8 284.8 %copy-start.33 = (f32[1024]{0:T(1024)S(1)}, f32[1024]{0:T(1024)}, u32[]{:S(2)}) copy-start(f32[1024]{0:T(1024)} %copy-done.32) | copy-start | bytes 12292
  844.8 284.8 %copy-start.31 = (f32[1024]{0:T(1024)S(1)}, f32[1024]{0:T(1024)}, u32[]{:S(2)}) copy-start(f32[1024]{0:T(1024)} %copy-done.30) | copy-start | bytes 12292
  844.9 436.4 %reduce-scatter.6.cloned.1.call-start = ((), (), s32[]{:S(2)}) async-start(), calls=%async_computation.11 | async-start | bytes 73728 | tf_op jit(solution)/shard_map/reduce_scatter | solution.py:232
  1135.5 11.2 copy-start.17
  1135.5 11.2 copy-start.47
  1146.5 345.5 %reduce-scatter.8.cloned.1.call-start = ((), (), s32[]{:S(2)}) async-start(), calls=%async_computation.12 | async-start | bytes 14155776 | tf_op jit(solution)/shard_map/reduce_scatter | solution.py:228
  1160.3 616.9 %reduce-scatter.12.cloned.1.call-start = ((), (), s32[]{:S(2)}) async-start(), calls=%async_computation.14 | async-start | bytes 18874368 | tf_op jit(solution)/shard_map/reduce_scatter | solution.py:230
  1177.4 885.3 %reduce-scatter.14.cloned.1.call-start = ((), (), s32[]{:S(2)}) async-start(), calls=%async_computation.15 | async-start | bytes 18874368 | tf_op jit(solution)/shard_map/reduce_scatter | solution.py:231
  1194.8 871.9 %copy-start.34 = (f32[2048,1]{0,1:T(1,128)S(1)}, f32[2048,1]{0,1:T(1,128)}, u32[]{:S(2)}) copy-start(f32[2048,1]{0,1:T(1,128)} %get-tuple-element.119) | copy-start | bytes 24580
  2066.7 50.2 %copy-start.50 = (f32[2048]{0:T(1024)S(1)}, f32[2048]{0:T(1024)}, u32[]{:S(2)}) copy-start(f32[2048]{0:T(1024)} %param.42) | copy-start | bytes 24580
  2066.8 51.6 %copy-start.41 = (f32[2,512]{1,0:T(2,128)S(1)}, f32[2,512]{1,0:T(2,128)}, u32[]{:S(2)}) copy-start(f32[2,512]{1,0:T(2,128)} %param.32) | copy-start | bytes 12292
  2066.8 51.6 %copy-start.53 = (f32[2,512]{1,0:T(2,128)S(1)}, f32[2,512]{1,0:T(2,128)}, u32[]{:S(2)}) copy-start(f32[2,512]{1,0:T(2,128)} %param.39) | copy-start | bytes 12292
  2066.8 52.2 %copy-start.52 = (f32[2,512]{1,0:T(2,128)S(1)}, f32[2,512]{1,0:T(2,128)}, u32[]{:S(2)}) copy-start(f32[2,512]{1,0:T(2,128)} %param.46) | copy-start | bytes 12292
  2066.8 52.7 %copy-start.42 = (f32[2048]{0:T(1024)S(1)}, f32[2048]{0:T(1024)}, u32[]{:S(2)}) copy-start(f32[2048]{0:T(1024)} %param.49) | copy-start | bytes 24580
  2066.8 53.3 %copy-start.37 = (f32[256,6]{0,1:T(8,128)S(1)}, f32[256,6]{0,1:T(8,128)}, u32[]{:S(2)}) copy-start(f32[256,6]{0,1:T(8,128)} %param.31) | copy-start | bytes 18436
  2066.8 53.3 %copy-start.38 = (f32[256,6]{0,1:T(8,128)S(1)}, f32[256,6]{0,1:T(8,128)}, u32[]{:S(2)}) copy-start(f32[256,6]{0,1:T(8,128)} %reduce-scatter.6.cloned.1.call-done) | copy-start | bytes 18436
  2066.8 53.3 %copy-start.51 = (f32[256,6]{0,1:T(8,128)S(1)}, f32[256,6]{0,1:T(8,128)}, u32[]{:S(2)}) copy-start(f32[256,6]{0,1:T(8,128)} %param.38) | copy-start | bytes 18436
  2066.8 54.6 %copy-start.43 = (f32[256,6]{0,1:T(8,128)S(1)}, f32[256,6]{0,1:T(8,128)}, u32[]{:S(2)}) copy-start(f32[256,6]{0,1:T(8,128)} %param.45) | copy-start | bytes 18436
  2066.9 60.6 %copy-start.12 = (f32[256,3,512]{2,0,1:T(8,128)S(1)}, f32[256,3,512]{2,0,1:T(8,128)}, u32[]{:S(2)}) copy-start(f32[256,3,512]{2,0,1:T(8,128)} %param.33) | copy-start | bytes 4718596
  2066.9 60.6 %copy-start.13 = (f32[256,3,512]{2,0,1:T(8,128)S(1)}, f32[256,3,512]{2,0,1:T(8,128)}, u32[]{:S(2)}) copy-start(f32[256,3,512]{2,0,1:T(8,128)} %reduce-scatter.8.cloned.1.call-done) | copy-start | bytes 4718596
  2116.9 16.5 copy-start.25
  2118.3 16.7 copy-start.35
  2118.9 16.1 copy-start.39
  2121.4 13.7 copy-start.36
  2125.3 15.0 copy-start.22
  2125.3 9.8 copy-start.11
  2125.3 9.8 copy-start.23
  (23 other events, 132.8 us)
Sparse Core Ops, SparseCore 0:
  10.7 102.9 all-gather.4
  116.4 47.5 all-gather.6
  171.5 151.3 all-reduce.5
  325.5 125.0 all-gather.8
  453.1 123.1 all-gather.10
  610.4 151.0 all-reduce.7
  834.2 288.9 all-reduce.9
  1127.5 88.2 reduce-scatter.9
  1220.1 61.1 reduce-scatter.5
  1285.1 206.7 reduce-scatter.7
  1496.2 280.9 reduce-scatter.11
  1780.9 281.7 reduce-scatter.13
where the time goes:
time: 2160 us; the launch traced here: 2150 us
  waiting for transfers between devices  1660 us (77%)
  matrix products  195 us (9%)
  other arithmetic  128 us (6%)
  blocking collectives  128 us (6%)
  between operations  23.6 us (1%)
    psum x3, waiting for transfers between devices, sum_over_mp(): summed = lax.psum(term_fn(0, row_count), 'mp')  533 us
    reduce_scatter x1, waiting for transfers between devices, local(): lax.psum_scatter(down_sum, 'dp', scatter_dimension=0, tiled=True)  281 us
    reduce_scatter x1, waiting for transfers between devices, local(): lax.psum_scatter(fc_sum, 'dp', scatter_dimension=0, tiled=True)  281 us
    reduce_scatter x1, waiting for transfers between devices, local(): lax.psum_scatter(qkv_sum, 'dp', scatter_dimension=0, tiled=True)  208 us
    all_gather x1, waiting for transfers between devices, local(): lax.all_gather(low_fc, 'dp', axis=0, tiled=True)  118 us
    all_gather x1, waiting for transfers between devices, local(): lax.all_gather(low_down, 'dp', axis=0, tiled=True)  110 us
    all_gather x1, waiting for transfers between devices, local(): lax.all_gather(low_qkv, 'dp', axis=0, tiled=True)  61 us
  transfers between devices with their start and end apart: 12, of which 11 were waited for; matrix products, arithmetic and copies ran while one was open for 8% of the time, Pallas kernels for 0%

commit v1 on v0

v1 whole, which is shorter than its diff:
```python
import math

import jax
import jax.numpy as jnp
from jax import lax
from jax.sharding import PartitionSpec as P

HEAD_DIM = 128
LEN = 1024


EPS = 1e-05
MOMENTUM = 0.9
RATE = 192.0
KEEP = 0.9
NEG = -1e30
BF16 = jnp.bfloat16
F32 = jnp.float32


def dot_f32(eq, left, right):
    return jnp.einsum(eq, left, right, preferred_element_type=F32)


def after(value, *gates):
    return lax.optimization_barrier((value, *gates))[0]


def swap(value, axis, flip):
    size = lax.axis_size(axis)
    return lax.ppermute(value, axis, [(i, i ^ flip) for i in range(size)])


def turn(value, steps):
    size = lax.axis_size("dp")
    outer = size // 2
    pairs = [(i, ((i // 2 + steps) % outer) * 2 + i % 2) for i in range(size)]
    return lax.ppermute(value, "dp", pairs)


def tree_sum(value, axis):
    bits = lax.axis_size(axis).bit_length() - 1
    low = 0
    while low < bits:
        span = min(3, bits - low)
        parts = [value] + [swap(value, axis, k << low) for k in range(1, 1 << span)]
        while len(parts) > 1:
            parts = [parts[i] + parts[i + 1] for i in range(0, len(parts), 2)]
        value = parts[0]
        low += span
    return value


def norm_stats(value):
    centre = jnp.mean(value, axis=-1, keepdims=True)
    centred = value - centre
    spread = jnp.mean(centred * centred, axis=-1, keepdims=True)
    inverse = lax.rsqrt(spread + EPS)
    return centred * inverse, inverse


def gelu_parts(value):
    inner = 0.7978845608028654 * (value + 0.044715 * value * value * value)
    return jnp.tanh(inner)


def gelu_tanh(value):
    return 0.5 * value * (1.0 + gelu_parts(value))


def gelu_slope(value):
    tanh = gelu_parts(value)
    rise = 0.7978845608028654 * (1.0 + 3.0 * 0.044715 * value * value)
    return 0.5 * (1.0 + tanh) + 0.5 * value * (1.0 - tanh * tanh) * rise


def local(
    tokens,
    out_cot,
    lengths,
    seq_family,
    family_tokens,
    norm_master,
    attn_bias_master,
    qkv_master,
    proj_master,
    fc_bias_master,
    fc_master,
    down_master,
    norm_moment,
    attn_bias_moment,
    qkv_moment,
    proj_moment,
    fc_bias_moment,
    fc_moment,
    down_moment,
    norm_average,
    attn_bias_average,
    qkv_average,
    proj_average,
    fc_bias_average,
    fc_average,
    down_average,
):
    seq_count = lengths.shape[0]
    row_count = tokens.shape[0]
    seq_len = row_count // seq_count
    family_count = family_tokens.shape[0]
    depth, _, head_width = qkv_master.shape
    local_heads = head_width // HEAD_DIM
    scale = 1.0 / math.sqrt(HEAD_DIM)
    mp_count = lax.axis_size("mp")
    dp_count = lax.axis_size("dp")
    outer = dp_count // 2
    place = lax.axis_index("dp")
    place_out, place_in = place // 2, place % 2
    side = lax.axis_index("mp") % 2
    half = row_count // 2

    def block_at(s, r):
        return ((place_out + (outer - r)) % outer) * 2 + (place_in + s) % 2

    def to_local(value):
        parts = [
            lax.dynamic_slice_in_dim(value, block_at(s, r) * depth, depth, 1)
            for s in range(2)
            for r in range(outer)
        ]
        return jnp.concatenate(parts, axis=1)

    def to_global(value):
        parts = []
        for b in range(dp_count):
            s = (b % 2 + place_in) % 2
            r = (place_out + outer - b // 2) % outer
            parts.append(lax.dynamic_slice_in_dim(value, (s * outer + r) * depth, depth, 1))
        return jnp.concatenate(parts, axis=1)

    def own_rows(value):
        return lax.dynamic_slice_in_dim(value, side * half, half, 0)

    def other_rows(value):
        return lax.dynamic_slice_in_dim(value, (1 - side) * half, half, 0)

    def halves_swapped(own, other):
        return jnp.where(
            side == 0,
            jnp.concatenate([own, other], axis=0),
            jnp.concatenate([other, own], axis=0),
        )

    def gather(shard, gate=None, axis=0):
        if gate is not None:
            shard = after(shard, *gate)
        near = [shard] + [turn(shard, r) for r in range(1, outer)]
        far = [swap(part, "dp", 1) for part in near]
        return jnp.concatenate(near + far, axis=axis), near[1:]

    low_norm = norm_master.astype(BF16).T
    low_qkv = qkv_master.astype(BF16).reshape(depth, 3 * head_width)
    low_proj = proj_master.astype(BF16)
    low_fc = fc_master.astype(BF16)
    low_down = down_master.astype(BF16)

    w_norm, _ = gather(low_norm, axis=1)
    w_qkv, gate_qkv = gather(low_qkv)
    w_proj, gate_proj = gather(low_proj, gate_qkv[:1])
    w_fc, gate_fc = gather(low_fc, gate_qkv)
    w_down, _ = gather(low_down, gate_fc)

    family_ids = jnp.arange(family_count, dtype=jnp.int32)
    member = seq_family == family_ids[None, :]
    local_counts = jnp.sum(jnp.where(member, lengths[:, None], 0), axis=0).astype(F32)
    counts = tree_sum(local_counts, "dp")
    valid_total = jnp.sum(counts)
    share = family_tokens.astype(F32) / jnp.sum(family_tokens).astype(F32)
    family_weight = share * valid_total / jnp.maximum(counts, float(LEN // 2))
    seq_weight = jnp.sum(jnp.where(member, family_weight[None, :], 0.0), axis=1)
    places = jnp.arange(seq_len, dtype=jnp.int32)
    token_weight = jnp.where(places[None, :] < lengths[:, None], seq_weight[:, None], 0.0).reshape(
        row_count
    )
    causal = places[:, None] >= places[None, :]

    norm_full = w_norm.astype(F32)
    gain1, shift1, gain2, shift2, bias_p, bias_d = [norm_full[i][None] for i in range(6)]
    bias_row = jnp.concatenate(
        [attn_bias_master[0], jnp.zeros_like(attn_bias_master[0]), attn_bias_master[1]], axis=0
    )
    x_low = to_local(tokens)
    cot_low = to_local(out_cot)

    x_hat, _ = norm_stats(x_low.astype(F32))
    ln1_low = (x_hat * gain1 + shift1).astype(BF16)
    qkv = (dot_f32("td,de->te", ln1_low, w_qkv) + bias_row[None]).astype(BF16)
    heads = qkv.reshape(seq_count, seq_len, 3, local_heads, HEAD_DIM)

    def attend(one_seq):
        query_rows = one_seq[:, 0]
        key_rows = one_seq[:, 1]
        value_rows = one_seq[:, 2]
        scores = dot_f32("qhd,khd->hqk", query_rows, key_rows) * scale
        scores = jnp.where(causal[None], scores, NEG)
        row_top = jnp.max(scores, axis=-1, keepdims=True)
        log_total = row_top + jnp.log(jnp.sum(jnp.exp(scores - row_top), axis=-1, keepdims=True))
        attn_prob = jnp.exp(scores - log_total).astype(BF16)
        mixed = dot_f32("hqk,khd->qhd", attn_prob, value_rows)
        return (mixed.astype(BF16), log_total)

    mixed_low, log_kept = lax.map(attend, heads)
    mixed_low = mixed_low.reshape(row_count, head_width)
    mixed_low = halves_swapped(mixed_low[:half], mixed_low[half:])

    def sum_over_mp(product, left):
        other = swap(product(left[half:]).astype(BF16), "mp", 1)
        part = (product(left[:half]) + other.astype(F32)).astype(BF16)
        flip = 2
        while flip < mp_count:
            part = part.astype(F32) + swap(part, "mp", flip).astype(F32)
            flip *= 2
            if flip < mp_count:
                part = part.astype(BF16)
        return part.astype(F32)

    x_own = own_rows(x_low).astype(F32)
    attn_out = sum_over_mp(lambda rows: dot_f32("te,de->td", rows, w_proj), mixed_low)
    residual = x_own + attn_out + bias_p
    hat2, inverse2 = norm_stats(residual)
    ln2_own = (hat2 * gain2 + shift2).astype(BF16)
    ln2_low = jnp.concatenate([ln2_own, swap(ln2_own, "mp", 1)], axis=0)
    pre_act = dot_f32("td,df->tf", ln2_low, w_fc) + fc_bias_master[None]
    hidden_low = gelu_tanh(pre_act).astype(BF16)

    weight_own, weight_other = own_rows(token_weight), other_rows(token_weight)
    upstream = weight_own[:, None] * own_rows(cot_low).astype(F32)
    upstream_other = weight_other[:, None] * other_rows(cot_low).astype(F32)
    upstream_low = jnp.concatenate([upstream, upstream_other], axis=0).astype(BF16)

    def reduce_grad(left, right, group):
        total = None
        for first in range(0, outer, group):
            count = min(group, outer - first)

            def block(s):
                start = (s * outer + first) * depth
                return dot_f32("td,tf->df", left[:, start : start + count * depth], right)

            given = swap(block(1).astype(BF16), "dp", 1)
            part = block(0) + given.astype(F32)
            for r in range(first, first + count):
                piece = part[(r - first) * depth : (r - first + 1) * depth]
                if r:
                    piece = turn(piece.astype(BF16), -r).astype(F32)
                total = piece if total is None else total + piece
        return total

    down_reduced = reduce_grad(upstream_low, hidden_low, 1)

    mlp_out = sum_over_mp(lambda rows: dot_f32("tf,df->td", rows, w_down), hidden_low)
    block_own = (residual + mlp_out + bias_d).astype(BF16)
    block_part = to_global(halves_swapped(block_own, swap(block_own, "mp", 1)))

    back_act = dot_f32("td,df->tf", upstream_low, w_down)
    back_pre = (back_act * gelu_slope(pre_act)).astype(BF16)
    fc_bias_sum = jnp.sum(back_pre, axis=0, dtype=F32)
    fc_reduced = reduce_grad(ln2_low, back_pre, 1)

    def norm_back(back, hat, inverse, gain):
        scaled = back * gain
        mean = jnp.mean(scaled, axis=-1, keepdims=True)
        slope = jnp.mean(scaled * hat, axis=-1, keepdims=True)
        return inverse * (scaled - mean - hat * slope)

    back_ln2 = sum_over_mp(lambda rows: dot_f32("tf,df->td", rows, w_fc), back_pre)
    gain2_sum = jnp.sum(back_ln2 * hat2, axis=0)
    shift2_sum = jnp.sum(back_ln2, axis=0)
    back_resid = upstream + norm_back(back_ln2, hat2, inverse2, gain2)
    ga_own = back_resid.astype(BF16)
    ga_low = jnp.concatenate([ga_own, swap(ga_own, "mp", 1)], axis=0)
    proj_reduced = reduce_grad(ga_low, mixed_low, outer)
    back_mixed = dot_f32("td,de->te", ga_low, w_proj).astype(BF16)
    back_mixed = halves_swapped(back_mixed[:half], back_mixed[half:])
    back_mixed = back_mixed.reshape(seq_count, seq_len, local_heads, HEAD_DIM)

    def attend_back(items):
        one_seq, log_total, back_seq = items
        query_rows = one_seq[:, 0]
        key_rows = one_seq[:, 1]
        value_rows = one_seq[:, 2]
        scores = dot_f32("qhd,khd->hqk", query_rows, key_rows) * scale
        scores = jnp.where(causal[None], scores, NEG)
        attn_prob = jnp.exp(scores - log_total)
        prob_low = attn_prob.astype(BF16)
        back_value = dot_f32("hqk,qhd->khd", prob_low, back_seq)
        back_prob = dot_f32("qhd,khd->hqk", back_seq, value_rows)
        back_score = attn_prob * (
            back_prob - jnp.sum(attn_prob * back_prob, axis=-1, keepdims=True)
        )
        back_score = back_score.astype(BF16)
        back_query = dot_f32("hqk,khd->qhd", back_score, key_rows) * scale
        back_key = dot_f32("hqk,qhd->khd", back_score, query_rows) * scale
        return jnp.stack([back_query, back_key, back_value], axis=1).astype(BF16)

    back_heads = lax.map(attend_back, (heads, log_kept, back_mixed))
    back_qkv = back_heads.reshape(row_count, 3 * head_width)
    attn_bias_sum = jnp.sum(back_qkv, axis=0, dtype=F32).reshape(3, head_width)[0::2]
    qkv_reduced = reduce_grad(ln1_low, back_qkv, 1)

    back_qkv_local = halves_swapped(back_qkv[:half], back_qkv[half:])
    back_ln1 = sum_over_mp(lambda rows: dot_f32("te,de->td", rows, w_qkv), back_qkv_local)
    hat1, inverse1 = norm_stats(x_own)
    gain1_sum = jnp.sum(back_ln1 * hat1, axis=0)
    shift1_sum = jnp.sum(back_ln1, axis=0)
    whole_own = back_resid + norm_back(back_ln1, hat1, inverse1, gain1)
    whole = to_global(halves_swapped(whole_own, swap(whole_own, "mp", 1)))

    norm_part = jnp.stack(
        [
            gain1_sum,
            shift1_sum,
            gain2_sum,
            shift2_sum,
            jnp.sum(back_resid, axis=0),
            jnp.sum(upstream, axis=0),
        ],
        axis=0,
    )
    norm_part = norm_part + swap(norm_part, "mp", 1)
    wide = outer * depth
    norm_part = norm_part[:, :wide] + swap(norm_part[:, wide:], "dp", 1)
    norm_reduced = norm_part[:, :depth]
    for r in range(1, outer):
        norm_reduced = norm_reduced + turn(norm_part[:, r * depth : (r + 1) * depth], -r)
    norm_reduced = norm_reduced.T

    attn_bias_reduced = tree_sum(attn_bias_sum, "dp")
    fc_bias_reduced = tree_sum(fc_bias_sum, "dp")
    qkv_reduced = qkv_reduced.reshape(depth, 3, head_width)
    raw_grads = [
        reduced / valid_total
        for reduced in (
            norm_reduced,
            attn_bias_reduced,
            qkv_reduced,
            proj_reduced,
            fc_bias_reduced,
            fc_reduced,
            down_reduced,
        )
    ]
    local_squares = jnp.sum(raw_grads[0] * raw_grads[0]) / float(mp_count)
    local_squares = local_squares + jnp.sum(raw_grads[1] * raw_grads[1]) / float(dp_count)
    local_squares = local_squares + jnp.sum(raw_grads[4] * raw_grads[4]) / float(dp_count)
    for grad_raw in (raw_grads[2], raw_grads[3], raw_grads[5], raw_grads[6]):
        local_squares = local_squares + jnp.sum(grad_raw * grad_raw)
    squares = tree_sum(tree_sum(local_squares, "mp"), "dp")
    grad_norm = jnp.sqrt(squares)
    clip_factor = jnp.minimum(1.0, 1.0 / (grad_norm + 1e-06))
    masters = (
        norm_master,
        attn_bias_master,
        qkv_master,
        proj_master,
        fc_bias_master,
        fc_master,
        down_master,
    )
    moments = (
        norm_moment,
        attn_bias_moment,
        qkv_moment,
        proj_moment,
        fc_bias_moment,
        fc_moment,
        down_moment,
    )
    averages = (
        norm_average,
        attn_bias_average,
        qkv_average,
        proj_average,
        fc_bias_average,
        fc_average,
        down_average,
    )
    grads_out = []
    momenta_out = []
    averaged_out = []
    updated_out = []
    copies_out = []
    for master, moment, average, grad_raw in zip(masters, moments, averages, raw_grads):
        clipped = grad_raw * clip_factor
        momentum = MOMENTUM * moment + clipped
        updated = master - RATE * (clipped + MOMENTUM * momentum)
        averaged = KEEP * average + (1.0 - KEEP) * updated
        grads_out.append(clipped)
        momenta_out.append(momentum)
        averaged_out.append(averaged)
        updated_out.append(updated)
        copies_out.append(updated.astype(jnp.bfloat16))
    return (
        block_part,
        whole,
        grads_out[0],
        grads_out[1],
        grads_out[2],
        grads_out[3],
        grads_out[4],
        grads_out[5],
        grads_out[6],
        momenta_out[0],
        momenta_out[1],
        momenta_out[2],
        momenta_out[3],
        momenta_out[4],
        momenta_out[5],
        momenta_out[6],
        averaged_out[0],
        averaged_out[1],
        averaged_out[2],
        averaged_out[3],
        averaged_out[4],
        averaged_out[5],
        averaged_out[6],
        updated_out[0],
        updated_out[1],
        updated_out[2],
        updated_out[3],
        updated_out[4],
        updated_out[5],
        updated_out[6],
        copies_out[0],
        copies_out[1],
        copies_out[2],
        copies_out[3],
        copies_out[4],
        copies_out[5],
        copies_out[6],
        grad_norm,
    )


def solution(mesh):
    placed = (
        P("dp", None),
        P("dp", None),
        P("dp"),
        P("dp", None),
        P(),
        P("dp", None),
        P(None, "mp"),
        P("dp", None, "mp"),
        P("dp", "mp"),
        P("mp"),
        P("dp", "mp"),
        P("dp", "mp"),
        P("dp", None),
        P(None, "mp"),
        P("dp", None, "mp"),
        P("dp", "mp"),
        P("mp"),
        P("dp", "mp"),
        P("dp", "mp"),
        P("dp", None),
        P(None, "mp"),
        P("dp", None, "mp"),
        P("dp", "mp"),
        P("mp"),
        P("dp", "mp"),
        P("dp", "mp"),
    )
    return jax.shard_map(
        local,
        mesh=mesh,
        in_specs=placed,
        out_specs=(
            P("dp", None),
            P("dp", None),
            P("dp", None),
            P(None, "mp"),
            P("dp", None, "mp"),
            P("dp", "mp"),
            P("mp"),
            P("dp", "mp"),
            P("dp", "mp"),
            P("dp", None),
            P(None, "mp"),
            P("dp", None, "mp"),
            P("dp", "mp"),
            P("mp"),
            P("dp", "mp"),
            P("dp", "mp"),
            P("dp", None),
            P(None, "mp"),
            P("dp", None, "mp"),
            P("dp", "mp"),
            P("mp"),
            P("dp", "mp"),
            P("dp", "mp"),
            P("dp", None),
            P(None, "mp"),
            P("dp", None, "mp"),
            P("dp", "mp"),
            P("mp"),
            P("dp", "mp"),
            P("dp", "mp"),
            P("dp", None),
            P(None, "mp"),
            P("dp", None, "mp"),
            P("dp", "mp"),
            P("mp"),
            P("dp", "mp"),
            P("dp", "mp"),
            P(),
        ),
        check_vma=False,
    )
```

time: 2160 us -> 1270 us (0.59)
  waiting for transfers between devices: 1660 us -> 536 us
  starting transfers between devices: 1.29 us -> 304 us
  blocking collectives: 128 us -> 0 us
  local copies, waits for them, and re-layouts: 18.8 us -> 88.9 us
    reduce_scatter x5 -> x0, waiting for transfers between devices: 812 us -> none  [the longest x1 281 us: local(): lax.psum_scatter(down_sum, 'dp', scatter_dimension=0, tiled=True)]
    ppermute x0 -> x108, waiting for transfers between devices: none -> 536 us  [the longest x78 302 us: swap(): return lax.ppermute(value, axis, [(i, i ^ flip) for i in range(size)])]
    psum x3 -> x0, waiting for transfers between devices: 533 us -> none  [sum_over_mp(): summed = lax.psum(term_fn(0, row_count), 'mp')]
    all_gather x4 -> x0, waiting for transfers between devices: 312 us -> none  [the longest x1 118 us: local(): lax.all_gather(low_fc, 'dp', axis=0, tiled=True)]
    ppermute x0 -> x108, starting transfers between devices: none -> 304 us  [the longest x30 171 us: turn(): return lax.ppermute(value, 'dp', pairs)]
    psum x3 -> x0, blocking collectives: 95.4 us -> none  [the longest x1 39.2 us: local(): squares = lax.psum(local_squares, ('dp', 'mp'))]
    unnamed x119 -> x241, local copies, waits for them, and re-layouts: 14 us -> 70.4 us
    all_gather x1 -> x0, blocking collectives: 32.9 us -> none  [local(): lax.all_gather(low_norm, 'dp', axis=0, tiled=True)]
  transfers between devices with their start and end apart: 12 -> 108, of which waited for: 11 -> 46; matrix products, arithmetic and copies ran while one was open for 8% -> 22% of each run, Pallas kernels for 0% -> 0%
where the time goes in v1:
time: 1270 us
  waiting for transfers between devices  536 us (42%)
  starting transfers between devices  304 us (24%)
  matrix products  202 us (16%)
  other arithmetic  118 us (9%)
  local copies, waits for them, and re-layouts  88.9 us (7%)
  between operations  16.8 us (1%)
    ppermute x78, waiting for transfers between devices, swap(): return lax.ppermute(value, axis, [(i, i ^ flip) for i in range(size)])  302 us
    ppermute x30, waiting for transfers between devices, turn(): return lax.ppermute(value, 'dp', pairs)  234 us
    dot_general x44, matrix products, dot_f32(): return jnp.einsum(eq, left, right, preferred_element_type=F32)  202 us
    ppermute x30, starting transfers between devices, turn(): return lax.ppermute(value, 'dp', pairs)  171 us
    ppermute x78, starting transfers between devices, swap(): return lax.ppermute(value, axis, [(i, i ^ flip) for i in range(size)])  133 us
    unnamed x241, local copies, waits for them, and re-layouts  70.4 us
  transfers between devices with their start and end apart: 108, of which 46 were waited for; matrix products, arithmetic and copies ran while one was open for 22% of the time, Pallas kernels for 0%

profile of v1, /device:TPU:0, one launch (start us, length us, event | category | flops | bytes accessed | tf_op | source)
XLA Modules:
  0.0 1265.1 jit_solution(10752382951159993144)
XLA Ops:
  34.5 24.8 %collective-permute-done = bf16[6,256]{1,0:T(8,128)(2,1)S(1)} collective-permute-done((bf16[6,256]{1,0:T(8,128)(2,1)S(1)}, bf16[6,256]{1,0:T(8,128)(2,1)S(1)}, u32[]{:S(2)}, u32[]{:S(2)}) %collective-permute-start) | collective-permute-done | bytes 3104 | tf_op jit(solution)/shard_map/ppermute | solution.py:38
  59.4 16.8 %collective-permute-done.1 = bf16[6,256]{1,0:T(8,128)(2,1)S(1)} collective-permute-done((bf16[6,256]{1,0:T(8,128)(2,1)S(1)}, bf16[6,256]{1,0:T(8,128)(2,1)S(1)}, u32[]{:S(2)}, u32[]{:S(2)}) %collective-permute-start.1) | collective-permute-done | bytes 3104 | tf_op jit(solution)/shard_map/ppermute | solution.py:38
  81.4 15.4 %collective-permute-done.4 = bf16[6,256]{1,0:T(8,128)(2,1)S(1)} collective-permute-done((bf16[6,256]{1,0:T(8,128)(2,1)S(1)}, bf16[6,256]{1,0:T(8,128)(2,1)S(1)}, u32[]{:S(2)}, u32[]{:S(2)}) %collective-permute-start.4) | collective-permute-done | bytes 3104 | tf_op jit(solution)/shard_map/ppermute | solution.py:31
  129.3 36.4 %collective-permute-done.18 = bf16[256,512]{1,0:T(8,128)(2,1)S(1)} collective-permute-done((bf16[256,512]{1,0:T(8,128)(2,1)S(1)}, bf16[256,512]{1,0:T(8,128)(2,1)S(1)}, u32[]{:S(2)}, u32[]{:S(2)}) %collective-permute-start.18) | collective-permute-done | bytes 262176 | tf_op jit(solution)/shard_map/ppermute | solution.py:31
  179.0 9.7 collective-permute-done.13
  189.7 10.1 add_convert_fusion
  278.5 17.2 %collective-permute-done.24 = bf16[256,2048]{1,0:T(8,128)(2,1)S(1)} collective-permute-done((bf16[256,2048]{1,0:T(8,128)(2,1)S(1)}, bf16[256,2048]{1,0:T(8,128)(2,1)S(1)}, u32[]{:S(2)}, u32[]{:S(2)}) %collective-permute-start.24) | collective-permute-done | bytes 1048608 | tf_op jit(solution)/shard_map/ppermute | solution.py:38
  295.7 41.7 %collective-permute-done.25 = bf16[256,2048]{1,0:T(8,128)(2,1)S(1)} collective-permute-done((bf16[256,2048]{1,0:T(8,128)(2,1)S(1)}, bf16[256,2048]{1,0:T(8,128)(2,1)S(1)}, u32[]{:S(2)}, u32[]{:S(2)}) %collective-permute-start.25) | collective-permute-done | bytes 1048608 | tf_op jit(solution)/shard_map/ppermute | solution.py:38
  339.1 44.6 %collective-permute-start.31 = (bf16[256,2048]{1,0:T(8,128)(2,1)S(1)}, bf16[256,2048]{1,0:T(8,128)(2,1)S(1)}, u32[]{:S(2)}, u32[]{:S(2)}) collective-permute-start(bf16[256,2048]{1,0:T(8,128)(2,1)S(1)} %convert_element_type.341), channel_id=1, source_target_pairs={{0,8},{4,12},{8,16},{12,20},{16,24},{20,28},{24,0},{28,4},{1,9},{5... | collective-permute-start | bytes 3145736 | tf_op jit(solution)/shard_map/ppermute | solution.py:38
  387.9 19.3 %collective-permute-done.31 = bf16[256,2048]{1,0:T(8,128)(2,1)S(1)} collective-permute-done((bf16[256,2048]{1,0:T(8,128)(2,1)S(1)}, bf16[256,2048]{1,0:T(8,128)(2,1)S(1)}, u32[]{:S(2)}, u32[]{:S(2)}) %collective-permute-start.31) | collective-permute-done | bytes 1048608 | tf_op jit(solution)/shard_map/ppermute | solution.py:38
  414.9 20.2 %collective-permute-done.29 = bf16[256,2048]{1,0:T(8,128)(2,1)S(1)} collective-permute-done((bf16[256,2048]{1,0:T(8,128)(2,1)S(1)}, bf16[256,2048]{1,0:T(8,128)(2,1)S(1)}, u32[]{:S(2)}, u32[]{:S(2)}) %collective-permute-start.29) | collective-permute-done | bytes 1048608 | tf_op jit(solution)/shard_map/ppermute | solution.py:31
  436.5 14.0 %collective-permute-done.33 = bf16[256,2048]{1,0:T(8,128)(2,1)S(1)} collective-permute-done((bf16[256,2048]{1,0:T(8,128)(2,1)S(1)}, bf16[256,2048]{1,0:T(8,128)(2,1)S(1)}, u32[]{:S(2)}, u32[]{:S(2)}) %collective-permute-start.33) | collective-permute-done | bytes 1048608 | tf_op jit(solution)/shard_map/ppermute | solution.py:38
  461.2 18.9 %collective-permute-done.35 = bf16[256,2048]{1,0:T(8,128)(2,1)S(1)} collective-permute-done((bf16[256,2048]{1,0:T(8,128)(2,1)S(1)}, bf16[256,2048]{1,0:T(8,128)(2,1)S(1)}, u32[]{:S(2)}, u32[]{:S(2)}) %collective-permute-start.35) | collective-permute-done | bytes 1048608 | tf_op jit(solution)/shard_map/ppermute | solution.py:31
  480.1 22.4 %collective-permute-done.36 = bf16[256,2048]{1,0:T(8,128)(2,1)S(1)} collective-permute-done((bf16[256,2048]{1,0:T(8,128)(2,1)S(1)}, bf16[256,2048]{1,0:T(8,128)(2,1)S(1)}, u32[]{:S(2)}, u32[]{:S(2)}) %collective-permute-start.36) | collective-permute-done | bytes 1048608 | tf_op jit(solution)/shard_map/ppermute | solution.py:31
  502.6 20.1 %collective-permute-done.37 = bf16[256,2048]{1,0:T(8,128)(2,1)S(1)} collective-permute-done((bf16[256,2048]{1,0:T(8,128)(2,1)S(1)}, bf16[256,2048]{1,0:T(8,128)(2,1)S(1)}, u32[]{:S(2)}, u32[]{:S(2)}) %collective-permute-start.37) | collective-permute-done | bytes 1048608 | tf_op jit(solution)/shard_map/ppermute | solution.py:31
  526.1 15.5 %multiply_convert_fusion.1 = (bf16[1024,2048]{1,0:T(8,128)(2,1)S(1)}, f32[1024,2048]{1,0:T(8,128)}) fusion(f32[2048]{0:T(1024)S(1)} %copy-done.77, bf16[2048,2048]{1,0:T(8,128)(2,1)} %constant_dynamic-update-slice_fusion.24, bf16[512,2048]{1,0:T(8,128)(2,1)S(1)} %collective-permute-done.23, bf16[512,2048]{1,0:T(8,128)(2,1)S(1)} %add_convert_fusion.5), kind=kOutput, calls=%fused_computation.61 | convolution fusion | flops 8619294720 | bytes 25174016 | tf_op jit(solution)/shard_map/td,df->tf/dot_general | solution.py:22
  548.4 9.1 convolution_convert_fusion.2
  557.5 17.1 %convert_reduce_fusion.1 = (f32[2048]{0:T(1024)S(1)}, bf16[1024,2048]{1,0:T(8,128)(2,1)S(1)}) fusion(f32[1024,2048]{1,0:T(8,128)} %get-tuple-element.243, f32[2048]{0:T(1024)S(1)} %copy-done.77, bf16[2048,2048]{1,0:T(8,128)(2,1)} %copy-done.56, bf16[512,2048]{1,0:T(8,128)(2,1)S(1)} %get-tuple-element.213, bf16[512,2048]{1,0:T(8,128)(2,1)S(1)} %get-tuple-element.212), kind=kOutput, calls=%fused_computation.60 | convolution fusion | flops 8644458496 | bytes 25182208 | tf_op jit(solution)/shard_map/td,df->tf/dot_general | solution.py:22
  574.6 11.0 convolution_convert_fusion.1
  597.4 17.9 %collective-permute-done.89 = bf16[256,2048]{1,0:T(8,128)(2,1)S(1)} collective-permute-done((bf16[256,2048]{1,0:T(8,128)(2,1)S(1)}, bf16[256,2048]{1,0:T(8,128)(2,1)S(1)}, u32[]{:S(2)}, u32[]{:S(2)}) %collective-permute-start.89) | collective-permute-done | bytes 1048608 | tf_op jit(solution)/shard_map/ppermute | solution.py:31
  619.3 18.5 %collective-permute-done.87 = bf16[256,2048]{1,0:T(8,128)(2,1)S(1)} collective-permute-done((bf16[256,2048]{1,0:T(8,128)(2,1)S(1)}, bf16[256,2048]{1,0:T(8,128)(2,1)S(1)}, u32[]{:S(2)}, u32[]{:S(2)}) %collective-permute-start.87) | collective-permute-done | bytes 1048608 | tf_op jit(solution)/shard_map/ppermute | solution.py:31
  642.0 9.4 add_convert_fusion.2
  653.0 9.6 add_convert_fusion.4
  666.7 16.1 %collective-permute-done.94 = bf16[256,2048]{1,0:T(8,128)(2,1)} collective-permute-done((bf16[256,2048]{1,0:T(8,128)(2,1)}, bf16[256,2048]{1,0:T(8,128)(2,1)}, u32[]{:S(2)}, u32[]{:S(2)}) %collective-permute-start.94) | collective-permute-done | bytes 1048608 | tf_op jit(solution)/shard_map/ppermute | solution.py:31
  689.6 14.6 %collective-permute-done.92 = bf16[256,2048]{1,0:T(8,128)(2,1)} collective-permute-done((bf16[256,2048]{1,0:T(8,128)(2,1)}, bf16[256,2048]{1,0:T(8,128)(2,1)}, u32[]{:S(2)}, u32[]{:S(2)}) %collective-permute-start.92) | collective-permute-done | bytes 1048608 | tf_op jit(solution)/shard_map/ppermute | solution.py:31
  704.2 21.6 %collective-permute-start.69 = (f32[2048]{0:T(1024)S(1)}, f32[2048]{0:T(1024)S(1)}, u32[]{:S(2)}, u32[]{:S(2)}) collective-permute-start(f32[2048]{0:T(1024)S(1)} %get-tuple-element.246), channel_id=1, source_target_pairs={{0,16},{4,20},{8,24},{12,28},{16,0},{20,4},{24,8},{28,12},{1,17},{... | collective-permute-start | bytes 24584 | tf_op jit(solution)/shard_map/ppermute | solution.py:31
  744.3 6.5 fusion.170
  752.6 10.4 collective-permute-done.85
  766.5 16.1 %collective-permute-done.91 = bf16[256,2048]{1,0:T(8,128)(2,1)} collective-permute-done((bf16[256,2048]{1,0:T(8,128)(2,1)S(1)}, bf16[256,2048]{1,0:T(8,128)(2,1)}, u32[]{:S(2)}, u32[]{:S(2)}) %collective-permute-start.91) | collective-permute-done | bytes 1048608 | tf_op jit(solution)/shard_map/ppermute | solution.py:31
  784.2 26.3 %collective-permute-start.90 = (bf16[256,2048]{1,0:T(8,128)(2,1)}, bf16[256,2048]{1,0:T(8,128)(2,1)}, u32[]{:S(2)}, u32[]{:S(2)}) collective-permute-start(bf16[256,2048]{1,0:T(8,128)(2,1)} %fusion.43), channel_id=1, source_target_pairs={{0,8},{4,12},{8,16},{12,20},{16,24},{20,28},{24,0},{28,4},{1,9},{5... | collective-permute-start | bytes 3145736 | tf_op jit(solution)/shard_map/ppermute | solution.py:38
  812.7 57.1 %collective-permute-start.86 = (bf16[256,2048]{1,0:T(8,128)(2,1)}, bf16[256,2048]{1,0:T(8,128)(2,1)}, u32[]{:S(2)}, u32[]{:S(2)}) collective-permute-start(bf16[256,2048]{1,0:T(8,128)(2,1)} %fusion.41), channel_id=1, source_target_pairs={{0,24},{4,28},{8,0},{12,4},{16,8},{20,12},{24,16},{28,20},{1,25},{... | collective-permute-start | bytes 3145736 | tf_op jit(solution)/shard_map/ppermute | solution.py:38
  874.3 6.8 multiply_reduce_fusion.4
  881.1 17.5 %collective-permute-done.88 = bf16[256,2048]{1,0:T(8,128)(2,1)} collective-permute-done((bf16[256,2048]{1,0:T(8,128)(2,1)}, bf16[256,2048]{1,0:T(8,128)(2,1)}, u32[]{:S(2)}, u32[]{:S(2)}) %collective-permute-start.88) | collective-permute-done | bytes 1048608 | tf_op jit(solution)/shard_map/ppermute | solution.py:38
  898.6 11.0 collective-permute-done.86
  909.6 6.5 multiply_reduce_fusion.5
  922.0 9.0 convolution_bitcast_fusion
  931.0 12.7 %multiply_reduce_fusion = (f32[4,1024]{1,0:T(4,128)S(1)}, f32[4,1024,1024]{1,2,0:T(8,128)}) fusion(f32[4,1024,1024]{1,2,0:T(8,128)} %copy-done.2, f32[4,1024]{1,0:T(4,128)S(1)} %copy-done.52, pred[1024,1024]{0,1:T(8,128)(4,1)S(1)} %copy-done.9, bf16[1024,4,128]{0,2,1:T(8,128)(2,1)S(1)} %bitcast.131, bf16[1024,1,4,128]{0,3,2,1:T(8,128)(2,1)S(1)} %copy-done.33), kind=kOutput, calls=%fused_computation.1 | convolution fusion | flops 1094709248 | bytes 36732928 | tf_op jit(solution)/shard_map/while/body/eval_jaxpr/qhd,khd->hqk/dot_general | solution.py:22
  943.7 12.2 multiply_convert_fusion
  960.9 12.4 collective-permute-start.64
  975.8 6.8 convolution_convert_fusion
  1007.3 13.3 %collective-permute-done.76 = bf16[256,1536]{1,0:T(8,128)(2,1)S(1)} collective-permute-done((bf16[256,1536]{1,0:T(8,128)(2,1)S(1)}, bf16[256,1536]{1,0:T(8,128)(2,1)S(1)}, u32[]{:S(2)}, u32[]{:S(2)}) %collective-permute-start.76) | collective-permute-done | bytes 786464 | tf_op jit(solution)/shard_map/ppermute | solution.py:31
  1029.5 17.3 %collective-permute-done.80 = bf16[1024,512]{1,0:T(8,128)(2,1)S(1)} collective-permute-done((bf16[1024,512]{1,0:T(8,128)(2,1)S(1)}, bf16[1024,512]{1,0:T(8,128)(2,1)S(1)}, u32[]{:S(2)}, u32[]{:S(2)}) %collective-permute-start.80) | collective-permute-done | bytes 1048608 | tf_op jit(solution)/shard_map/ppermute | solution.py:31
  1069.2 8.5 collective-permute-start.79
  1077.7 32.1 %collective-permute-done.82 = bf16[256,512]{1,0:T(8,128)(2,1)S(1)} collective-permute-done((bf16[256,512]{1,0:T(8,128)(2,1)S(1)}, bf16[256,512]{1,0:T(8,128)(2,1)S(1)}, u32[]{:S(2)}, u32[]{:S(2)}) %collective-permute-start.82) | collective-permute-done | bytes 262176 | tf_op jit(solution)/shard_map/ppermute | solution.py:38
  1117.5 15.0 %collective-permute-done.77 = bf16[256,1536]{1,0:T(8,128)(2,1)} collective-permute-done((bf16[256,1536]{1,0:T(8,128)(2,1)}, bf16[256,1536]{1,0:T(8,128)(2,1)}, u32[]{:S(2)}, u32[]{:S(2)}) %collective-permute-start.77) | collective-permute-done | bytes 786464 | tf_op jit(solution)/shard_map/ppermute | solution.py:38
  1132.4 16.7 %collective-permute-done.75 = bf16[256,1536]{1,0:T(8,128)(2,1)} collective-permute-done((bf16[256,1536]{1,0:T(8,128)(2,1)}, bf16[256,1536]{1,0:T(8,128)(2,1)}, u32[]{:S(2)}, u32[]{:S(2)}) %collective-permute-start.75) | collective-permute-done | bytes 786464 | tf_op jit(solution)/shard_map/ppermute | solution.py:38
  1166.9 6.5 fusion.24
  1252.0 7.1 maximum_select_fusion
  (545 shorter events, 428.4 us)
Async XLA Ops:
  2.7 105.3 %collective-permute-start.7 = (bf16[256,1536]{0,1:T(8,128)(2,1)S(1)}, bf16[256,1536]{0,1:T(8,128)(2,1)}, u32[]{:S(2)}, u32[]{:S(2)}) collective-permute-start(bf16[256,1536]{0,1:T(8,128)(2,1)S(1)} %bitcast.132), channel_id=1, source_target_pairs={{0,8},{4,12},{8,16},{12,20},{16,24},{20,28},{24,0},{28,4},{1,9},{5... | collective-permute-start | bytes 2359304 | tf_op jit(solution)/shard_map/ppermute | solution.py:38
  5.8 106.0 %collective-permute-start.8 = (bf16[256,1536]{0,1:T(8,128)(2,1)S(1)}, bf16[256,1536]{0,1:T(8,128)(2,1)}, u32[]{:S(2)}, u32[]{:S(2)}) collective-permute-start(bf16[256,1536]{0,1:T(8,128)(2,1)S(1)} %bitcast.133), channel_id=1, source_target_pairs={{0,16},{4,20},{8,24},{12,28},{16,0},{20,4},{24,8},{28,12},{1,17},{... | collective-permute-start | bytes 2359304 | tf_op jit(solution)/shard_map/ppermute | solution.py:38
  8.3 105.5 %collective-permute-start.9 = (bf16[256,1536]{0,1:T(8,128)(2,1)S(1)}, bf16[256,1536]{0,1:T(8,128)(2,1)S(1)}, u32[]{:S(2)}, u32[]{:S(2)}) collective-permute-start(bf16[256,1536]{0,1:T(8,128)(2,1)S(1)} %bitcast.134), channel_id=1, source_target_pairs={{0,24},{4,28},{8,0},{12,4},{16,8},{20,12},{24,16},{28,20},{1,25},{... | collective-permute-start | bytes 2359304 | tf_op jit(solution)/shard_map/ppermute | solution.py:38
  9.7 49.6 %collective-permute-start = (bf16[6,256]{1,0:T(8,128)(2,1)S(1)}, bf16[6,256]{1,0:T(8,128)(2,1)S(1)}, u32[]{:S(2)}, u32[]{:S(2)}) collective-permute-start(bf16[6,256]{1,0:T(8,128)(2,1)S(1)} %get-tuple-element.208), channel_id=1, source_target_pairs={{0,8},{4,12},{8,16},{12,20},{16,24},{20,28},{24,0},{28,4},{1,9},{5... | collective-permute-start | bytes 9224 | tf_op jit(solution)/shard_map/ppermute | solution.py:38
  10.4 65.8 %collective-permute-start.1 = (bf16[6,256]{1,0:T(8,128)(2,1)S(1)}, bf16[6,256]{1,0:T(8,128)(2,1)S(1)}, u32[]{:S(2)}, u32[]{:S(2)}) collective-permute-start(bf16[6,256]{1,0:T(8,128)(2,1)S(1)} %get-tuple-element.208), channel_id=1, source_target_pairs={{0,16},{4,20},{8,24},{12,28},{16,0},{20,4},{24,8},{28,12},{1,17},{... | collective-permute-start | bytes 9224 | tf_op jit(solution)/shard_map/ppermute | solution.py:38
  118.6 58.4 %collective-permute-start.11 = (bf16[256,1536]{0,1:T(8,128)(2,1)}, bf16[256,1536]{0,1:T(8,128)(2,1)S(1)}, u32[]{:S(2)}, u32[]{:S(2)}) collective-permute-start(bf16[256,1536]{0,1:T(8,128)(2,1)} %collective-permute-done.7), channel_id=1, source_target_pairs={{0,4},{4,0},{8,12},{12,8},{16,20},{20,16},{24,28},{28,24},{1,5},{5... | collective-permute-start | bytes 2359304 | tf_op jit(solution)/shard_map/ppermute | solution.py:31
  120.2 57.8 %collective-permute-start.12 = (bf16[256,1536]{0,1:T(8,128)(2,1)}, bf16[256,1536]{0,1:T(8,128)(2,1)S(1)}, u32[]{:S(2)}, u32[]{:S(2)}) collective-permute-start(bf16[256,1536]{0,1:T(8,128)(2,1)} %collective-permute-done.8), channel_id=1, source_target_pairs={{0,4},{4,0},{8,12},{12,8},{16,20},{20,16},{24,28},{28,24},{1,5},{5... | collective-permute-start | bytes 2359304 | tf_op jit(solution)/shard_map/ppermute | solution.py:31
  128.2 48.8 %collective-permute-start.20 = (bf16[256,512]{1,0:T(8,128)(2,1)S(1)}, bf16[256,512]{1,0:T(8,128)(2,1)S(1)}, u32[]{:S(2)}, u32[]{:S(2)}) collective-permute-start(bf16[256,512]{1,0:T(8,128)(2,1)S(1)} %collective-permute-done.16), channel_id=1, source_target_pairs={{0,4},{4,0},{8,12},{12,8},{16,20},{20,16},{24,28},{28,24},{1,5},{5... | collective-permute-start | bytes 786440 | tf_op jit(solution)/shard_map/ppermute | solution.py:31
  268.7 68.7 %collective-permute-start.25 = (bf16[256,2048]{1,0:T(8,128)(2,1)S(1)}, bf16[256,2048]{1,0:T(8,128)(2,1)S(1)}, u32[]{:S(2)}, u32[]{:S(2)}) collective-permute-start(bf16[256,2048]{1,0:T(8,128)(2,1)S(1)} %copy-done.26), channel_id=1, source_target_pairs={{0,16},{4,20},{8,24},{12,28},{16,0},{20,4},{24,8},{28,12},{1,17},{... | collective-permute-start | bytes 3145736 | tf_op jit(solution)/shard_map/ppermute | solution.py:38
  269.0 68.4 %collective-permute-start.26 = (bf16[256,2048]{1,0:T(8,128)(2,1)S(1)}, bf16[256,2048]{1,0:T(8,128)(2,1)S(1)}, u32[]{:S(2)}, u32[]{:S(2)}) collective-permute-start(bf16[256,2048]{1,0:T(8,128)(2,1)S(1)} %copy-done.26), channel_id=1, source_target_pairs={{0,24},{4,28},{8,0},{12,4},{16,8},{20,12},{24,16},{28,20},{1,25},{... | collective-permute-start | bytes 3145736 | tf_op jit(solution)/shard_map/ppermute | solution.py:38
  274.5 134.1 %collective-permute-start.22 = (bf16[512,2048]{1,0:T(8,128)(2,1)S(1)}, bf16[512,2048]{1,0:T(8,128)(2,1)S(1)}, u32[]{:S(2)}, u32[]{:S(2)}) collective-permute-start(bf16[512,2048]{1,0:T(8,128)(2,1)S(1)} %add_convert_fusion.6), channel_id=1, source_target_pairs={{0,2},{1,3},{2,0},{3,1},{4,6},{5,7},{6,4},{7,5},{8,10},{9,11},{10,... | collective-permute-start | bytes 6291464 | tf_op jit(solution)/shard_map/ppermute | solution.py:31
  276.8 107.0 %collective-permute-start.27 = (bf16[256,2048]{1,0:T(8,128)(2,1)S(1)}, bf16[256,2048]{1,0:T(8,128)(2,1)S(1)}, u32[]{:S(2)}, u32[]{:S(2)}) collective-permute-start(bf16[256,2048]{1,0:T(8,128)(2,1)S(1)} %copy-done.26), channel_id=1, source_target_pairs={{0,4},{4,0},{8,12},{12,8},{16,20},{20,16},{24,28},{28,24},{1,5},{5... | collective-permute-start | bytes 3145736 | tf_op jit(solution)/shard_map/ppermute | solution.py:31
  337.4 49.0 %collective-permute-start.28 = (bf16[256,2048]{1,0:T(8,128)(2,1)S(1)}, bf16[256,2048]{1,0:T(8,128)(2,1)S(1)}, u32[]{:S(2)}, u32[]{:S(2)}) collective-permute-start(bf16[256,2048]{1,0:T(8,128)(2,1)S(1)} %collective-permute-done.24), channel_id=1, source_target_pairs={{0,4},{4,0},{8,12},{12,8},{16,20},{20,16},{24,28},{28,24},{1,5},{5... | collective-permute-start | bytes 3145736 | tf_op jit(solution)/shard_map/ppermute | solution.py:31
  339.1 68.2 %collective-permute-start.31 = (bf16[256,2048]{1,0:T(8,128)(2,1)S(1)}, bf16[256,2048]{1,0:T(8,128)(2,1)S(1)}, u32[]{:S(2)}, u32[]{:S(2)}) collective-permute-start(bf16[256,2048]{1,0:T(8,128)(2,1)S(1)} %convert_element_type.341), channel_id=1, source_target_pairs={{0,8},{4,12},{8,16},{12,20},{16,24},{20,28},{24,0},{28,4},{1,9},{5... | collective-permute-start | bytes 3145736 | tf_op jit(solution)/shard_map/ppermute | solution.py:38
  383.6 52.8 %collective-permute-start.32 = (bf16[256,2048]{1,0:T(8,128)(2,1)S(1)}, bf16[256,2048]{1,0:T(8,128)(2,1)S(1)}, u32[]{:S(2)}, u32[]{:S(2)}) collective-permute-start(bf16[256,2048]{1,0:T(8,128)(2,1)S(1)} %convert_element_type.341), channel_id=1, source_target_pairs={{0,16},{4,20},{8,24},{12,28},{16,0},{20,4},{24,8},{28,12},{1,17},{... | collective-permute-start | bytes 3145736 | tf_op jit(solution)/shard_map/ppermute | solution.py:38
  383.9 66.6 %collective-permute-start.33 = (bf16[256,2048]{1,0:T(8,128)(2,1)S(1)}, bf16[256,2048]{1,0:T(8,128)(2,1)S(1)}, u32[]{:S(2)}, u32[]{:S(2)}) collective-permute-start(bf16[256,2048]{1,0:T(8,128)(2,1)S(1)} %convert_element_type.341), channel_id=1, source_target_pairs={{0,24},{4,28},{8,0},{12,4},{16,8},{20,12},{24,16},{28,20},{1,25},{... | collective-permute-start | bytes 3145736 | tf_op jit(solution)/shard_map/ppermute | solution.py:38
  386.5 74.6 %collective-permute-start.34 = (bf16[256,2048]{1,0:T(8,128)(2,1)S(1)}, bf16[256,2048]{1,0:T(8,128)(2,1)S(1)}, u32[]{:S(2)}, u32[]{:S(2)}) collective-permute-start(bf16[256,2048]{1,0:T(8,128)(2,1)S(1)} %convert_element_type.341), channel_id=1, source_target_pairs={{0,4},{4,0},{8,12},{12,8},{16,20},{20,16},{24,28},{28,24},{1,5},{5... | collective-permute-start | bytes 3145736 | tf_op jit(solution)/shard_map/ppermute | solution.py:31
  408.6 48.9 %collective-permute-start.30 = (bf16[256,2048]{1,0:T(8,128)(2,1)S(1)}, bf16[256,2048]{1,0:T(8,128)(2,1)S(1)}, u32[]{:S(2)}, u32[]{:S(2)}) collective-permute-start(bf16[256,2048]{1,0:T(8,128)(2,1)S(1)} %collective-permute-done.26), channel_id=1, source_target_pairs={{0,4},{4,0},{8,12},{12,8},{16,20},{20,16},{24,28},{28,24},{1,5},{5... | collective-permute-start | bytes 3145736 | tf_op jit(solution)/shard_map/ppermute | solution.py:31
  436.4 89.7 %collective-permute-start.23 = (bf16[512,2048]{1,0:T(8,128)(2,1)S(1)}, bf16[512,2048]{1,0:T(8,128)(2,1)S(1)}, u32[]{:S(2)}, u32[]{:S(2)}) collective-permute-start(bf16[512,2048]{1,0:T(8,128)(2,1)S(1)} %add_convert_fusion.5), channel_id=1, source_target_pairs={{0,1},{1,0},{2,3},{3,2},{4,5},{5,4},{6,7},{7,6},{8,9},{9,8},{10,11... | collective-permute-start | bytes 6291464 | tf_op jit(solution)/shard_map/ppermute | solution.py:31
  450.5 52.0 %collective-permute-start.36 = (bf16[256,2048]{1,0:T(8,128)(2,1)S(1)}, bf16[256,2048]{1,0:T(8,128)(2,1)S(1)}, u32[]{:S(2)}, u32[]{:S(2)}) collective-permute-start(bf16[256,2048]{1,0:T(8,128)(2,1)S(1)} %collective-permute-done.32), channel_id=1, source_target_pairs={{0,4},{4,0},{8,12},{12,8},{16,20},{20,16},{24,28},{28,24},{1,5},{5... | collective-permute-start | bytes 3145736 | tf_op jit(solution)/shard_map/ppermute | solution.py:31
  457.6 65.1 %collective-permute-start.37 = (bf16[256,2048]{1,0:T(8,128)(2,1)S(1)}, bf16[256,2048]{1,0:T(8,128)(2,1)S(1)}, u32[]{:S(2)}, u32[]{:S(2)}) collective-permute-start(bf16[256,2048]{1,0:T(8,128)(2,1)S(1)} %collective-permute-done.33), channel_id=1, source_target_pairs={{0,4},{4,0},{8,12},{12,8},{16,20},{20,16},{24,28},{28,24},{1,5},{5... | collective-permute-start | bytes 3145736 | tf_op jit(solution)/shard_map/ppermute | solution.py:31
  585.6 56.1 %collective-permute-start.48 = (bf16[512,2048]{1,0:T(8,128)(2,1)}, bf16[512,2048]{1,0:T(8,128)(2,1)}, u32[]{:S(2)}, u32[]{:S(2)}) collective-permute-start(bf16[512,2048]{1,0:T(8,128)(2,1)} %convolution_convert_fusion.1), channel_id=1, source_target_pairs={{0,1},{1,0},{2,3},{3,2},{4,5},{5,4},{6,7},{7,6},{8,9},{9,8},{10,11... | collective-permute-start | bytes 6291464 | tf_op jit(solution)/shard_map/ppermute | solution.py:31
  585.7 65.8 %collective-permute-start.38 = (bf16[512,2048]{1,0:T(8,128)(2,1)}, bf16[512,2048]{1,0:T(8,128)(2,1)}, u32[]{:S(2)}, u32[]{:S(2)}) collective-permute-start(bf16[512,2048]{1,0:T(8,128)(2,1)} %convolution_convert_fusion.2), channel_id=1, source_target_pairs={{0,1},{1,0},{2,3},{3,2},{4,5},{5,4},{6,7},{7,6},{8,9},{9,8},{10,11... | collective-permute-start | bytes 6291464 | tf_op jit(solution)/shard_map/ppermute | solution.py:31
  586.2 147.0 %collective-permute-start.71 = (f32[2048]{0:T(1024)S(1)}, f32[2048]{0:T(1024)S(1)}, u32[]{:S(2)}, u32[]{:S(2)}) collective-permute-start(f32[2048]{0:T(1024)S(1)} %get-tuple-element.246), channel_id=1, source_target_pairs={{0,24},{4,28},{8,16},{12,20},{16,8},{20,12},{24,0},{28,4},{1,25},{... | collective-permute-start | bytes 24584 | tf_op jit(solution)/shard_map/ppermute | solution.py:31
  592.2 45.5 %collective-permute-start.87 = (bf16[256,2048]{1,0:T(8,128)(2,1)S(1)}, bf16[256,2048]{1,0:T(8,128)(2,1)S(1)}, u32[]{:S(2)}, u32[]{:S(2)}) collective-permute-start(bf16[256,2048]{1,0:T(8,128)(2,1)S(1)} %convolution_convert_fusion.9), channel_id=1, source_target_pairs={{0,4},{4,0},{8,12},{12,8},{16,20},{20,16},{24,28},{28,24},{1,5},{5... | collective-permute-start | bytes 3145736 | tf_op jit(solution)/shard_map/ppermute | solution.py:31
  615.3 47.3 %collective-permute-start.96 = (bf16[256,2048]{1,0:T(8,128)(2,1)}, bf16[256,2048]{1,0:T(8,128)(2,1)}, u32[]{:S(2)}, u32[]{:S(2)}) collective-permute-start(bf16[256,2048]{1,0:T(8,128)(2,1)} %convolution_convert_fusion.4), channel_id=1, source_target_pairs={{0,4},{4,0},{8,12},{12,8},{16,20},{20,16},{24,28},{28,24},{1,5},{5... | collective-permute-start | bytes 3145736 | tf_op jit(solution)/shard_map/ppermute | solution.py:31
  637.7 45.0 %collective-permute-start.94 = (bf16[256,2048]{1,0:T(8,128)(2,1)}, bf16[256,2048]{1,0:T(8,128)(2,1)}, u32[]{:S(2)}, u32[]{:S(2)}) collective-permute-start(bf16[256,2048]{1,0:T(8,128)(2,1)} %convolution_convert_fusion.5), channel_id=1, source_target_pairs={{0,4},{4,0},{8,12},{12,8},{16,20},{20,16},{24,28},{28,24},{1,5},{5... | collective-permute-start | bytes 3145736 | tf_op jit(solution)/shard_map/ppermute | solution.py:31
  641.7 62.5 %collective-permute-start.92 = (bf16[256,2048]{1,0:T(8,128)(2,1)}, bf16[256,2048]{1,0:T(8,128)(2,1)}, u32[]{:S(2)}, u32[]{:S(2)}) collective-permute-start(bf16[256,2048]{1,0:T(8,128)(2,1)} %convolution_convert_fusion.6), channel_id=1, source_target_pairs={{0,4},{4,0},{8,12},{12,8},{16,20},{20,16},{24,28},{28,24},{1,5},{5... | collective-permute-start | bytes 3145736 | tf_op jit(solution)/shard_map/ppermute | solution.py:31
  651.5 77.8 %collective-permute-start.49 = (bf16[512,2048]{1,0:T(8,128)(2,1)}, bf16[512,2048]{1,0:T(8,128)(2,1)}, u32[]{:S(2)}, u32[]{:S(2)}) collective-permute-start(bf16[512,2048]{1,0:T(8,128)(2,1)} %add_convert_fusion.2), channel_id=1, source_target_pairs={{0,2},{1,3},{2,0},{3,1},{4,6},{5,7},{6,4},{7,5},{8,10},{9,11},{10,... | collective-permute-start | bytes 6291464 | tf_op jit(solution)/shard_map/ppermute | solution.py:31
  662.6 80.2 %collective-permute-start.39 = (bf16[512,2048]{1,0:T(8,128)(2,1)}, bf16[512,2048]{1,0:T(8,128)(2,1)S(1)}, u32[]{:S(2)}, u32[]{:S(2)}) collective-permute-start(bf16[512,2048]{1,0:T(8,128)(2,1)} %add_convert_fusion.4), channel_id=1, source_target_pairs={{0,2},{1,3},{2,0},{3,1},{4,6},{5,7},{6,4},{7,5},{8,10},{9,11},{10,... | collective-permute-start | bytes 6291464 | tf_op jit(solution)/shard_map/ppermute | solution.py:31
  682.8 51.8 %collective-permute-start.72 = (f32[2048]{0:T(1024)S(1)}, f32[2048]{0:T(1024)S(1)}, u32[]{:S(2)}, u32[]{:S(2)}) collective-permute-start(f32[2048]{0:T(1024)S(1)} %get-tuple-element.246), channel_id=1, source_target_pairs={{0,28},{4,24},{8,20},{12,16},{16,12},{20,8},{24,4},{28,0},{1,29},{... | collective-permute-start | bytes 24584 | tf_op jit(solution)/shard_map/ppermute | solution.py:31
  740.2 72.3 %collective-permute-start.95 = (bf16[256,2048]{1,0:T(8,128)(2,1)}, bf16[256,2048]{1,0:T(8,128)(2,1)}, u32[]{:S(2)}, u32[]{:S(2)}) collective-permute-start(bf16[256,2048]{1,0:T(8,128)(2,1)} %add_convert_fusion.8), channel_id=1, source_target_pairs={{0,16},{4,20},{8,24},{12,28},{16,0},{20,4},{24,8},{28,12},{1,17},{... | collective-permute-start | bytes 3145736 | tf_op jit(solution)/shard_map/ppermute | solution.py:38
  742.8 69.9 %collective-permute-start.93 = (bf16[256,2048]{1,0:T(8,128)(2,1)}, bf16[256,2048]{1,0:T(8,128)(2,1)}, u32[]{:S(2)}, u32[]{:S(2)}) collective-permute-start(bf16[256,2048]{1,0:T(8,128)(2,1)} %add_convert_fusion.9), channel_id=1, source_target_pairs={{0,24},{4,28},{8,0},{12,4},{16,8},{20,12},{24,16},{28,20},{1,25},{... | collective-permute-start | bytes 3145736 | tf_op jit(solution)/shard_map/ppermute | solution.py:38
  763.0 153.2 %collective-permute-start.50 = (bf16[512,2048]{1,0:T(8,128)(2,1)}, bf16[512,2048]{1,0:T(8,128)(2,1)}, u32[]{:S(2)}, u32[]{:S(2)}) collective-permute-start(bf16[512,2048]{1,0:T(8,128)(2,1)} %convert_element_type.359), channel_id=1, source_target_pairs={{0,1},{1,0},{2,3},{3,2},{4,5},{5,4},{6,7},{7,6},{8,9},{9,8},{10,11... | collective-permute-start | bytes 6291464 | tf_op jit(solution)/shard_map/ppermute | solution.py:31
  782.6 98.5 %collective-permute-start.84 = (bf16[256,2048]{1,0:T(8,128)(2,1)S(1)}, bf16[256,2048]{1,0:T(8,128)(2,1)}, u32[]{:S(2)}, u32[]{:S(2)}) collective-permute-start(bf16[256,2048]{1,0:T(8,128)(2,1)S(1)} %convolution_convert_fusion.11), channel_id=1, source_target_pairs={{0,4},{4,0},{8,12},{12,8},{16,20},{20,16},{24,28},{28,24},{1,5},{5... | collective-permute-start | bytes 3145736 | tf_op jit(solution)/shard_map/ppermute | solution.py:31
  784.2 96.9 %collective-permute-start.90 = (bf16[256,2048]{1,0:T(8,128)(2,1)}, bf16[256,2048]{1,0:T(8,128)(2,1)}, u32[]{:S(2)}, u32[]{:S(2)}) collective-permute-start(bf16[256,2048]{1,0:T(8,128)(2,1)} %fusion.43), channel_id=1, source_target_pairs={{0,8},{4,12},{8,16},{12,20},{16,24},{20,28},{24,0},{28,4},{1,9},{5... | collective-permute-start | bytes 3145736 | tf_op jit(solution)/shard_map/ppermute | solution.py:38
  812.5 86.1 %collective-permute-start.88 = (bf16[256,2048]{1,0:T(8,128)(2,1)}, bf16[256,2048]{1,0:T(8,128)(2,1)}, u32[]{:S(2)}, u32[]{:S(2)}) collective-permute-start(bf16[256,2048]{1,0:T(8,128)(2,1)} %fusion.42), channel_id=1, source_target_pairs={{0,16},{4,20},{8,24},{12,28},{16,0},{20,4},{24,8},{28,12},{1,17},{... | collective-permute-start | bytes 3145736 | tf_op jit(solution)/shard_map/ppermute | solution.py:38
  812.7 96.9 %collective-permute-start.86 = (bf16[256,2048]{1,0:T(8,128)(2,1)}, bf16[256,2048]{1,0:T(8,128)(2,1)}, u32[]{:S(2)}, u32[]{:S(2)}) collective-permute-start(bf16[256,2048]{1,0:T(8,128)(2,1)} %fusion.41), channel_id=1, source_target_pairs={{0,24},{4,28},{8,0},{12,4},{16,8},{20,12},{24,16},{28,20},{1,25},{... | collective-permute-start | bytes 3145736 | tf_op jit(solution)/shard_map/ppermute | solution.py:38
  916.2 69.4 %collective-permute-start.40 = (bf16[512,2048]{1,0:T(8,128)(2,1)}, bf16[512,2048]{1,0:T(8,128)(2,1)}, u32[]{:S(2)}, u32[]{:S(2)}) collective-permute-start(bf16[512,2048]{1,0:T(8,128)(2,1)} %get-tuple-element.210), channel_id=1, source_target_pairs={{0,1},{1,0},{2,3},{3,2},{4,5},{5,4},{6,7},{7,6},{8,9},{9,8},{10,11... | collective-permute-start | bytes 6291464 | tf_op jit(solution)/shard_map/ppermute | solution.py:31
  960.9 91.5 %collective-permute-start.64 = (f32[2,512]{1,0:T(2,128)S(1)}, f32[2,512]{1,0:T(2,128)S(1)}, u32[]{:S(2)}, u32[]{:S(2)}) collective-permute-start(f32[2,512]{1,0:T(2,128)S(1)} %slice.246), channel_id=1, source_target_pairs={{0,24},{4,28},{8,16},{12,20},{16,8},{20,12},{24,0},{28,4},{1,25},{... | collective-permute-start | bytes 12296 | tf_op jit(solution)/shard_map/ppermute | solution.py:31
  973.3 80.0 %collective-permute-start.65 = (f32[2,512]{1,0:T(2,128)S(1)}, f32[2,512]{1,0:T(2,128)S(1)}, u32[]{:S(2)}, u32[]{:S(2)}) collective-permute-start(f32[2,512]{1,0:T(2,128)S(1)} %slice.246), channel_id=1, source_target_pairs={{0,28},{4,24},{8,20},{12,16},{16,12},{20,8},{24,4},{28,0},{1,29},{... | collective-permute-start | bytes 12296 | tf_op jit(solution)/shard_map/ppermute | solution.py:31
  1004.4 52.1 %collective-permute-start.62 = (f32[2,512]{1,0:T(2,128)S(1)}, f32[2,512]{1,0:T(2,128)S(1)}, u32[]{:S(2)}, u32[]{:S(2)}) collective-permute-start(f32[2,512]{1,0:T(2,128)S(1)} %slice.246), channel_id=1, source_target_pairs={{0,16},{4,20},{8,24},{12,28},{16,0},{20,4},{24,8},{28,12},{1,17},{... | collective-permute-start | bytes 12296 | tf_op jit(solution)/shard_map/ppermute | solution.py:31
  1046.8 106.5 %collective-permute-start.52 = (bf16[512,2048]{1,0:T(8,128)(2,1)}, bf16[512,2048]{1,0:T(8,128)(2,1)}, u32[]{:S(2)}, u32[]{:S(2)}) collective-permute-start(bf16[512,2048]{1,0:T(8,128)(2,1)} %add_convert_fusion.1), channel_id=1, source_target_pairs={{0,2},{1,3},{2,0},{3,1},{4,6},{5,7},{6,4},{7,5},{8,10},{9,11},{10,... | collective-permute-start | bytes 6291464 | tf_op jit(solution)/shard_map/ppermute | solution.py:31
  1061.5 48.3 %collective-permute-start.82 = (bf16[256,512]{1,0:T(8,128)(2,1)S(1)}, bf16[256,512]{1,0:T(8,128)(2,1)S(1)}, u32[]{:S(2)}, u32[]{:S(2)}) collective-permute-start(bf16[256,512]{1,0:T(8,128)(2,1)S(1)} %get-tuple-element.222), channel_id=1, source_target_pairs={{0,16},{4,20},{8,24},{12,28},{16,0},{20,4},{24,8},{28,12},{1,17},{... | collective-permute-start | bytes 786440 | tf_op jit(solution)/shard_map/ppermute | solution.py:38
  1062.6 47.2 %collective-permute-start.81 = (bf16[256,512]{1,0:T(8,128)(2,1)S(1)}, bf16[256,512]{1,0:T(8,128)(2,1)S(1)}, u32[]{:S(2)}, u32[]{:S(2)}) collective-permute-start(bf16[256,512]{1,0:T(8,128)(2,1)S(1)} %get-tuple-element.220), channel_id=1, source_target_pairs={{0,24},{4,28},{8,0},{12,4},{16,8},{20,12},{24,16},{28,20},{1,25},{... | collective-permute-start | bytes 786440 | tf_op jit(solution)/shard_map/ppermute | solution.py:38
  1068.2 49.3 %collective-permute-start.73 = (bf16[256,1536]{1,0:T(8,128)(2,1)}, bf16[256,1536]{1,0:T(8,128)(2,1)}, u32[]{:S(2)}, u32[]{:S(2)}) collective-permute-start(bf16[256,1536]{1,0:T(8,128)(2,1)} %convolution_convert_fusion.15), channel_id=1, source_target_pairs={{0,4},{4,0},{8,12},{12,8},{16,20},{20,16},{24,28},{28,24},{1,5},{5... | collective-permute-start | bytes 2359304 | tf_op jit(solution)/shard_map/ppermute | solution.py:31
  1069.2 48.3 %collective-permute-start.79 = (bf16[256,1536]{1,0:T(8,128)(2,1)}, bf16[256,1536]{1,0:T(8,128)(2,1)}, u32[]{:S(2)}, u32[]{:S(2)}) collective-permute-start(bf16[256,1536]{1,0:T(8,128)(2,1)} %add_convert_fusion.10), channel_id=1, source_target_pairs={{0,8},{4,12},{8,16},{12,20},{16,24},{20,28},{24,0},{28,4},{1,9},{5... | collective-permute-start | bytes 2359304 | tf_op jit(solution)/shard_map/ppermute | solution.py:38
  1173.4 78.6 %collective-permute-start.53 = (f32[512,2048]{1,0:T(8,128)}, f32[512,2048]{1,0:T(8,128)}, u32[]{:S(2)}, u32[]{:S(2)}) collective-permute-start(f32[512,2048]{1,0:T(8,128)} %fusion.24), channel_id=1, source_target_pairs={{0,1},{1,0},{2,3},{3,2},{4,5},{5,4},{6,7},{7,6},{8,9},{9,8},{10,11... | collective-permute-start | bytes 12582920 | tf_op jit(solution)/shard_map/ppermute | solution.py:31
  (145 other events, 2898.1 us)

commit v2 on v1

v2 whole, which is shorter than its diff:
```python
import functools
import math

import jax
import jax.numpy as jnp
from jax import lax
from jax.experimental import pallas as pl
from jax.experimental.pallas import tpu as pltpu
from jax.sharding import PartitionSpec as P

HEAD_DIM = 128
LEN = 1024


EPS = 1e-05
MOMENTUM = 0.9
RATE = 192.0
KEEP = 0.9
NEG = -1e30
BF16 = jnp.bfloat16
F32 = jnp.float32
MESH = pl.DeviceIdType.MESH


def dot_f32(eq, left, right):
    return jnp.einsum(eq, left, right, preferred_element_type=F32)


def swap(value, axis, flip):
    size = lax.axis_size(axis)
    return lax.ppermute(value, axis, [(i, i ^ flip) for i in range(size)])


def gather_kernel(outer, pieces, count, *refs):
    shards, wholes = refs[:count], refs[count : 2 * count]
    send, recv, local = refs[2 * count :]
    me = lax.axis_index("dp")
    out, side = me // 2, me % 2
    pair = out * 2 + 1 - side
    hops = outer - 1
    total = len(pieces)
    line = ((0, 1), (1, -1))

    def has(way, steps):
        return out >= steps if way > 0 else out + steps < outer

    def follows(way):
        return out + 1 < outer if way > 0 else out >= 1

    barrier = pltpu.get_barrier_semaphore()
    for peer in [lax.rem(out + r, outer) * 2 + side for r in range(1, outer)] + [pair]:
        pl.semaphore_signal(barrier, inc=1, device_id={"dp": peer}, device_id_type=MESH)
    pl.semaphore_wait(barrier, outer)

    def slot(p, device):
        a, plane, start, rows, _ = pieces[p]
        depth = shards[a].shape[-2]
        where = pl.ds(device * depth + start, rows)
        if plane is None:
            return wholes[a].at[where]
        width = shards[a].shape[-1]
        return wholes[a].at[where, pl.ds(plane * width, width)]

    def own(p):
        a, plane, start, rows, _ = pieces[p]
        where = pl.ds(start, rows)
        return shards[a].at[where] if plane is None else shards[a].at[plane, where]

    def remote(p, lane, source, target, peer):
        return pltpu.make_async_remote_copy(
            src_ref=source,
            dst_ref=target,
            send_sem=send.at[p, lane],
            recv_sem=recv.at[p, lane],
            device_id={"dp": peer},
            device_id_type=MESH,
        )

    def pass_on(p, other, index, way, steps):
        origin = (out - way * (steps - 1)) * 2 + (1 - side if other else side)
        here = slot(p, origin)
        source = own(p) if steps == 1 and not other else here
        lane = (2 * int(other) + index) * hops + steps - 1
        return remote(p, lane, source, here, (out + way) * 2 + side)

    def arrival(p, other, index, way, steps):
        origin = (out - way * steps) * 2 + (1 - side if other else side)
        lane = (2 * int(other) + index) * hops + steps - 1
        return remote(p, lane, slot(p, origin), slot(p, origin), pair)

    def to_pair(p, index, way, steps):
        if steps == 0:
            return remote(p, 4 * hops, own(p), slot(p, me), pair)
        here = slot(p, (out - way * steps) * 2 + side)
        return remote(p, (2 + index) * hops + steps - 1, here, here, pair)

    def begin(p):
        to_pair(p, 0, 1, 0).start()
        pltpu.make_async_copy(own(p), slot(p, me), local.at[p]).start()
        for index, way in line:

            @pl.when(follows(way))
            def _():
                pass_on(p, False, index, way, 1).start()

    def proceed(p, other, steps):
        early = pieces[p][4]
        for index, way in line:

            @pl.when(has(way, steps))
            def _():
                arrival(p, other, index, way, steps).wait_recv()
                if not early:
                    to_pair(p, index, way, steps).start()

            if steps < hops:

                @pl.when(jnp.logical_and(has(way, steps), follows(way)))
                def _():
                    pass_on(p, other, index, way, steps + 1).start()

    def cross(p):
        to_pair(p, 0, 1, 0).wait_recv()
        for index, way in line:

            @pl.when(follows(way))
            def _():
                pass_on(p, True, index, way, 1).start()

    lead = 4
    for p in range(min(lead, total)):
        begin(p)
    for wave in range(total + outer):
        if wave + lead < total:
            begin(wave + lead)
        if wave < total and pieces[wave][4]:
            cross(wave)
        for steps in range(1, outer):
            p = wave - steps + 1
            if 0 <= p < total:
                proceed(p, False, steps)
            p -= 1
            if 0 <= p < total and pieces[p][4]:
                proceed(p, True, steps)
    for p in range(total):
        early = pieces[p][4]
        to_pair(p, 0, 1, 0).wait_send()
        if not early:
            to_pair(p, 0, 1, 0).wait_recv()
        pltpu.make_async_copy(own(p), slot(p, me), local.at[p]).wait()
        for index, way in line:
            for other in (False, True) if early else (False,):
                for steps in range(1, outer):

                    @pl.when(jnp.logical_and(has(way, steps - 1), follows(way)))
                    def _():
                        pass_on(p, other, index, way, steps).wait_send()

            if not early:
                for steps in range(1, outer):

                    @pl.when(has(way, steps))
                    def _():
                        to_pair(p, index, way, steps).wait_send()
                        remote(
                            p,
                            (2 + index) * hops + steps - 1,
                            slot(p, me),
                            slot(p, (out - way * steps) * 2 + 1 - side),
                            pair,
                        ).wait_recv()


def gather_rows(shards, cuts, early, collective_id):
    size = lax.axis_size("dp")
    outer = size // 2
    count = len(shards)
    pieces, shapes = [], []
    for a, shard in enumerate(shards):
        depth, width = shard.shape[-2:]
        planes = [None] if shard.ndim == 2 else list(range(shard.shape[0]))
        rows = depth // cuts[a]
        for plane in planes:
            for i in range(cuts[a]):
                pieces.append((a, plane, i * rows, rows, len(pieces) in early))
        shapes.append(jax.ShapeDtypeStruct((size * depth, width * len(planes)), shard.dtype))
    anywhere = pl.BlockSpec(memory_space=pl.ANY)
    lanes = pltpu.SemaphoreType.DMA((len(pieces), 4 * outer - 3))
    return pl.pallas_call(
        functools.partial(gather_kernel, outer, pieces, count),
        out_shape=shapes,
        in_specs=[anywhere] * count,
        out_specs=[anywhere] * count,
        scratch_shapes=[lanes, lanes, pltpu.SemaphoreType.DMA((len(pieces),))],
        compiler_params=pltpu.CompilerParams(collective_id=collective_id, has_side_effects=True),
    )(*shards)


def reduce_kernel(outer, depth, cuts, count, crossings, *refs):
    refs = list(refs)

    def take(number):
        return [refs.pop(0) for _ in range(number)]

    grads, (total_ref,), crossed = take(count), take(1), take(crossings)
    raws, (square_ref,), taken = take(count), take(1), take(crossings)
    rest = refs
    own, got, given, come = [rest[i * count : (i + 1) * count] for i in range(4)]
    pair_send, pair_recv, turn_send, turn_recv, local, cross_send, cross_recv = rest[4 * count :]
    me, across = lax.axis_index("dp"), lax.axis_index("mp")
    out, side = me // 2, me % 2
    pair = out * 2 + 1 - side
    other = lax.rem(across + 2, 4)

    def member(steps):
        return lax.rem(out + steps, outer) * 2 + side

    barrier = pltpu.get_barrier_semaphore()
    for peer in [member(r) for r in range(1, outer)] + [pair]:
        pl.semaphore_signal(barrier, inc=1, device_id={"dp": peer}, device_id_type=MESH)
    pl.semaphore_signal(barrier, inc=1, device_id={"mp": other}, device_id_type=MESH)
    pl.semaphore_wait(barrier, outer + 1)

    crosses = [
        pltpu.make_async_remote_copy(
            src_ref=crossed[i],
            dst_ref=taken[i],
            send_sem=cross_send.at[i],
            recv_sem=cross_recv.at[i],
            device_id={"mp": other},
            device_id_type=MESH,
        )
        for i in range(crossings)
    ]
    for cross in crosses:
        cross.start()
    loads = [
        pltpu.make_async_copy(grads[a].at[pl.ds(0, outer * depth)], own[a], local.at[a])
        for a in range(count)
    ]
    for load in loads:
        load.start()

    pieces = []
    for a in range(count):
        rows = depth // cuts[a]
        pieces += [(a, i * rows, rows) for i in range(cuts[a])]
    order = list(range(1, outer)) + [0]

    def to_pair(p, a, start, rows, r):
        return pltpu.make_async_remote_copy(
            src_ref=grads[a].at[pl.ds((outer + r) * depth + start, rows)],
            dst_ref=got[a].at[pl.ds(r * depth + start, rows)],
            send_sem=pair_send.at[p, r],
            recv_sem=pair_recv.at[p, r],
            device_id={"dp": pair},
            device_id_type=MESH,
        )

    def to_member(p, a, start, rows, r):
        return pltpu.make_async_remote_copy(
            src_ref=given[a].at[pl.ds(r * depth + start, rows)],
            dst_ref=come[a].at[pl.ds(r * depth + start, rows)],
            send_sem=turn_send.at[p, r],
            recv_sem=turn_recv.at[p, r],
            device_id={"dp": member(outer - r)},
            device_id_type=MESH,
        )

    for p, piece in enumerate(pieces):
        for r in order:
            to_pair(p, *piece, r).start()
    for load in loads:
        load.wait()
    for p, (a, start, rows) in enumerate(pieces):
        for r in order:
            where = pl.ds(r * depth + start, rows)
            to_pair(p, a, start, rows, r).wait_recv()
            part = own[a][where].astype(F32) + got[a][where].astype(F32)
            if r:
                given[a][where] = part.astype(BF16)
                to_member(p, a, start, rows, r).start()
            else:
                raws[a][pl.ds(start, rows)] = part
    total = total_ref[0:1, 0:1]
    square = jnp.zeros((1, 1), F32)
    for p, (a, start, rows) in enumerate(pieces):
        part = raws[a][pl.ds(start, rows)]
        for r in range(1, outer):
            to_member(p, a, start, rows, r).wait_recv()
            part = part + come[a][pl.ds(r * depth + start, rows)].astype(F32)
        part = part / total
        raws[a][pl.ds(start, rows)] = part
        square = square + jnp.sum(part * part, keepdims=True)
    square_ref[...] = jnp.broadcast_to(square, square_ref.shape)
    for p, piece in enumerate(pieces):
        for r in order:
            to_pair(p, *piece, r).wait_send()
            if r:
                to_member(p, *piece, r).wait_send()
    for cross in crosses:
        cross.wait()


def reduce_rows(grads, total, crossed, cuts, collective_id):
    size = lax.axis_size("dp")
    outer = size // 2
    count, depth, number = len(grads), grads[0].shape[0] // size, sum(cuts)
    anywhere = pl.BlockSpec(memory_space=pl.ANY)
    inside = pl.BlockSpec(memory_space=pltpu.VMEM)
    buffers = [pltpu.VMEM((outer * depth, grad.shape[1]), BF16) for grad in grads]
    ways = pltpu.SemaphoreType.DMA((number, outer))
    crossings = len(crossed)
    results = pl.pallas_call(
        functools.partial(reduce_kernel, outer, depth, cuts, count, crossings),
        out_shape=[jax.ShapeDtypeStruct((depth, grad.shape[1]), F32) for grad in grads]
        + [jax.ShapeDtypeStruct((8, 128), F32)]
        + [jax.ShapeDtypeStruct(part.shape, part.dtype) for part in crossed],
        in_specs=[anywhere] * count + [inside] + [anywhere] * crossings,
        out_specs=[inside] * (count + 1) + [anywhere] * crossings,
        scratch_shapes=buffers * 4
        + [ways] * 4
        + [pltpu.SemaphoreType.DMA((count,))]
        + [pltpu.SemaphoreType.DMA((crossings,))] * 2,
        compiler_params=pltpu.CompilerParams(
            collective_id=collective_id, has_side_effects=True, vmem_limit_bytes=56 << 20
        ),
    )(*grads, total, *crossed)
    return results[:count], results[count], results[count + 1 :]


def finish_kernel(dp_count, mp_count, *refs):
    norm_ref, bias_ref, square_ref, total_ref, whole_ref = refs[:5]
    norm_out, bias_out, square_out, whole_out = refs[5:9]
    norm_in, bias_in, square_in, square_own = refs[9:13]
    norm_send, norm_recv, bias_send, bias_recv, square_send, square_recv = refs[13:19]
    whole_send, whole_recv = refs[19:21]
    me, across = lax.axis_index("dp"), lax.axis_index("mp")
    side = across % 2
    near = across + 1 - 2 * side

    def spot(kd, km):
        return {"dp": lax.rem(me + kd, dp_count), "mp": lax.rem(across + km, mp_count)}

    hops = [(kd, km) for kd in range(dp_count) for km in range(mp_count)][1:]
    barrier = pltpu.get_barrier_semaphore()
    for kd, km in hops:
        pl.semaphore_signal(barrier, inc=1, device_id=spot(kd, km), device_id_type=MESH)
    pl.semaphore_wait(barrier, len(hops))

    def send(source, target, send_sem, recv_sem, device):
        return pltpu.make_async_remote_copy(
            src_ref=source,
            dst_ref=target,
            send_sem=send_sem,
            recv_sem=recv_sem,
            device_id=device,
            device_id_type=MESH,
        )

    whole = send(whole_ref, whole_out, whole_send, whole_recv, {"mp": near})
    sent = []
    for kd in range(dp_count):
        owner = lax.rem(me + kd, dp_count)
        for flip in range(2):
            if kd or flip:
                column = near if flip else across
                copy = send(
                    norm_ref.at[owner],
                    norm_in.at[me * 2 + side],
                    norm_send.at[kd, flip],
                    norm_recv.at[kd, flip],
                    {"dp": owner, "mp": column},
                )
                copy.start()
                sent.append(copy)
    for kd in range(1, dp_count):
        copy = send(bias_ref, bias_in.at[me], bias_send.at[kd], bias_recv.at[kd], spot(kd, 0))
        copy.start()
        sent.append(copy)
    whole.start()
    norm_in[me * 2 + side] = norm_ref[me]
    bias_in[me] = bias_ref[...]
    for copy in sent:
        copy.wait_recv()
    total = total_ref[0:1, 0:1]
    norm = norm_in[0]
    for i in range(1, 2 * dp_count):
        norm = norm + norm_in[i]
    bias = bias_in[0]
    for i in range(1, dp_count):
        bias = bias + bias_in[i]
    norm = norm / total
    bias = bias / total
    norm_out[...] = norm
    bias_out[...] = bias
    square = jnp.sum(norm * norm, keepdims=True) / float(mp_count)
    square = square + jnp.sum(bias * bias, keepdims=True) / float(dp_count)
    square_own[...] = square_ref[...] + square
    slot = me * mp_count + across
    square_in[slot] = square_own[...]
    last = []
    for i, (kd, km) in enumerate(hops):
        copy = send(
            square_own, square_in.at[slot], square_send.at[i], square_recv.at[i], spot(kd, km)
        )
        copy.start()
        last.append(copy)
    for copy in last:
        copy.wait_recv()
    square = square_in[0]
    for i in range(1, dp_count * mp_count):
        square = square + square_in[i]
    square_out[...] = square
    for copy in sent + last:
        copy.wait_send()
    whole.wait()


def finish_sums(norm_part, bias_part, square, total, whole, collective_id):
    dp_count, mp_count = lax.axis_size("dp"), lax.axis_size("mp")
    anywhere = pl.BlockSpec(memory_space=pl.ANY)
    inside = pl.BlockSpec(memory_space=pltpu.VMEM)
    tile = jax.ShapeDtypeStruct((8, 128), F32)
    hops = dp_count * mp_count - 1
    return pl.pallas_call(
        functools.partial(finish_kernel, dp_count, mp_count),
        out_shape=[
            jax.ShapeDtypeStruct(norm_part.shape[1:], F32),
            jax.ShapeDtypeStruct(bias_part.shape, F32),
            tile,
            jax.ShapeDtypeStruct(whole.shape, whole.dtype),
        ],
        in_specs=[inside] * 4 + [anywhere],
        out_specs=[inside] * 3 + [anywhere],
        scratch_shapes=[
            pltpu.VMEM((2 * dp_count, *norm_part.shape[1:]), F32),
            pltpu.VMEM((dp_count, *bias_part.shape), F32),
            pltpu.VMEM((dp_count * mp_count, 8, 128), F32),
            pltpu.VMEM((8, 128), F32),
        ]
        + [pltpu.SemaphoreType.DMA((dp_count, 2))] * 2
        + [pltpu.SemaphoreType.DMA((dp_count,))] * 2
        + [pltpu.SemaphoreType.DMA((hops,))] * 2
        + [pltpu.SemaphoreType.DMA] * 2,
        compiler_params=pltpu.CompilerParams(
            collective_id=collective_id, has_side_effects=True, vmem_limit_bytes=32 << 20
        ),
    )(norm_part, bias_part, square, total, whole)


def step_kernel(count, whole_count, square_ref, total_ref, *refs):
    raws, masters, moments, averages = [refs[i * count : (i + 1) * count] for i in range(4)]
    outs = [refs[(4 + i) * count : (5 + i) * count] for i in range(5)]
    clip = jnp.minimum(1.0, 1.0 / (jnp.sqrt(square_ref[0:1, 0:1]) + 1e-06))
    total = total_ref[0:1, 0:1]

    def update(raw, master, moment, average):
        if raw.dtype == BF16:
            raw = raw.astype(F32) / total
        clipped = raw * clip
        momentum = MOMENTUM * moment + clipped
        updated = master - RATE * (clipped + MOMENTUM * momentum)
        averaged = KEEP * average + (1.0 - KEEP) * updated
        return clipped, momentum, averaged, updated, updated.astype(BF16)

    def apply(a):
        if len(masters[a].shape) == 2:
            results = update(raws[a][...], masters[a][...], moments[a][...], averages[a][...])
            for out, result in zip(outs, results):
                out[a][...] = result
        else:
            width = masters[a].shape[2]
            for c in range(masters[a].shape[0]):
                results = update(
                    raws[a][:, c * width : (c + 1) * width],
                    masters[a][c],
                    moments[a][c],
                    averages[a][c],
                )
                for out, result in zip(outs, results):
                    out[a][c] = result

    for a in range(whole_count, count):
        apply(a)

    @pl.when(pl.program_id(0) == 0)
    def _():
        for a in range(whole_count):
            apply(a)


def step_all(square, total, raws, masters, moments, averages, whole_count):
    depth = raws[-1].shape[0]
    rows = min(32, depth)

    def spec(value, a):
        shape = value.shape
        if a < whole_count:
            return pl.BlockSpec(shape, lambda i, n=len(shape): (0,) * n)
        if len(shape) == 3:
            return pl.BlockSpec((shape[0], rows, shape[2]), lambda i: (0, i, 0))
        return pl.BlockSpec((rows, shape[1]), lambda i: (i, 0))

    def specs(values):
        return [spec(value, a) for a, value in enumerate(values)]

    tile = pl.BlockSpec((8, 128), lambda i: (0, 0))
    wide = [jax.ShapeDtypeStruct(master.shape, F32) for master in masters]
    slim = [jax.ShapeDtypeStruct(master.shape, BF16) for master in masters]
    results = pl.pallas_call(
        functools.partial(step_kernel, len(masters), whole_count),
        grid=(depth // rows,),
        out_shape=wide * 4 + slim,
        in_specs=[tile, tile] + specs(raws) + specs(masters) * 3,
        out_specs=specs(masters) * 5,
        compiler_params=pltpu.CompilerParams(vmem_limit_bytes=56 << 20),
    )(square, total, *raws, *masters, *moments, *averages)
    count = len(masters)
    return [results[i * count : (i + 1) * count] for i in range(5)]


def merge_kernel(side_ref, own_ref, other_ref, out_ref):
    @pl.when(pl.program_id(0) == 0)
    def _():
        out_ref[...] = own_ref[...]

    @pl.when(pl.program_id(0) == 1)
    def _():
        out_ref[...] = other_ref[...]


def merge_halves(side, own, other):
    half, width = own.shape
    rows = min(128, half)
    steps = half // rows
    return pl.pallas_call(
        merge_kernel,
        out_shape=jax.ShapeDtypeStruct((2 * half, width), own.dtype),
        grid_spec=pltpu.PrefetchScalarGridSpec(
            num_scalar_prefetch=1,
            grid=(2, steps),
            in_specs=[
                pl.BlockSpec((rows, width), lambda h, i, side: (jnp.where(h == 0, i, steps - 1), 0)),
                pl.BlockSpec((rows, width), lambda h, i, side: (jnp.where(h == 0, 0, i), 0)),
            ],
            out_specs=pl.BlockSpec(
                (rows, width),
                lambda h, i, side: (jnp.where(h == 0, side[0], 1 - side[0]) * steps + i, 0),
            ),
        ),
    )(jnp.reshape(side, (1,)).astype(jnp.int32), own, other)


def score_block(query_ref, key_ref, first, rows, scale):
    width = first + rows
    scores = scale * lax.dot_general(
        query_ref[first:width], key_ref[:width], (((1,), (1,)), ((), ())), preferred_element_type=F32
    )
    row = first + lax.broadcasted_iota(jnp.int32, (rows, width), 0)
    column = lax.broadcasted_iota(jnp.int32, (rows, width), 1)
    scores = jnp.where(column <= row, scores, NEG)
    raised = jnp.exp(scores - jnp.max(scores, axis=-1, keepdims=True))
    return raised / jnp.sum(raised, axis=-1, keepdims=True)


def attend_kernel(rows, scale, query_ref, key_ref, value_ref, out_ref):
    for first in range(0, query_ref.shape[0], rows):
        prob = score_block(query_ref, key_ref, first, rows, scale)
        out_ref[first : first + rows] = jnp.dot(
            prob.astype(BF16), value_ref[: first + rows], preferred_element_type=F32
        ).astype(BF16)


def attend_back_kernel(
    rows, scale, query_ref, key_ref, value_ref, back_ref, gq_ref, gk_ref, gv_ref, key_sum, value_sum
):
    key_sum[...] = jnp.zeros_like(key_sum)
    value_sum[...] = jnp.zeros_like(value_sum)
    over_rows = (((0,), (0,)), ((), ()))
    for first in range(0, query_ref.shape[0], rows):
        width = first + rows
        prob = score_block(query_ref, key_ref, first, rows, scale)
        back = back_ref[first:width]
        back_prob = lax.dot_general(
            back, value_ref[:width], (((1,), (1,)), ((), ())), preferred_element_type=F32
        )
        value_sum[:width] += lax.dot_general(
            prob.astype(BF16), back, over_rows, preferred_element_type=F32
        )
        slope = jnp.sum(prob * back_prob, axis=-1, keepdims=True)
        back_score = (prob * (back_prob - slope)).astype(BF16)
        gq_ref[first:width] = (
            scale * jnp.dot(back_score, key_ref[:width], preferred_element_type=F32)
        ).astype(BF16)
        key_sum[:width] += lax.dot_general(
            back_score, query_ref[first:width], over_rows, preferred_element_type=F32
        )
    gk_ref[...] = (scale * key_sum[...]).astype(BF16)
    gv_ref[...] = value_sum[...].astype(BF16)


def attend(qkv, seq_count, heads):
    seq_len = qkv.shape[0] // seq_count
    rows = min(256, seq_len)
    columns = [
        pl.BlockSpec((seq_len, HEAD_DIM), lambda i, h, part=part: (i, part * heads + h))
        for part in range(3)
    ]
    return pl.pallas_call(
        functools.partial(attend_kernel, rows, 1.0 / math.sqrt(HEAD_DIM)),
        grid=(seq_count, heads),
        out_shape=jax.ShapeDtypeStruct((qkv.shape[0], heads * HEAD_DIM), BF16),
        in_specs=columns,
        out_specs=columns[0],
        compiler_params=pltpu.CompilerParams(vmem_limit_bytes=48 << 20),
    )(qkv, qkv, qkv)


def attend_back(qkv, back, seq_count, heads):
    seq_len = qkv.shape[0] // seq_count
    rows = min(256, seq_len)
    columns = [
        pl.BlockSpec((seq_len, HEAD_DIM), lambda i, h, part=part: (i, part * heads + h))
        for part in range(3)
    ]
    grads = jax.ShapeDtypeStruct((qkv.shape[0], heads * HEAD_DIM), BF16)
    return pl.pallas_call(
        functools.partial(attend_back_kernel, rows, 1.0 / math.sqrt(HEAD_DIM)),
        grid=(seq_count, heads),
        out_shape=[grads] * 3,
        in_specs=columns + columns[:1],
        out_specs=columns[:1] * 3,
        scratch_shapes=[pltpu.VMEM((seq_len, HEAD_DIM), F32)] * 2,
        compiler_params=pltpu.CompilerParams(vmem_limit_bytes=48 << 20),
    )(qkv, qkv, qkv, back)


def norm_stats(value):
    centre = jnp.mean(value, axis=-1, keepdims=True)
    centred = value - centre
    spread = jnp.mean(centred * centred, axis=-1, keepdims=True)
    inverse = lax.rsqrt(spread + EPS)
    return centred * inverse, inverse


def gelu_parts(value):
    inner = 0.7978845608028654 * (value + 0.044715 * value * value * value)
    return jnp.tanh(inner)


def gelu_tanh(value):
    return 0.5 * value * (1.0 + gelu_parts(value))


def gelu_slope(value):
    tanh = gelu_parts(value)
    rise = 0.7978845608028654 * (1.0 + 3.0 * 0.044715 * value * value)
    return 0.5 * (1.0 + tanh) + 0.5 * value * (1.0 - tanh * tanh) * rise


def local(
    tokens,
    out_cot,
    lengths,
    seq_family,
    family_tokens,
    norm_master,
    attn_bias_master,
    qkv_master,
    proj_master,
    fc_bias_master,
    fc_master,
    down_master,
    norm_moment,
    attn_bias_moment,
    qkv_moment,
    proj_moment,
    fc_bias_moment,
    fc_moment,
    down_moment,
    norm_average,
    attn_bias_average,
    qkv_average,
    proj_average,
    fc_bias_average,
    fc_average,
    down_average,
):
    seq_count = lengths.shape[0]
    row_count = tokens.shape[0]
    seq_len = row_count // seq_count
    family_count = family_tokens.shape[0]
    depth, _, head_width = qkv_master.shape
    local_heads = head_width // HEAD_DIM
    mp_count = lax.axis_size("mp")
    dp_count = lax.axis_size("dp")
    outer = dp_count // 2
    place = lax.axis_index("dp")
    place_out, place_in = place // 2, place % 2
    side = lax.axis_index("mp") % 2
    half = row_count // 2

    def block_at(s, r):
        return ((place_out + (outer - r)) % outer) * 2 + (place_in + s) % 2

    def to_local(value):
        parts = [
            lax.dynamic_slice_in_dim(value, block_at(s, r) * depth, depth, 1)
            for s in range(2)
            for r in range(outer)
        ]
        return jnp.concatenate(parts, axis=1)

    def own_rows(value):
        return lax.dynamic_slice_in_dim(value, side * half, half, 0)

    def other_rows(value):
        return lax.dynamic_slice_in_dim(value, (1 - side) * half, half, 0)

    def halves_swapped(own, other):
        return jnp.where(
            side == 0,
            jnp.concatenate([own, other], axis=0),
            jnp.concatenate([other, own], axis=0),
        )

    columns = norm_master.shape[1]
    low_norm = jnp.pad(norm_master.astype(BF16).T, ((0, 16 - columns), (0, 0)))
    low_qkv = jnp.moveaxis(qkv_master, 1, 0).astype(BF16)
    low_proj = proj_master.astype(BF16)
    low_fc = fc_master.astype(BF16)
    low_down = down_master.astype(BF16)

    family_ids = jnp.arange(family_count, dtype=jnp.int32)
    member = seq_family == family_ids[None, :]
    local_counts = jnp.sum(jnp.where(member, lengths[:, None], 0), axis=0).astype(F32)
    count_tile = jnp.broadcast_to(jnp.pad(local_counts, (0, 128 - family_count))[None], (8, 128))
    w_norm, all_counts, w_qkv, w_proj, w_fc = gather_rows(
        [low_norm, count_tile, low_qkv, low_proj, low_fc], (1, 1, 2, 2, 8), (3, 8, 13), 0
    )
    w_norm = jnp.moveaxis(w_norm.reshape(dp_count, 16, depth), 0, 1).reshape(16, dp_count * depth)
    counts = jnp.sum(all_counts.reshape(dp_count, 8, 128)[:, 0], axis=0)[:family_count]
    low_down, w_fc = lax.optimization_barrier((low_down, w_fc))
    w_down = lax.all_gather(low_down, "dp", axis=0, tiled=True)

    valid_total = jnp.sum(counts)
    share = family_tokens.astype(F32) / jnp.sum(family_tokens).astype(F32)
    family_weight = share * valid_total / jnp.maximum(counts, float(LEN // 2))
    seq_weight = jnp.sum(jnp.where(member, family_weight[None, :], 0.0), axis=1)
    places = jnp.arange(seq_len, dtype=jnp.int32)
    token_weight = jnp.where(places[None, :] < lengths[:, None], seq_weight[:, None], 0.0).reshape(
        row_count
    )

    norm_full = w_norm.astype(F32)
    gain1, shift1, gain2, shift2, bias_p, bias_d = [norm_full[i][None] for i in range(6)]
    bias_row = jnp.concatenate(
        [attn_bias_master[0], jnp.zeros_like(attn_bias_master[0]), attn_bias_master[1]], axis=0
    )
    x_low = tokens
    cot_low = out_cot

    x_hat, _ = norm_stats(x_low.astype(F32))
    ln1_low = (x_hat * gain1 + shift1).astype(BF16)
    qkv = (dot_f32("td,de->te", ln1_low, w_qkv) + bias_row[None]).astype(BF16)
    mixed_low = attend(qkv, seq_count, local_heads)
    mixed_low = halves_swapped(mixed_low[:half], mixed_low[half:])

    def sum_over_cores(product, left):
        other = swap(product(left[half:]).astype(BF16), "mp", 1)
        return (product(left[:half]) + other.astype(F32)).astype(BF16)

    def sum_over_mp(product, left):
        part = sum_over_cores(product, left)
        flip = 2
        while flip < mp_count:
            part = part.astype(F32) + swap(part, "mp", flip).astype(F32)
            flip *= 2
            if flip < mp_count:
                part = part.astype(BF16)
        return part.astype(F32)

    x_own = own_rows(x_low).astype(F32)
    attn_out = sum_over_mp(lambda rows: dot_f32("te,de->td", rows, w_proj), mixed_low)
    residual = x_own + attn_out + bias_p
    hat2, inverse2 = norm_stats(residual)
    ln2_own = (hat2 * gain2 + shift2).astype(BF16)
    ln2_low = jnp.concatenate([ln2_own, swap(ln2_own, "mp", 1)], axis=0)
    pre_act = dot_f32("td,df->tf", ln2_low, w_fc) + fc_bias_master[None]
    hidden_low = gelu_tanh(pre_act).astype(BF16)

    weight_own, weight_other = own_rows(token_weight), other_rows(token_weight)
    upstream = weight_own[:, None] * own_rows(cot_low).astype(F32)
    upstream_other = weight_other[:, None] * other_rows(cot_low).astype(F32)
    upstream_low = jnp.concatenate([upstream, upstream_other], axis=0).astype(BF16)

    def scatter_product(product):
        return lax.psum_scatter(product, "dp", scatter_dimension=0, tiled=True)

    down_product = dot_f32("td,tf->df", upstream_low, hidden_low).astype(BF16)
    down_reduced = scatter_product(down_product)

    back_act = dot_f32("td,df->tf", upstream_low, w_down)
    back_pre = (back_act * gelu_slope(pre_act)).astype(BF16)
    fc_bias_sum = jnp.sum(back_pre, axis=0, dtype=F32)
    fc_product = dot_f32("td,tf->df", ln2_low, back_pre).astype(BF16)

    def norm_back(back, hat, inverse, gain):
        scaled = back * gain
        mean = jnp.mean(scaled, axis=-1, keepdims=True)
        slope = jnp.mean(scaled * hat, axis=-1, keepdims=True)
        return inverse * (scaled - mean - hat * slope)

    back_ln2 = sum_over_mp(lambda rows: dot_f32("tf,df->td", rows, w_fc), back_pre)
    mlp_part = sum_over_cores(lambda rows: dot_f32("tf,df->td", rows, w_down), hidden_low)
    fc_product, mlp_part, back_ln2 = lax.optimization_barrier((fc_product, mlp_part, back_ln2))
    fc_reduced = scatter_product(fc_product)
    gain2_sum = jnp.sum(back_ln2 * hat2, axis=0)
    shift2_sum = jnp.sum(back_ln2, axis=0)
    back_resid = upstream + norm_back(back_ln2, hat2, inverse2, gain2)
    ga_own = back_resid.astype(BF16)
    ga_low = jnp.concatenate([ga_own, swap(ga_own, "mp", 1)], axis=0)
    back_mixed = dot_f32("td,de->te", ga_low, w_proj).astype(BF16)
    back_mixed = halves_swapped(back_mixed[:half], back_mixed[half:])
    back_qkv = jnp.concatenate(attend_back(qkv, back_mixed, seq_count, local_heads), axis=1)
    attn_bias_sum = jnp.sum(back_qkv, axis=0, dtype=F32).reshape(3, head_width)[0::2]
    back_qkv_local = halves_swapped(back_qkv[:half], back_qkv[half:])
    back_part = sum_over_cores(lambda rows: dot_f32("te,de->td", rows, w_qkv), back_qkv_local)
    qkv_part = dot_f32("td,te->de", to_local(ln1_low), back_qkv).astype(BF16)
    proj_part = dot_f32("td,te->de", to_local(ga_low), mixed_low).astype(BF16)
    total_tile = jnp.broadcast_to(valid_total, (8, 128))
    (qkv_raw, proj_raw), square, (back_taken, mlp_taken) = reduce_rows(
        [qkv_part, proj_part], total_tile, [back_part, mlp_part], (4, 1), 1
    )
    back_ln1 = back_part.astype(F32) + back_taken.astype(F32)
    mlp_out = mlp_part.astype(F32) + mlp_taken.astype(F32)
    block_own = (residual + mlp_out + bias_d).astype(BF16)
    hat1, inverse1 = norm_stats(x_own)
    gain1_sum = jnp.sum(back_ln1 * hat1, axis=0)
    shift1_sum = jnp.sum(back_ln1, axis=0)
    whole_own = back_resid + norm_back(back_ln1, hat1, inverse1, gain1)

    norm_part = jnp.stack(
        [
            gain1_sum,
            shift1_sum,
            gain2_sum,
            shift2_sum,
            jnp.sum(back_resid, axis=0),
            jnp.sum(upstream, axis=0),
            jnp.zeros_like(gain1_sum),
            jnp.zeros_like(gain1_sum),
        ],
        axis=0,
    )
    norm_part = jnp.moveaxis(norm_part.reshape(8, dp_count, depth), 1, 0)
    bias_part = jnp.concatenate([attn_bias_sum.reshape(-1), fc_bias_sum]).reshape(-1, 128)
    for reduced in (fc_reduced, down_reduced):
        raw = reduced.astype(F32) / valid_total
        square = square + jnp.sum(raw * raw)
    norm_raw, bias_raw, square, whole_other = finish_sums(
        norm_part, bias_part, square, total_tile, whole_own, 2
    )
    whole = merge_halves(side, whole_own, whole_other)
    block_part = merge_halves(side, block_own, swap(block_own, "mp", 1))
    grad_norm = jnp.sqrt(square[0, 0])
    bias_raw = bias_raw.reshape(-1)
    raw_grads = [
        norm_raw[:columns],
        bias_raw[: 2 * head_width].reshape(2, head_width),
        bias_raw[2 * head_width :].reshape(1, -1),
        qkv_raw,
        proj_raw,
        fc_reduced,
        down_reduced,
    ]
    masters = (
        norm_master,
        attn_bias_master,
        qkv_master,
        proj_master,
        fc_bias_master,
        fc_master,
        down_master,
    )
    moments = (
        norm_moment,
        attn_bias_moment,
        qkv_moment,
        proj_moment,
        fc_bias_moment,
        fc_moment,
        down_moment,
    )
    averages = (
        norm_average,
        attn_bias_average,
        qkv_average,
        proj_average,
        fc_bias_average,
        fc_average,
        down_average,
    )
    order = (0, 1, 4, 2, 3, 5, 6)

    def arranged(values):
        values = [values[i] for i in order]
        values[0] = values[0].T
        values[2] = values[2].reshape(1, -1)
        values[3] = jnp.moveaxis(values[3], 1, 0)
        return values

    def returned(values):
        values = list(values)
        values[0] = values[0].T
        values[2] = values[2].reshape(-1)
        values[3] = jnp.moveaxis(values[3], 0, 1)
        return [values[order.index(i)] for i in range(7)]

    grads_out, momenta_out, averaged_out, updated_out, copies_out = [
        returned(values)
        for values in step_all(
            square, total_tile, raw_grads, arranged(masters), arranged(moments), arranged(averages), 3
        )
    ]
    return (
        block_part,
        whole,
        grads_out[0],
        grads_out[1],
        grads_out[2],
        grads_out[3],
        grads_out[4],
        grads_out[5],
        grads_out[6],
        momenta_out[0],
        momenta_out[1],
        momenta_out[2],
        momenta_out[3],
        momenta_out[4],
        momenta_out[5],
        momenta_out[6],
        averaged_out[0],
        averaged_out[1],
        averaged_out[2],
        averaged_out[3],
        averaged_out[4],
        averaged_out[5],
        averaged_out[6],
        updated_out[0],
        updated_out[1],
        updated_out[2],
        updated_out[3],
        updated_out[4],
        updated_out[5],
        updated_out[6],
        copies_out[0],
        copies_out[1],
        copies_out[2],
        copies_out[3],
        copies_out[4],
        copies_out[5],
        copies_out[6],
        grad_norm,
    )


def solution(mesh):
    placed = (
        P("dp", None),
        P("dp", None),
        P("dp"),
        P("dp", None),
        P(),
        P("dp", None),
        P(None, "mp"),
        P("dp", None, "mp"),
        P("dp", "mp"),
        P("mp"),
        P("dp", "mp"),
        P("dp", "mp"),
        P("dp", None),
        P(None, "mp"),
        P("dp", None, "mp"),
        P("dp", "mp"),
        P("mp"),
        P("dp", "mp"),
        P("dp", "mp"),
        P("dp", None),
        P(None, "mp"),
        P("dp", None, "mp"),
        P("dp", "mp"),
        P("mp"),
        P("dp", "mp"),
        P("dp", "mp"),
    )
    return jax.shard_map(
        local,
        mesh=mesh,
        in_specs=placed,
        out_specs=(
            P("dp", None),
            P("dp", None),
            P("dp", None),
            P(None, "mp"),
            P("dp", None, "mp"),
            P("dp", "mp"),
            P("mp"),
            P("dp", "mp"),
            P("dp", "mp"),
            P("dp", None),
            P(None, "mp"),
            P("dp", None, "mp"),
            P("dp", "mp"),
            P("mp"),
            P("dp", "mp"),
            P("dp", "mp"),
            P("dp", None),
            P(None, "mp"),
            P("dp", None, "mp"),
            P("dp", "mp"),
            P("mp"),
            P("dp", "mp"),
            P("dp", "mp"),
            P("dp", None),
            P(None, "mp"),
            P("dp", None, "mp"),
            P("dp", "mp"),
            P("mp"),
            P("dp", "mp"),
            P("dp", "mp"),
            P("dp", None),
            P(None, "mp"),
            P("dp", None, "mp"),
            P("dp", "mp"),
            P("mp"),
            P("dp", "mp"),
            P("dp", "mp"),
            P(),
        ),
        check_vma=False,
    )
```

time: 1270 us -> 756 us (0.60)
  waiting for transfers between devices: 536 us -> 84.5 us
  Pallas kernels: 0 us -> 396 us
  starting transfers between devices: 304 us -> 4.08 us
  matrix products: 202 us -> 134 us
  local copies, waits for them, and re-layouts: 88.9 us -> 31.8 us
  other arithmetic: 118 us -> 76.8 us
    pallas_call x0 -> x8, Pallas kernels: none -> 396 us  [the longest x1 178 us: gather_rows(): pl.pallas_call(functools.partial(gather_kernel, outer, pieces, count), ou...]
    ppermute x30 -> x0, waiting for transfers between devices: 234 us -> none  [turn(): return lax.ppermute(value, 'dp', pairs)]
    ppermute x78 -> x9, waiting for transfers between devices: 302 us -> 72.6 us  [swap(): return lax.ppermute(value, axis, [(i, i ^ flip) for i in range(size)])]
    ppermute x30 -> x0, starting transfers between devices: 171 us -> none  [turn(): return lax.ppermute(value, 'dp', pairs)]
    ppermute x78 -> x9, starting transfers between devices: 133 us -> 3.96 us  [swap(): return lax.ppermute(value, axis, [(i, i ^ flip) for i in range(size)])]
    dot_general x44 -> x16, matrix products: 202 us -> 134 us  [dot_f32(): return jnp.einsum(eq, left, right, preferred_element_type=F32)]
    unnamed x241 -> x118, local copies, waits for them, and re-layouts: 70.4 us -> 25 us
    convert_element_type x9 -> x3, other arithmetic: 26 us -> 8.27 us  [the longest x1 4.88 us: local(): block_own = (residual + mlp_out + bias_d).astype(BF16)]
  transfers between devices with their start and end apart: 108 -> 12, of which waited for: 46 -> 4; matrix products, arithmetic and copies ran while one was open for 22% -> 28% of each run, Pallas kernels for 0% -> 23%
where the time goes in v2:
time: 756 us; the launch traced here: 746 us
  Pallas kernels  396 us (52%)
  matrix products  134 us (18%)
  waiting for transfers between devices  84.5 us (11%)
  other arithmetic  76.8 us (10%)
  local copies, waits for them, and re-layouts  31.8 us (4%)
  between operations  19.3 us (3%)
    pallas_call x1, Pallas kernels, gather_rows(): pl.pallas_call(functools.partial(gather_kernel, outer, pieces, count), ou...  178 us
    pallas_call x1, Pallas kernels, reduce_rows(): pl.pallas_call(functools.partial(reduce_kernel, outer, depth, cuts, count...  140 us
    dot_general x16, matrix products, dot_f32(): return jnp.einsum(eq, left, right, preferred_element_type=F32)  134 us
    ppermute x9, waiting for transfers between devices, swap(): return lax.ppermute(value, axis, [(i, i ^ flip) for i in range(size)])  72.6 us
    unnamed x118, local copies, waits for them, and re-layouts  25 us
    pallas_call x1, Pallas kernels, step_all(): pl.pallas_call(functools.partial(step_kernel, len(masters), whole_count),...  19.6 us
    pallas_call x2, Pallas kernels, merge_halves(): pl.pallas_call(merge_kernel, out_shape=jax.ShapeDtypeStruct((2 * half, wi...  16.6 us
    pallas_call x1, Pallas kernels, attend_back(): pl.pallas_call(functools.partial(attend_back_kernel, rows, 1.0 / math.sqr...  16.3 us
  transfers between devices with their start and end apart: 12, of which 4 were waited for; matrix products, arithmetic and copies ran while one was open for 28% of the time, Pallas kernels for 23%

profile of v2, /device:TPU:0, one launch (start us, length us, event | category | flops | bytes accessed | tf_op | source)
XLA Modules:
  0.0 746.3 jit_solution(2182210582681622503)
XLA Ops:
  9.8 2.4 bitcast_convert_fusion.refs_2_
  17.4 177.5 %shard_map.545 = (bf16[128,256]{1,0:T(8,128)(2,1)}, f32[64,128]{1,0:T(8,128)}, bf16[2048,1536]{1,0:T(8,128)(2,1)}, bf16[2048,512]{1,0:T(8,128)(2,1)}, bf16[2048,2048]{1,0:T(8,128)(2,1)}) custom-call(bf16[16,256]{1,0:T(8,128)(2,1)} %pad.8.refs_0_, f32[8,128]{1,0:T(8,128)} %broadcast_in_dim.41.refs_1_, bf16[3,256,512]{2,1,0:T(8,128)(2,1)} %bitcast_convert_fusion.refs_2_, ...), custom_call_target="tpu_custom_call" | custom-call | tf_op jit(solution)/shard_map/pallas_call | solution.py:189
  196.7 2.8 convert_reduce_fusion
  200.8 1.9 fusion.5
  202.8 1.9 copy-done.17
  204.7 6.9 add_convert_fusion.query_ref.key_ref.value_ref
  211.6 9.9 %shard_map.546 = bf16[1024,512]{1,0:T(8,128)(2,1)S(1)} custom-call(bf16[1024,1536]{1,0:T(8,128)(2,1)S(1)} %add_convert_fusion.query_ref.key_ref.value_ref, bf16[1024,1536]{1,0:T(8,128)(2,1)S(1)} %add_convert_fusion.query_ref.key_ref.value_ref, bf16[1024,1536]{1,0:T(8,128)(2,1)S(1)} %add_convert_fusion.query_ref.key_ref.value_ref), custom_call_target="tpu_custom_call" | custom-call | tf_op jit(solution)/shard_map/pallas_call | solution.py:610
  226.9 4.1 collective-permute-done
  233.9 1.9 convert_reduce_fusion.3
  235.8 44.3 %collective-permute-done.1 = bf16[512,2048]{1,0:T(8,128)(2,1)} collective-permute-done((bf16[512,2048]{1,0:T(8,128)(2,1)S(1)}, bf16[512,2048]{1,0:T(8,128)(2,1)}, u32[]{:S(2)}, u32[]{:S(2)}) %collective-permute-start.1) | collective-permute-done | bytes 2097184 | tf_op jit(solution)/shard_map/ppermute | solution.py:31
  280.2 4.1 fusion.78
  290.9 3.1 fusion.28
  294.1 16.9 %multiply_convert_fusion = (bf16[1024,2048]{1,0:T(8,128)(2,1)S(1)}, f32[1024,2048]{1,0:T(8,128)}) fusion(f32[2048]{0:T(1024)S(1)} %copy-done.36, bf16[2048,2048]{1,0:T(8,128)(2,1)} %get-tuple-element.101, bf16[512,2048]{1,0:T(8,128)(2,1)} %collective-permute-done.2, bf16[512,2048]{1,0:T(8,128)(2,1)S(1)} %add_convert_fusion.5), kind=kOutput, calls=%fused_computation.36 | convolution fusion | flops 8619294720 | bytes 25174016 | tf_op jit(solution)/shard_map/td,df->tf/dot_general | solution.py:26
  311.0 1.9 copy-done.43
  312.9 11.8 %convolution_convert_fusion = bf16[2048,2048]{1,0:T(8,128)(2,1)} fusion(bf16[1024,2048]{1,0:T(8,128)(2,1)S(1)} %get-tuple-element.184, bf16[512,2048]{1,0:T(8,128)(2,1)S(1)} %get-tuple-element.167, bf16[512,2048]{1,0:T(8,128)(2,1)S(1)} %get-tuple-element.166), kind=kOutput, calls=%fused_computation.37 | convolution fusion | flops 8602517504 | bytes 16777216 | tf_op jit(solution)/shard_map/td,tf->df/dot_general | solution.py:26
  324.9 19.2 %convert_reduce_fusion.1 = (f32[2048]{0:T(1024)S(1)}, bf16[1024,2048]{1,0:T(8,128)(2,1)S(1)}) fusion(f32[1024,2048]{1,0:T(8,128)} %get-tuple-element.185, f32[2048]{0:T(1024)S(1)} %copy-done.36, bf16[2048,2048]{1,0:T(8,128)(2,1)} %all-gather.2.cloned.1.call-done, bf16[512,2048]{1,0:T(8,128)(2,1)} %copy-done.25, bf16[512,2048]{1,0:T(8,128)(2,1)} %copy-done.24), kind=kOutput, calls=%fused_computation.35 | convolution fusion | flops 8644458496 | bytes 25182208 | tf_op jit(solution)/shard_map/td,df->tf/dot_general | solution.py:26
  344.1 2.0 copy-done.44
  346.1 9.3 %convolution_convert_fusion.5 = bf16[512,2048]{1,0:T(8,128)(2,1)} fusion(bf16[2048,2048]{1,0:T(8,128)(2,1)} %get-tuple-element.101, bf16[1024,2048]{1,0:T(8,128)(2,1)S(1)} %get-tuple-element.187), kind=kOutput, calls=%fused_computation.84 | convolution fusion | flops 4296015872 | bytes 12582912 | tf_op jit(solution)/shard_map/tf,df->td/dot_general | solution.py:26
  356.3 7.8 %convolution_convert_fusion.6 = bf16[512,2048]{1,0:T(8,128)(2,1)} fusion(bf16[2048,2048]{1,0:T(8,128)(2,1)S(1)} %copy-done.39, bf16[1024,2048]{1,0:T(8,128)(2,1)} %copy-done.43), kind=kOutput, calls=%fused_computation.85 | convolution fusion | flops 4296015872 | bytes 12582912 | tf_op jit(solution)/shard_map/tf,df->td/dot_general | solution.py:26
  364.1 8.2 %add_convert_fusion.3 = bf16[512,2048]{1,0:T(8,128)(2,1)} fusion(bf16[512,2048]{1,0:T(8,128)(2,1)} %collective-permute-done.4, bf16[2048,2048]{1,0:T(8,128)(2,1)S(1)} %bitcast.119, bf16[1024,2048]{1,0:T(8,128)(2,1)} %copy-done.44), kind=kOutput, calls=%fused_computation.67 | convolution fusion | flops 4298113024 | bytes 14680064 | tf_op jit(solution)/shard_map/tf,df->td/dot_general | solution.py:26
  373.4 12.8 %convolution_convert_fusion.2 = bf16[2048,2048]{1,0:T(8,128)(2,1)} fusion(bf16[1024,2048]{1,0:T(8,128)(2,1)S(1)} %copy-done.45, bf16[512,2048]{1,0:T(8,128)(2,1)} %collective-permute-done.2, bf16[512,2048]{1,0:T(8,128)(2,1)S(1)} %add_convert_fusion.5), kind=kOutput, calls=%fused_computation.39 | convolution fusion | flops 8602517504 | bytes 16777216 | tf_op jit(solution)/shard_map/td,tf->df/dot_general | solution.py:26
  386.2 10.5 %add_convert_fusion.4.refs_4_ = bf16[512,2048]{1,0:T(8,128)(2,1)} fusion(bf16[512,2048]{1,0:T(8,128)(2,1)} %collective-permute-done.3, bf16[2048,2048]{1,0:T(8,128)(2,1)} %all-gather.2.cloned.1.call-done, bf16[1024,2048]{1,0:T(8,128)(2,1)} %copy-done.43), kind=kOutput, calls=%fused_computation.68 | convolution fusion | flops 4298113024 | bytes 14680064 | tf_op jit(solution)/shard_map/tf,df->td/dot_general | solution.py:26
  396.7 24.1 %collective-permute-done.5 = bf16[512,2048]{1,0:T(8,128)(2,1)} collective-permute-done((bf16[512,2048]{1,0:T(8,128)(2,1)}, bf16[512,2048]{1,0:T(8,128)(2,1)}, u32[]{:S(2)}, u32[]{:S(2)}) %collective-permute-start.5) | collective-permute-done | bytes 2097184 | tf_op jit(solution)/shard_map/ppermute | solution.py:31
  420.8 5.0 convert_add_fusion.2
  425.9 5.1 multiply_reduce_fusion
  431.8 4.1 fusion.77
  435.9 2.0 copy-done.12
  444.0 1.9 copy-done.30
  446.0 4.0 fusion.48
  450.3 16.3 %shard_map.547 = (bf16[1024,512]{1,0:T(8,128)(2,1)S(1)}, bf16[1024,512]{1,0:T(8,128)(2,1)S(1)}, bf16[1024,512]{1,0:T(8,128)(2,1)S(1)}) custom-call(bf16[1024,1536]{1,0:T(8,128)(2,1)} %copy-done, bf16[1024,1536]{1,0:T(8,128)(2,1)} %copy-done, bf16[1024,1536]{1,0:T(8,128)(2,1)} %copy-done, bf16[1024,512]{1,0:T(8,128)(2,1)S(1)} %maximum_select_fusion.2.back_ref), custom_call_target="tpu_custom_call" | custom-call | tf_op jit(solution)/shard_map/pallas_call | solution.py:628
  468.0 2.2 slice-done.4
  470.9 5.0 convolution_convert_fusion.4
  485.4 3.8 convolution_convert_fusion.3.refs_1_
  489.2 8.9 %convolution_convert_fusion.1.refs_0_ = bf16[2048,1536]{1,0:T(8,128)(2,1)} fusion(bf16[1024,2048]{1,0:T(8,128)(2,1)S(1)} %copy-done.31, bf16[1024,1536]{1,0:T(8,128)(2,1)S(1)} %copy-done.15), kind=kOutput, calls=%fused_computation.38 | convolution fusion | flops 6445596672 | bytes 13631488 | tf_op jit(solution)/shard_map/td,te->de/dot_general | solution.py:26
  498.1 5.9 add_convert_fusion.2.refs_3_
  505.2 140.2 %shard_map.548 = (f32[256,1536]{1,0:T(8,128)}, f32[256,512]{1,0:T(8,128)}, f32[8,128]{1,0:T(8,128)}, bf16[512,2048]{1,0:T(8,128)(2,1)}, bf16[512,2048]{1,0:T(8,128)(2,1)}) custom-call(bf16[2048,1536]{1,0:T(8,128)(2,1)} %convolution_convert_fusion.1.refs_0_, bf16[2048,512]{1,0:T(8,128)(2,1)} %convolution_convert_fusion.3.refs_1_, ...), custom_call_target="tpu_custom_call" | custom-call | tf_op jit(solution)/shard_map/pallas_call | solution.py:314
  645.5 4.9 add_convert_fusion.1.own_ref
  650.4 2.7 fusion.23
  653.3 5.8 fusion.22.refs_4_.own_ref
  659.1 3.0 multiply_reduce_fusion.4
  662.1 7.2 shard_map.549
  669.3 11.8 %reduce-scatter.3.cloned.1.call-done.refs_5_ = bf16[256,2048]{1,0:T(8,128)(2,1)} async-done(((bf16[2048,2048]{1,0:T(8,128)(2,1)}), bf16[256,2048]{1,0:T(8,128)(2,1)}) %reduce-scatter.3.cloned.1.call-update) | async-done | bytes 1048592 | tf_op jit(solution)/shard_map/reduce_scatter | solution.py:799
  681.1 3.0 multiply_reduce_fusion.5
  685.4 2.2 copy-done.1
  687.6 16.0 %shard_map.550 = (f32[8,256]{1,0:T(8,128)S(1)}, f32[24,128]{1,0:T(8,128)S(1)}, f32[8,128]{1,0:T(8,128)S(1)}, f32[512,2048]{1,0:T(8,128)S(1)}) custom-call(f32[8,8,256]{2,1,0:T(8,128)S(1)} %bitcast.81, f32[24,128]{1,0:T(8,128)S(1)} %maximum_bitcast_fusion.refs_1_, f32[8,128]{1,0:T(8,128)S(1)} %add_add_fusion.refs_2_, f32[8,128]{1,0:T(8,128)S(1)} %copy-done.4, ...), custom_call_target="tpu_custom_call" | custom-call | tf_op jit(solution)/shard_map/pallas_call | solution.py:426
  703.7 1.9 copy-done.3
  706.2 9.5 %shard_map.551 = f32[1024,2048]{1,0:T(8,128)} custom-call(s32[1]{0:T(128)} %bitcast.side_ref, f32[512,2048]{1,0:T(8,128)} %fusion.22.refs_4_.own_ref, f32[512,2048]{1,0:T(8,128)} %copy-done.3), custom_call_target="tpu_custom_call" | custom-call | tf_op jit(solution)/shard_map/pallas_call | solution.py:537
  717.5 19.6 %shard_map.552 = (f32[6,256]{1,0:T(8,128)}, f32[2,512]{1,0:T(2,128)}, f32[1,2048]{1,0:T(1,128)}, f32[3,256,512]{2,1,0:T(8,128)}, f32[256,512]{1,0:T(8,128)}, /*i...) custom-call(f32[8,128]{1,0:T(8,128)} %copy-done.6, ...), custom_call_target="tpu_custom_call" | custom-call | tf_op jit(solution)/shard_map/pallas_call | solution.py:511
  (200 shorter events, 49.3 us)
Async XLA Ops:
  7.2 6.7 copy-start.20
  7.2 317.6 %all-gather.2.cloned.1.call-start = ((), (), s32[]{:S(2)}) async-start(), calls=%async_computation.2 | async-start | bytes 9437184 | tf_op jit(solution)/shard_map/all_gather | solution.py:745
  7.3 7.8 %copy-start.21 = (f32[256,2048]{1,0:T(8,128)S(1)}, f32[256,2048]{1,0:T(8,128)}, u32[]{:S(2)}) copy-start(f32[256,2048]{1,0:T(8,128)} %refs_13_.1) | copy-start | bytes 6291460
  195.0 464.1 %reduce-scatter.5.cloned.1.call-start = ((), (), s32[]{:S(2)}) async-start(), calls=%async_computation.4 | async-start | bytes 9437184 | tf_op jit(solution)/shard_map/reduce_scatter | solution.py:799
  195.0 4.5 copy-start.10
  196.7 4.1 copy-start.28
  196.7 4.1 copy-start.35
  199.5 5.1 slice-start.2
  200.8 3.8 slice-start.3
  211.6 9.9 %copy-start = (bf16[1024,1536]{1,0:T(8,128)(2,1)}, bf16[1024,1536]{1,0:T(8,128)(2,1)S(1)}, u32[]{:S(2)}) copy-start(bf16[1024,1536]{1,0:T(8,128)(2,1)S(1)} %add_convert_fusion.query_ref.key_ref.value_ref) | copy-start | bytes 9437188
  225.4 5.6 copy-start.26
  225.4 5.6 copy-start.41
  226.8 4.2 collective-permute-start
  232.3 47.8 %collective-permute-start.1 = (bf16[512,2048]{1,0:T(8,128)(2,1)S(1)}, bf16[512,2048]{1,0:T(8,128)(2,1)}, u32[]{:S(2)}, u32[]{:S(2)}) collective-permute-start(bf16[512,2048]{1,0:T(8,128)(2,1)S(1)} %add_convert_fusion.6), channel_id=1, source_target_pairs={{0,2},{1,3},{2,0},{3,1},{4,6},{5,7},{6,4},{7,5},{8,10},{9,11},{10,... | collective-permute-start | bytes 6291464 | tf_op jit(solution)/shard_map/ppermute | solution.py:31
  235.8 48.4 %copy-start.32 = (f32[512]{0:T(512)}, f32[512]{0:T(512)S(1)}, u32[]{:S(2)}) copy-start(f32[512]{0:T(512)S(1)} %broadcast_multiply_fusion.3) | copy-start | bytes 6148
  286.3 7.8 %collective-permute-start.2 = (bf16[512,2048]{1,0:T(8,128)(2,1)S(1)}, bf16[512,2048]{1,0:T(8,128)(2,1)}, u32[]{:S(2)}, u32[]{:S(2)}) collective-permute-start(bf16[512,2048]{1,0:T(8,128)(2,1)S(1)} %add_convert_fusion.5), channel_id=1, source_target_pairs={{0,1},{1,0},{2,3},{3,2},{4,5},{5,4},{6,7},{7,6},{8,9},{9,8},{10,11... | collective-permute-start | bytes 6291464 | tf_op jit(solution)/shard_map/ppermute | solution.py:31
  294.0 16.9 %copy-start.24 = (bf16[512,2048]{1,0:T(8,128)(2,1)}, bf16[512,2048]{1,0:T(8,128)(2,1)S(1)}, u32[]{:S(2)}) copy-start(bf16[512,2048]{1,0:T(8,128)(2,1)S(1)} %get-tuple-element.166) | copy-start | bytes 6291460
  294.1 16.9 %copy-start.25 = (bf16[512,2048]{1,0:T(8,128)(2,1)}, bf16[512,2048]{1,0:T(8,128)(2,1)S(1)}, u32[]{:S(2)}) copy-start(bf16[512,2048]{1,0:T(8,128)(2,1)S(1)} %get-tuple-element.167) | copy-start | bytes 6291460
  324.8 356.3 %reduce-scatter.3.cloned.1.call-start = ((), (), s32[]{:S(2)}) async-start(), calls=%async_computation.3 | async-start | bytes 9437184 | tf_op jit(solution)/shard_map/reduce_scatter | solution.py:799
  346.1 10.2 %copy-start.39 = (bf16[2048,2048]{1,0:T(8,128)(2,1)S(1)}, bf16[2048,2048]{1,0:T(8,128)(2,1)}, u32[]{:S(2)}) copy-start(bf16[2048,2048]{1,0:T(8,128)(2,1)} %all-gather.2.cloned.1.call-done) | copy-start | bytes 25165828
  346.1 18.0 %slice-start = ((s8[8388608]{0:T(1024)(128)(4,1)}), s8[4194304]{0:T(1024)(128)(4,1)S(1)}, s32[]{:S(2)}) async-start(s8[8388608]{0:T(1024)(128)(4,1)} %bitcast.118), calls=%async_computation.5 | async-start | bytes 8388608
  355.4 8.7 %slice-start.1 = ((s8[8388608]{0:T(1024)(128)(4,1)}), s8[4194304]{0:T(1024)(128)(4,1)S(1)}, s32[]{:S(2)}) async-start(s8[8388608]{0:T(1024)(128)(4,1)} %bitcast.118), calls=%async_computation.6 | async-start | bytes 8388608
  355.4 8.7 %collective-permute-start.4 = (bf16[512,2048]{1,0:T(8,128)(2,1)}, bf16[512,2048]{1,0:T(8,128)(2,1)}, u32[]{:S(2)}, u32[]{:S(2)}) collective-permute-start(bf16[512,2048]{1,0:T(8,128)(2,1)} %convolution_convert_fusion.5), channel_id=1, source_target_pairs={{0,1},{1,0},{2,3},{3,2},{4,5},{5,4},{6,7},{7,6},{8,9},{9,8},{10,11... | collective-permute-start | bytes 6291464 | tf_op jit(solution)/shard_map/ppermute | solution.py:31
  364.1 9.3 %copy-start.45 = (bf16[1024,2048]{1,0:T(8,128)(2,1)S(1)}, bf16[1024,2048]{1,0:T(8,128)(2,1)}, u32[]{:S(2)}) copy-start(bf16[1024,2048]{1,0:T(8,128)(2,1)} %copy-done.44) | copy-start | bytes 12582916
  364.1 22.1 %collective-permute-start.3 = (bf16[512,2048]{1,0:T(8,128)(2,1)}, bf16[512,2048]{1,0:T(8,128)(2,1)}, u32[]{:S(2)}, u32[]{:S(2)}) collective-permute-start(bf16[512,2048]{1,0:T(8,128)(2,1)} %convolution_convert_fusion.6), channel_id=1, source_target_pairs={{0,1},{1,0},{2,3},{3,2},{4,5},{5,4},{6,7},{7,6},{8,9},{9,8},{10,11... | collective-permute-start | bytes 6291464 | tf_op jit(solution)/shard_map/ppermute | solution.py:31
  372.4 48.5 %collective-permute-start.5 = (bf16[512,2048]{1,0:T(8,128)(2,1)}, bf16[512,2048]{1,0:T(8,128)(2,1)}, u32[]{:S(2)}, u32[]{:S(2)}) collective-permute-start(bf16[512,2048]{1,0:T(8,128)(2,1)} %add_convert_fusion.3), channel_id=1, source_target_pairs={{0,2},{1,3},{2,0},{3,1},{4,6},{5,7},{6,4},{7,5},{8,10},{9,11},{10,... | collective-permute-start | bytes 6291464 | tf_op jit(solution)/shard_map/ppermute | solution.py:31
  425.9 5.2 copy-start.8
  425.9 5.9 copy-start.13
  438.2 7.8 %collective-permute-start.6 = (bf16[512,2048]{1,0:T(8,128)(2,1)S(1)}, bf16[512,2048]{1,0:T(8,128)(2,1)}, u32[]{:S(2)}, u32[]{:S(2)}) collective-permute-start(bf16[512,2048]{1,0:T(8,128)(2,1)S(1)} %convert_element_type.194), channel_id=1, source_target_pairs={{0,1},{1,0},{2,3},{3,2},{4,5},{5,4},{6,7},{7,6},{8,9},{9,8},{10,11... | collective-permute-start | bytes 6291464 | tf_op jit(solution)/shard_map/ppermute | solution.py:31
  438.4 5.3 copy-start.18
  438.4 7.6 %copy-start.42 = (bf16[2048,512]{1,0:T(8,128)(2,1)S(1)}, bf16[2048,512]{1,0:T(8,128)(2,1)}, u32[]{:S(2)}) copy-start(bf16[2048,512]{1,0:T(8,128)(2,1)} %get-tuple-element.97) | copy-start | bytes 6291460
  466.9 9.5 %copy-start.14 = (bf16[1024,1536]{1,0:T(8,128)(2,1)}, bf16[1024,1536]{1,0:T(8,128)(2,1)S(1)}, u32[]{:S(2)}) copy-start(bf16[1024,1536]{1,0:T(8,128)(2,1)S(1)} %constant_dynamic-update-slice_fusion) | copy-start | bytes 9437188
  470.9 5.1 copy-start.22
  476.0 22.1 %collective-permute-start.7 = (bf16[512,2048]{1,0:T(8,128)(2,1)}, bf16[512,2048]{1,0:T(8,128)(2,1)}, u32[]{:S(2)}, u32[]{:S(2)}) collective-permute-start(bf16[512,2048]{1,0:T(8,128)(2,1)} %convolution_convert_fusion.4), channel_id=1, source_target_pairs={{0,1},{1,0},{2,3},{3,2},{4,5},{5,4},{6,7},{7,6},{8,9},{9,8},{10,11... | collective-permute-start | bytes 6291464 | tf_op jit(solution)/shard_map/ppermute | solution.py:31
  485.4 12.7 %slice-start.6 = ((s8[6291456]{0:T(1024)(128)(4,1)}), s8[4194304]{0:T(1024)(128)(4,1)S(1)}, s32[]{:S(2)}) async-start(s8[6291456]{0:T(1024)(128)(4,1)} %bitcast.124), calls=%async_computation.11 | async-start | bytes 8388608
  489.2 8.9 %copy-start.23 = (bf16[1024,1536]{1,0:T(8,128)(2,1)S(1)}, bf16[1024,1536]{1,0:T(8,128)(2,1)}, u32[]{:S(2)}) copy-start(bf16[1024,1536]{1,0:T(8,128)(2,1)} %copy-done.22) | copy-start | bytes 9437188
  489.2 8.9 %slice-start.7 = ((s8[6291456]{0:T(1024)(128)(4,1)}), s8[2097152]{0:T(1024)(128)(4,1)S(1)}, s32[]{:S(2)}) async-start(s8[6291456]{0:T(1024)(128)(4,1)} %bitcast.124), calls=%async_computation.12 | async-start | bytes 4194304
  505.2 140.2 %copy-start.9 = (f32[512,2048]{1,0:T(8,128)S(1)}, f32[512,2048]{1,0:T(8,128)}, u32[]{:S(2)}) copy-start(f32[512,2048]{1,0:T(8,128)} %copy-done.7) | copy-start | bytes 12582916
  505.2 140.2 %copy-start.34 = (f32[1,8,256]{2,0,1:T(1,128)S(1)}, f32[1,8,256]{2,0,1:T(1,128)}, u32[]{:S(2)}) copy-start(f32[1,8,256]{2,0,1:T(1,128)} %get-tuple-element.174) | copy-start | bytes 24580
  645.4 4.9 copy-start.11
  645.5 4.9 copy-start.16
  645.5 5.0 copy-start.19
  645.5 4.9 copy-start.29
  645.5 4.9 copy-start.33
  650.4 11.7 %collective-permute-start.8 = (bf16[512,2048]{1,0:T(8,128)(2,1)}, bf16[512,2048]{1,0:T(8,128)(2,1)}, u32[]{:S(2)}, u32[]{:S(2)}) collective-permute-start(bf16[512,2048]{1,0:T(8,128)(2,1)} %add_convert_fusion.1.own_ref), channel_id=1, source_target_pairs={{0,1},{1,0},{2,3},{3,2},{4,5},{5,4},{6,7},{7,6},{8,9},{9,8},{10,11... | collective-permute-start | bytes 6291464 | tf_op jit(solution)/shard_map/ppermute | solution.py:31
  662.1 22.0 %copy-start.37 = (f32[8,128]{1,0:T(8,128)S(1)}, f32[8,128]{1,0:T(8,128)}, u32[]{:S(2)}) copy-start(f32[8,128]{1,0:T(8,128)} %get-tuple-element.109) | copy-start | bytes 12292
  662.1 23.3 %copy-start.4 = (f32[8,128]{1,0:T(8,128)S(1)}, f32[8,128]{1,0:T(8,128)}, u32[]{:S(2)}) copy-start(f32[8,128]{1,0:T(8,128)} %broadcast_in_dim.72.refs_2_.refs_3_.total_ref) | copy-start | bytes 12292
  705.6 10.7 %copy-start.6 = (f32[8,128]{1,0:T(8,128)}, f32[8,128]{1,0:T(8,128)S(1)}, u32[]{:S(2)}) copy-start(f32[8,128]{1,0:T(8,128)S(1)} %get-tuple-element.112.square_ref) | copy-start | bytes 12292
  (18 other events, 42.1 us)
Sparse Core Ops, SparseCore 0:
  195.1 122.5 all-gather.1
  324.9 146.5 reduce-scatter.4
  476.1 204.9 reduce-scatter.2

commit v3 on v2

--- a/solution.py
+++ b/solution.py
@@ -196,194 +196,225 @@
     )(*shards)
 
 
-def reduce_kernel(outer, depth, cuts, count, crossings, *refs):
+def remote_copy(source, target, send_sem, recv_sem, device):
+    return pltpu.make_async_remote_copy(
+        src_ref=source,
+        dst_ref=target,
+        send_sem=send_sem,
+        recv_sem=recv_sem,
+        device_id=device,
+        device_id_type=MESH,
+    )
+
+
+def last_kernel(dp_count, mp_count, depth, pieces, count, tile_rows, *refs):
     refs = list(refs)
 
     def take(number):
         return [refs.pop(0) for _ in range(number)]
 
-    grads, (total_ref,), crossed = take(count), take(1), take(crossings)
-    raws, (square_ref,), taken = take(count), take(1), take(crossings)
-    rest = refs
-    own, got, given, come = [rest[i * count : (i + 1) * count] for i in range(4)]
-    pair_send, pair_recv, turn_send, turn_recv, local, cross_send, cross_recv = rest[4 * count :]
+    grads = take(count)
+    crossed = take(2)
+    x_hbm, back_hbm, resid_hbm, total_ref, gain_ref, shift_ref, norm_ref, bias_ref = take(8)
+    raws = take(count)
+    square_ref, norm_out, bias_out, whole_out, block_out = take(5)
+    bits = dp_count.bit_length() - 1
+    own = take(count)
+    got = [take(count) for _ in range(bits)]
+    parts, taken = take(2), take(2)
+    x_ref, back_ref, resid_ref, block_ref, sums, norm_own, norm_in, bias_in = take(8)
+    half_send, half_recv, local, loading = take(4)
+    cross_send, cross_recv, norm_send, norm_recv, bias_send, bias_recv = take(6)
+    core_send, core_recv, placing = take(3)
+
     me, across = lax.axis_index("dp"), lax.axis_index("mp")
-    out, side = me // 2, me % 2
-    pair = out * 2 + 1 - side
-    other = lax.rem(across + 2, 4)
-
-    def member(steps):
-        return lax.rem(out + steps, outer) * 2 + side
-
+    mine = [me // (1 << bit) % 2 for bit in range(bits)]
+    falling = list(reversed(range(bits)))
+    core = across % 2
+    near = across + 1 - 2 * core
+    other = {"mp": lax.rem(across + 2, 4)}
+    half = x_ref.shape[0]
+
+    def spot(kd, flip):
+        return {"dp": lax.rem(me + kd, dp_count), "mp": near if flip else across}
+
+    hops = [(kd, flip) for kd in range(dp_count) for flip in range(2)][1:]
     barrier = pltpu.get_barrier_semaphore()
-    for peer in [member(r) for r in range(1, outer)] + [pair]:
-        pl.semaphore_signal(barrier, inc=1, device_id={"dp": peer}, device_id_type=MESH)
-    pl.semaphore_signal(barrier, inc=1, device_id={"mp": other}, device_id_type=MESH)
-    pl.semaphore_wait(barrier, outer + 1)
+    for kd, flip in hops:
+        pl.semaphore_signal(barrier, inc=1, device_id=spot(kd, flip), device_id_type=MESH)
+    pl.semaphore_signal(barrier, inc=1, device_id=other, device_id_type=MESH)
+    pl.semaphore_wait(barrier, len(hops) + 1)
 
     crosses = [
-        pltpu.make_async_remote_copy(
-            src_ref=crossed[i],
-            dst_ref=taken[i],
-            send_sem=cross_send.at[i],
-            recv_sem=cross_recv.at[i],
-            device_id={"mp": other},
-            device_id_type=MESH,
+        remote_copy(crossed[i], taken[i], cross_send.at[i], cross_recv.at[i], other)
+        for i in range(2)
+    ]
+    crosses[0].start()
+
+    everything = slice(None)
+
+    def first_index(p, value):
+        return tuple(value if bit == pieces[p][3][0] else everything for bit in falling)
+
+    def index(p, phase, value):
+        order = pieces[p][3]
+        place = []
+        for bit in falling:
+            if bit in order[1:phase]:
+                place.append(mine[bit])
+            elif phase and bit == order[phase]:
+                place.append(value)
+            elif bit != order[0]:
+                place.append(everything)
+        return tuple(place)
+
+    def trade(p, phase):
+        a, start, rows, order = pieces[p]
+        bit, rows = order[phase], (pl.ds(start, rows),)
+        if phase:
+            source = own[a].at[index(p, phase, 1 - mine[bit]) + rows]
+        else:
+            source = grads[a].at[first_index(p, 1 - mine[bit]) + rows]
+        return remote_copy(
+            source,
+            got[phase][a].at[(everything,) * (bits - 1 - phase) + rows],
+            half_send.at[p, phase],
+            half_recv.at[p, phase],
+            {"dp": me + (1 - 2 * mine[bit]) * (1 << bit)},
         )
-        for i in range(crossings)
+
+    def load(p):
+        a, start, rows, order = pieces[p]
+        rows = (pl.ds(start, rows),)
+        return pltpu.make_async_copy(
+            grads[a].at[first_index(p, mine[order[0]]) + rows],
+            own[a].at[(everything,) * (bits - 1) + rows],
+            local.at[p],
+        )
+
+    lead, skew = 6, 2
+    for p in range(min(lead, len(pieces))):
+        trade(p, 0).start()
+    for p in range(len(pieces)):
+        load(p).start()
+    later = [
+        pltpu.make_async_copy(source, target, loading.at[i])
+        for i, (source, target) in enumerate(
+            [
+                (crossed[0], parts[0]),
+                (crossed[1], parts[1]),
+                (x_hbm, x_ref),
+                (back_hbm, back_ref),
+                (resid_hbm, resid_ref),
+            ]
+        )
     ]
-    for cross in crosses:
-        cross.start()
-    loads = [
-        pltpu.make_async_copy(grads[a].at[pl.ds(0, outer * depth)], own[a], local.at[a])
-        for a in range(count)
+    for copy in later:
+        copy.start()
+    norm_own[...] = norm_ref[...]
+    bias_in[me] = bias_ref[...]
+    bias_copies = [
+        remote_copy(bias_ref, bias_in.at[me], bias_send.at[kd], bias_recv.at[kd], spot(kd, 0))
+        for kd in range(1, dp_count)
     ]
-    for load in loads:
-        load.start()
-
-    pieces = []
-    for a in range(count):
-        rows = depth // cuts[a]
-        pieces += [(a, i * rows, rows) for i in range(cuts[a])]
-    order = list(range(1, outer)) + [0]
-
-    def to_pair(p, a, start, rows, r):
-        return pltpu.make_async_remote_copy(
-            src_ref=grads[a].at[pl.ds((outer + r) * depth + start, rows)],
-            dst_ref=got[a].at[pl.ds(r * depth + start, rows)],
-            send_sem=pair_send.at[p, r],
-            recv_sem=pair_recv.at[p, r],
-            device_id={"dp": pair},
-            device_id_type=MESH,
+    for copy in bias_copies:
+        copy.start()
+    total = total_ref[0:1, 0:1]
+    squares = []
+
+    def finish(p, phase):
+        a, start, rows, order = pieces[p]
+        rows = (pl.ds(start, rows),)
+        if phase == 0:
+            load(p).wait()
+        trade(p, phase).wait_recv()
+        if phase == 0 and p + lead < len(pieces):
+            trade(p + lead, 0).start()
+        kept = index(p, phase, mine[order[phase]]) + rows
+        both = own[a][kept].astype(F32)
+        both = both + got[phase][a][(everything,) * (bits - 1 - phase) + rows].astype(F32)
+        if phase < bits - 1:
+            own[a][kept] = both.astype(BF16)
+            trade(p, phase + 1).start()
+        else:
+            raw = both / total
+            raws[a][rows] = raw
+            squares.append(jnp.sum(raw * raw, keepdims=True))
+
+    waves = len(pieces) + skew * (bits - 1)
+
+    def advance(first, last):
+        for wave in range(first, last):
+            for phase in range(bits):
+                if 0 <= wave - skew * phase < len(pieces):
+                    finish(wave - skew * phase, phase)
+
+    middle, later_on = 2 * waves // 5, 4 * waves // 5
+    advance(0, middle)
+
+    for copy in later:
+        copy.wait()
+    crosses[0].wait_recv()
+    crosses[1].start()
+    sums[...] = jnp.zeros_like(sums)
+    gain = gain_ref[0:1]
+
+    @pl.loop(0, half // tile_rows)
+    def _(i):
+        where = pl.ds(pl.multiple_of(i * tile_rows, tile_rows), tile_rows)
+        hat, inverse = norm_stats(x_ref[where].astype(F32))
+        back = parts[0][where].astype(F32) + taken[0][where].astype(F32)
+        product = back * hat
+        sums[0] += jnp.sum(product.reshape(tile_rows // 8, 8, -1), axis=0)
+        sums[1] += jnp.sum(back.reshape(tile_rows // 8, 8, -1), axis=0)
+        back_ref[where] = back_ref[where] + norm_back(back, hat, inverse, gain)
+
+    whole_place = pl.ds(pl.multiple_of(core * half, half), half)
+    whole_copy = remote_copy(
+        back_ref, whole_out.at[whole_place], core_send.at[0], core_recv.at[0], spot(0, 1)
+    )
+    whole_copy.start()
+    whole_local = pltpu.make_async_copy(back_ref, whole_out.at[whole_place], placing.at[0])
+    whole_local.start()
+    for k in range(2):
+        row = jnp.sum(sums[k], axis=0, keepdims=True)
+        for d in range(dp_count):
+            norm_own[d, k : k + 1] = row[:, d * depth : (d + 1) * depth]
+    norm_copies = [
+        remote_copy(
+            norm_own.at[lax.rem(me + kd, dp_count)],
+            norm_in.at[me * 2 + core],
+            norm_send.at[kd, flip],
+            norm_recv.at[kd, flip],
+            spot(kd, flip),
         )
-
-    def to_member(p, a, start, rows, r):
-        return pltpu.make_async_remote_copy(
-            src_ref=given[a].at[pl.ds(r * depth + start, rows)],
-            dst_ref=come[a].at[pl.ds(r * depth + start, rows)],
-            send_sem=turn_send.at[p, r],
-            recv_sem=turn_recv.at[p, r],
-            device_id={"dp": member(outer - r)},
-            device_id_type=MESH,
-        )
-
-    for p, piece in enumerate(pieces):
-        for r in order:
-            to_pair(p, *piece, r).start()
-    for load in loads:
-        load.wait()
-    for p, (a, start, rows) in enumerate(pieces):
-        for r in order:
-            where = pl.ds(r * depth + start, rows)
-            to_pair(p, a, start, rows, r).wait_recv()
-            part = own[a][where].astype(F32) + got[a][where].astype(F32)
-            if r:
-                given[a][where] = part.astype(BF16)
-                to_member(p, a, start, rows, r).start()
-            else:
-                raws[a][pl.ds(start, rows)] = part
-    total = total_ref[0:1, 0:1]
-    square = jnp.zeros((1, 1), F32)
-    for p, (a, start, rows) in enumerate(pieces):
-        part = raws[a][pl.ds(start, rows)]
-        for r in range(1, outer):
-            to_member(p, a, start, rows, r).wait_recv()
-            part = part + come[a][pl.ds(r * depth + start, rows)].astype(F32)
-        part = part / total
-        raws[a][pl.ds(start, rows)] = part
-        square = square + jnp.sum(part * part, keepdims=True)
-    square_ref[...] = jnp.broadcast_to(square, square_ref.shape)
-    for p, piece in enumerate(pieces):
-        for r in order:
-            to_pair(p, *piece, r).wait_send()
-            if r:
-                to_member(p, *piece, r).wait_send()
-    for cross in crosses:
-        cross.wait()
-
-
-def reduce_rows(grads, total, crossed, cuts, collective_id):
-    size = lax.axis_size("dp")
-    outer = size // 2
-    count, depth, number = len(grads), grads[0].shape[0] // size, sum(cuts)
-    anywhere = pl.BlockSpec(memory_space=pl.ANY)
-    inside = pl.BlockSpec(memory_space=pltpu.VMEM)
-    buffers = [pltpu.VMEM((outer * depth, grad.shape[1]), BF16) for grad in grads]
-    ways = pltpu.SemaphoreType.DMA((number, outer))
-    crossings = len(crossed)
-    results = pl.pallas_call(
-        functools.partial(reduce_kernel, outer, depth, cuts, count, crossings),
-        out_shape=[jax.ShapeDtypeStruct((depth, grad.shape[1]), F32) for grad in grads]
-        + [jax.ShapeDtypeStruct((8, 128), F32)]
-        + [jax.ShapeDtypeStruct(part.shape, part.dtype) for part in crossed],
-        in_specs=[anywhere] * count + [inside] + [anywhere] * crossings,
-        out_specs=[inside] * (count + 1) + [anywhere] * crossings,
-        scratch_shapes=buffers * 4
-        + [ways] * 4
-        + [pltpu.SemaphoreType.DMA((count,))]
-        + [pltpu.SemaphoreType.DMA((crossings,))] * 2,
-        compiler_params=pltpu.CompilerParams(
-            collective_id=collective_id, has_side_effects=True, vmem_limit_bytes=56 << 20
-        ),
-    )(*grads, total, *crossed)
-    return results[:count], results[count], results[count + 1 :]
-
-
-def finish_kernel(dp_count, mp_count, *refs):
-    norm_ref, bias_ref, square_ref, total_ref, whole_ref = refs[:5]
-    norm_out, bias_out, square_out, whole_out = refs[5:9]
-    norm_in, bias_in, square_in, square_own = refs[9:13]
-    norm_send, norm_recv, bias_send, bias_recv, square_send, square_recv = refs[13:19]
-    whole_send, whole_recv = refs[19:21]
-    me, across = lax.axis_index("dp"), lax.axis_index("mp")
-    side = across % 2
-    near = across + 1 - 2 * side
-
-    def spot(kd, km):
-        return {"dp": lax.rem(me + kd, dp_count), "mp": lax.rem(across + km, mp_count)}
-
-    hops = [(kd, km) for kd in range(dp_count) for km in range(mp_count)][1:]
-    barrier = pltpu.get_barrier_semaphore()
-    for kd, km in hops:
-        pl.semaphore_signal(barrier, inc=1, device_id=spot(kd, km), device_id_type=MESH)
-    pl.semaphore_wait(barrier, len(hops))
-
-    def send(source, target, send_sem, recv_sem, device):
-        return pltpu.make_async_remote_copy(
-            src_ref=source,
-            dst_ref=target,
-            send_sem=send_sem,
-            recv_sem=recv_sem,
-            device_id=device,
-            device_id_type=MESH,
-        )
-
-    whole = send(whole_ref, whole_out, whole_send, whole_recv, {"mp": near})
-    sent = []
-    for kd in range(dp_count):
-        owner = lax.rem(me + kd, dp_count)
-        for flip in range(2):
-            if kd or flip:
-                column = near if flip else across
-                copy = send(
-                    norm_ref.at[owner],
-                    norm_in.at[me * 2 + side],
-                    norm_send.at[kd, flip],
-                    norm_recv.at[kd, flip],
-                    {"dp": owner, "mp": column},
-                )
-                copy.start()
-                sent.append(copy)
-    for kd in range(1, dp_count):
-        copy = send(bias_ref, bias_in.at[me], bias_send.at[kd], bias_recv.at[kd], spot(kd, 0))
+        for kd, flip in hops
+    ]
+    for copy in norm_copies:
         copy.start()
-        sent.append(copy)
-    whole.start()
-    norm_in[me * 2 + side] = norm_ref[me]
-    bias_in[me] = bias_ref[...]
-    for copy in sent:
+    norm_in[me * 2 + core] = norm_own[me]
+
+    advance(middle, later_on)
+
+    crosses[1].wait_recv()
+    shift = shift_ref[0:1]
+
+    @pl.loop(0, half // tile_rows)
+    def _(i):
+        where = pl.ds(pl.multiple_of(i * tile_rows, tile_rows), tile_rows)
+        mlp = parts[1][where].astype(F32) + taken[1][where].astype(F32)
+        block_ref[where] = (resid_ref[where] + mlp + shift).astype(BF16)
+
+    block_copy = remote_copy(
+        block_ref, block_out.at[whole_place], core_send.at[1], core_recv.at[1], spot(0, 1)
+    )
+    block_copy.start()
+    block_local = pltpu.make_async_copy(block_ref, block_out.at[whole_place], placing.at[1])
+    block_local.start()
+    advance(later_on, waves)
+
+    for copy in norm_copies + bias_copies:
         copy.wait_recv()
-    total = total_ref[0:1, 0:1]
     norm = norm_in[0]
     for i in range(1, 2 * dp_count):
         norm = norm + norm_in[i]
@@ -396,68 +427,162 @@
     bias_out[...] = bias
     square = jnp.sum(norm * norm, keepdims=True) / float(mp_count)
     square = square + jnp.sum(bias * bias, keepdims=True) / float(dp_count)
-    square_own[...] = square_ref[...] + square
-    slot = me * mp_count + across
-    square_in[slot] = square_own[...]
-    last = []
-    for i, (kd, km) in enumerate(hops):
-        copy = send(
-            square_own, square_in.at[slot], square_send.at[i], square_recv.at[i], spot(kd, km)
-        )
-        copy.start()
-        last.append(copy)
-    for copy in last:
-        copy.wait_recv()
-    square = square_in[0]
-    for i in range(1, dp_count * mp_count):
-        square = square + square_in[i]
-    square_out[...] = square
-    for copy in sent + last:
+
+    for part in squares:
+        square = square + part
+    square_ref[...] = jnp.broadcast_to(square, square_ref.shape)
+    for p in range(len(pieces)):
+        for phase in range(bits):
+            trade(p, phase).wait_send()
+    for copy in crosses + norm_copies + bias_copies:
         copy.wait_send()
-    whole.wait()
-
-
-def finish_sums(norm_part, bias_part, square, total, whole, collective_id):
+    whole_copy.wait()
+    whole_local.wait()
+    block_copy.wait()
+    block_local.wait()
+
+
+def last_sums(grads, crossed, x_own, back, residual, total, gain, shift, norm_part, bias_part):
     dp_count, mp_count = lax.axis_size("dp"), lax.axis_size("mp")
+    bits = dp_count.bit_length() - 1
+    count, depth = len(grads), grads[0].shape[0] // dp_count
+    half, width = x_own.shape
+    straight = list(range(bits))
+    turned = [1, 0] + straight[2:]
+    pieces = []
+    for a, grad in enumerate(grads):
+        rows = max(16, depth * 256 // grad.shape[1] // 4)
+        rows = min(rows // 16 * 16, depth)
+        number = depth // rows
+        for i in range(number):
+            order = turned if a == 0 and i % 2 == 0 else straight
+            pieces.append(((2 * i + 1) / number, (a, i * rows, rows, order)))
+    pieces = [piece for _, piece in sorted(pieces, key=lambda piece: piece[0])]
     anywhere = pl.BlockSpec(memory_space=pl.ANY)
     inside = pl.BlockSpec(memory_space=pltpu.VMEM)
-    tile = jax.ShapeDtypeStruct((8, 128), F32)
-    hops = dp_count * mp_count - 1
-    return pl.pallas_call(
-        functools.partial(finish_kernel, dp_count, mp_count),
-        out_shape=[
+
+    def blocks(number):
+        return [pltpu.VMEM((2,) * number + (depth, grad.shape[1]), BF16) for grad in grads]
+
+    slim, wide = pltpu.VMEM((half, width), BF16), pltpu.VMEM((half, width), F32)
+    dma = pltpu.SemaphoreType.DMA
+    results = pl.pallas_call(
+        functools.partial(last_kernel, dp_count, mp_count, depth, pieces, count, min(64, half)),
+        out_shape=[jax.ShapeDtypeStruct((depth, grad.shape[1]), F32) for grad in grads]
+        + [
+            jax.ShapeDtypeStruct((8, 128), F32),
             jax.ShapeDtypeStruct(norm_part.shape[1:], F32),
             jax.ShapeDtypeStruct(bias_part.shape, F32),
-            tile,
-            jax.ShapeDtypeStruct(whole.shape, whole.dtype),
+            jax.ShapeDtypeStruct((2 * half, width), F32),
+            jax.ShapeDtypeStruct((2 * half, width), BF16),
         ],
-        in_specs=[inside] * 4 + [anywhere],
-        out_specs=[inside] * 3 + [anywhere],
-        scratch_shapes=[
+        in_specs=[anywhere] * (count + 5) + [inside] * 5,
+        out_specs=[inside] * (count + 3) + [anywhere] * 2,
+        scratch_shapes=blocks(bits - 1)
+        + sum([blocks(bits - 1 - phase) for phase in range(bits)], [])
+        + [slim] * 4
+        + [slim, wide, wide, slim]
+        + [
+            pltpu.VMEM((2, 8, width), F32),
+            pltpu.VMEM(norm_part.shape, F32),
             pltpu.VMEM((2 * dp_count, *norm_part.shape[1:]), F32),
             pltpu.VMEM((dp_count, *bias_part.shape), F32),
-            pltpu.VMEM((dp_count * mp_count, 8, 128), F32),
-            pltpu.VMEM((8, 128), F32),
         ]
-        + [pltpu.SemaphoreType.DMA((dp_count, 2))] * 2
-        + [pltpu.SemaphoreType.DMA((dp_count,))] * 2
-        + [pltpu.SemaphoreType.DMA((hops,))] * 2
-        + [pltpu.SemaphoreType.DMA] * 2,
+        + [dma((len(pieces), bits))] * 2
+        + [dma((len(pieces),)), dma((5,))]
+        + [dma((2,))] * 2
+        + [dma((dp_count, 2))] * 2
+        + [dma((dp_count,))] * 2
+        + [dma((2,))] * 3,
         compiler_params=pltpu.CompilerParams(
-            collective_id=collective_id, has_side_effects=True, vmem_limit_bytes=32 << 20
+            collective_id=1, has_side_effects=True, vmem_limit_bytes=58 << 20
         ),
-    )(norm_part, bias_part, square, total, whole)
-
-
-def step_kernel(count, whole_count, square_ref, total_ref, *refs):
-    raws, masters, moments, averages = [refs[i * count : (i + 1) * count] for i in range(4)]
-    outs = [refs[(4 + i) * count : (5 + i) * count] for i in range(5)]
+    )(
+        *[grad.reshape((2,) * bits + (depth, -1)) for grad in grads],
+        *crossed,
+        x_own,
+        back,
+        residual,
+        total,
+        gain,
+        shift,
+        norm_part,
+        bias_part,
+    )
+    return results[:count], *results[count:]
+
+
+def everyone(dp_count, mp_count):
+    return [(kd, km) for kd in range(dp_count) for km in range(mp_count)][1:]
+
+
+def square_kernel(dp_count, mp_count, count, tile_ref, total_ref, *refs):
+    summed, (out_ref, tiles, own_ref, send, recv) = refs[:count], refs[count:]
+    me, across = lax.axis_index("dp"), lax.axis_index("mp")
+    hops = everyone(dp_count, mp_count)
+
+    def spot(kd, km):
+        return {"dp": lax.rem(me + kd, dp_count), "mp": lax.rem(across + km, mp_count)}
+
+    barrier = pltpu.get_barrier_semaphore()
+    for kd, km in hops:
+        pl.semaphore_signal(barrier, inc=1, device_id=spot(kd, km), device_id_type=MESH)
+    total = total_ref[0:1, 0:1]
+    square = tile_ref[...]
+    for ref in summed:
+        raw = ref[...].astype(F32) / total
+        square = square + jnp.sum(raw * raw)
+    own_ref[...] = square
+    pl.semaphore_wait(barrier, len(hops))
+    slot = me * mp_count + across
+    copies = [
+        remote_copy(own_ref, tiles.at[slot], send.at[i], recv.at[i], spot(kd, km))
+        for i, (kd, km) in enumerate(hops)
+    ]
+    for copy in copies:
+        copy.start()
+    tiles[slot] = own_ref[...]
+    for copy in copies:
+        copy.wait_recv()
+    square = tiles[0]
+    for i in range(1, dp_count * mp_count):
+        square = square + tiles[i]
+    out_ref[...] = square
+    for copy in copies:
+        copy.wait_send()
+
+
+def sum_everywhere(tile, total, summed, collective_id):
+    dp_count, mp_count = lax.axis_size("dp"), lax.axis_size("mp")
+    inside = pl.BlockSpec(memory_space=pltpu.VMEM)
+    hops = pltpu.SemaphoreType.DMA((dp_count * mp_count - 1,))
+    return pl.pallas_call(
+        functools.partial(square_kernel, dp_count, mp_count, len(summed)),
+        out_shape=jax.ShapeDtypeStruct(tile.shape, F32),
+        in_specs=[inside] * (2 + len(summed)),
+        out_specs=inside,
+        scratch_shapes=[
+            pltpu.VMEM((dp_count * mp_count, *tile.shape), F32),
+            pltpu.VMEM(tile.shape, F32),
+            hops,
+            hops,
+        ],
+        compiler_params=pltpu.CompilerParams(
+            collective_id=collective_id, has_side_effects=True, vmem_limit_bytes=16 << 20
+        ),
+    )(tile, total, *summed)
+
+
+def step_kernel(splits, divided, whole_count, square_ref, total_ref, *refs):
+    count = len(splits)
+    refs = list(refs)
+    raws = [[refs.pop(0) for _ in range(number)] for number in splits]
+    masters, moments, averages = [refs[i * count : (i + 1) * count] for i in range(3)]
+    outs = [refs[(3 + i) * count : (4 + i) * count] for i in range(5)]
     clip = jnp.minimum(1.0, 1.0 / (jnp.sqrt(square_ref[0:1, 0:1]) + 1e-06))
     total = total_ref[0:1, 0:1]
 
     def update(raw, master, moment, average):
-        if raw.dtype == BF16:
-            raw = raw.astype(F32) / total
         clipped = raw * clip
         momentum = MOMENTUM * moment + clipped
         updated = master - RATE * (clipped + MOMENTUM * momentum)
@@ -466,14 +591,18 @@
 
     def apply(a):
         if len(masters[a].shape) == 2:
-            results = update(raws[a][...], masters[a][...], moments[a][...], averages[a][...])
+            raw = [part[...].astype(F32) for part in raws[a]]
+            raw = raw[0] if len(raw) == 1 else jnp.concatenate(raw, axis=1)
+            if a >= divided:
+                raw = raw / total
+            results = update(raw, masters[a][...], moments[a][...], averages[a][...])
             for out, result in zip(outs, results):
                 out[a][...] = result
         else:
             width = masters[a].shape[2]
             for c in range(masters[a].shape[0]):
                 results = update(
-                    raws[a][:, c * width : (c + 1) * width],
+                    raws[a][0][:, c * width : (c + 1) * width],
                     masters[a][c],
                     moments[a][c],
                     averages[a][c],
@@ -490,8 +619,9 @@
             apply(a)
 
 
-def step_all(square, total, raws, masters, moments, averages, whole_count):
-    depth = raws[-1].shape[0]
+def step_all(square, total, raws, masters, moments, averages, whole_count, divided):
+    raws = [raw if isinstance(raw, tuple) else (raw,) for raw in raws]
+    depth = raws[-1][0].shape[0]
     rows = min(32, depth)
 
     def spec(value, a):
@@ -509,47 +639,17 @@
     wide = [jax.ShapeDtypeStruct(master.shape, F32) for master in masters]
     slim = [jax.ShapeDtypeStruct(master.shape, BF16) for master in masters]
     results = pl.pallas_call(
-        functools.partial(step_kernel, len(masters), whole_count),
+        functools.partial(step_kernel, [len(raw) for raw in raws], divided, whole_count),
         grid=(depth // rows,),
         out_shape=wide * 4 + slim,
-        in_specs=[tile, tile] + specs(raws) + specs(masters) * 3,
+        in_specs=[tile, tile]
+        + [spec(part, a) for a, raw in enumerate(raws) for part in raw]
+        + specs(masters) * 3,
         out_specs=specs(masters) * 5,
         compiler_params=pltpu.CompilerParams(vmem_limit_bytes=56 << 20),
-    )(square, total, *raws, *masters, *moments, *averages)
+    )(square, total, *sum(raws, ()), *masters, *moments, *averages)
     count = len(masters)
     return [results[i * count : (i + 1) * count] for i in range(5)]
-
-
-def merge_kernel(side_ref, own_ref, other_ref, out_ref):
-    @pl.when(pl.program_id(0) == 0)
-    def _():
-        out_ref[...] = own_ref[...]
-
-    @pl.when(pl.program_id(0) == 1)
-    def _():
-        out_ref[...] = other_ref[...]
-
-
-def merge_halves(side, own, other):
-    half, width = own.shape
-    rows = min(128, half)
-    steps = half // rows
-    return pl.pallas_call(
-        merge_kernel,
-        out_shape=jax.ShapeDtypeStruct((2 * half, width), own.dtype),
-        grid_spec=pltpu.PrefetchScalarGridSpec(
-            num_scalar_prefetch=1,
-            grid=(2, steps),
-            in_specs=[
-                pl.BlockSpec((rows, width), lambda h, i, side: (jnp.where(h == 0, i, steps - 1), 0)),
-                pl.BlockSpec((rows, width), lambda h, i, side: (jnp.where(h == 0, 0, i), 0)),
-            ],
-            out_specs=pl.BlockSpec(
-                (rows, width),
-                lambda h, i, side: (jnp.where(h == 0, side[0], 1 - side[0]) * steps + i, 0),
-            ),
-        ),
-    )(jnp.reshape(side, (1,)).astype(jnp.int32), own, other)
 
 
 def score_block(query_ref, key_ref, first, rows, scale):
@@ -642,6 +742,13 @@
     spread = jnp.mean(centred * centred, axis=-1, keepdims=True)
     inverse = lax.rsqrt(spread + EPS)
     return centred * inverse, inverse
+
+
+def norm_back(back, hat, inverse, gain):
+    scaled = back * gain
+    mean = jnp.mean(scaled, axis=-1, keepdims=True)
+    slope = jnp.mean(scaled * hat, axis=-1, keepdims=True)
+    return inverse * (scaled - mean - hat * slope)
 
 
 def gelu_parts(value):
@@ -701,17 +808,6 @@
     side = lax.axis_index("mp") % 2
     half = row_count // 2
 
-    def block_at(s, r):
-        return ((place_out + (outer - r)) % outer) * 2 + (place_in + s) % 2
-
-    def to_local(value):
-        parts = [
-            lax.dynamic_slice_in_dim(value, block_at(s, r) * depth, depth, 1)
-            for s in range(2)
-            for r in range(outer)
-        ]
-        return jnp.concatenate(parts, axis=1)
-
     def own_rows(value):
         return lax.dynamic_slice_in_dim(value, side * half, half, 0)
 
@@ -772,7 +868,9 @@
         return (product(left[:half]) + other.astype(F32)).astype(BF16)
 
     def sum_over_mp(product, left):
-        part = sum_over_cores(product, left)
+        return sum_across(sum_over_cores(product, left))
+
+    def sum_across(part):
         flip = 2
         while flip < mp_count:
             part = part.astype(F32) + swap(part, "mp", flip).astype(F32)
@@ -781,24 +879,25 @@
                 part = part.astype(BF16)
         return part.astype(F32)
 
-    x_own = own_rows(x_low).astype(F32)
+    x_own = own_rows(x_low)
     attn_out = sum_over_mp(lambda rows: dot_f32("te,de->td", rows, w_proj), mixed_low)
-    residual = x_own + attn_out + bias_p
+    weight_own, weight_other = own_rows(token_weight), other_rows(token_weight)
+    upstream = weight_own[:, None] * own_rows(cot_low).astype(F32)
+    upstream_other = weight_other[:, None] * other_rows(cot_low).astype(F32)
+    upstream_low = jnp.concatenate([upstream, upstream_other], axis=0).astype(BF16)
+    attn_out, upstream, upstream_low = lax.optimization_barrier((attn_out, upstream, upstream_low))
+    residual = x_own.astype(F32) + attn_out + bias_p
     hat2, inverse2 = norm_stats(residual)
     ln2_own = (hat2 * gain2 + shift2).astype(BF16)
     ln2_low = jnp.concatenate([ln2_own, swap(ln2_own, "mp", 1)], axis=0)
     pre_act = dot_f32("td,df->tf", ln2_low, w_fc) + fc_bias_master[None]
     hidden_low = gelu_tanh(pre_act).astype(BF16)
 
-    weight_own, weight_other = own_rows(token_weight), other_rows(token_weight)
-    upstream = weight_own[:, None] * own_rows(cot_low).astype(F32)
-    upstream_other = weight_other[:, None] * other_rows(cot_low).astype(F32)
-    upstream_low = jnp.concatenate([upstream, upstream_other], axis=0).astype(BF16)
-
     def scatter_product(product):
         return lax.psum_scatter(product, "dp", scatter_dimension=0, tiled=True)
 
     down_product = dot_f32("td,tf->df", upstream_low, hidden_low).astype(BF16)
+    down_product, w_down = lax.optimization_barrier((down_product, w_down))
     down_reduced = scatter_product(down_product)
 
     back_act = dot_f32("td,df->tf", upstream_low, w_down)
@@ -806,16 +905,10 @@
     fc_bias_sum = jnp.sum(back_pre, axis=0, dtype=F32)
     fc_product = dot_f32("td,tf->df", ln2_low, back_pre).astype(BF16)
 
-    def norm_back(back, hat, inverse, gain):
-        scaled = back * gain
-        mean = jnp.mean(scaled, axis=-1, keepdims=True)
-        slope = jnp.mean(scaled * hat, axis=-1, keepdims=True)
-        return inverse * (scaled - mean - hat * slope)
-
-    back_ln2 = sum_over_mp(lambda rows: dot_f32("tf,df->td", rows, w_fc), back_pre)
+    back_ln2 = sum_over_cores(lambda rows: dot_f32("tf,df->td", rows, w_fc), back_pre)
+    back_ln2 = sum_across(back_ln2)
     mlp_part = sum_over_cores(lambda rows: dot_f32("tf,df->td", rows, w_down), hidden_low)
     fc_product, mlp_part, back_ln2 = lax.optimization_barrier((fc_product, mlp_part, back_ln2))
-    fc_reduced = scatter_product(fc_product)
     gain2_sum = jnp.sum(back_ln2 * hat2, axis=0)
     shift2_sum = jnp.sum(back_ln2, axis=0)
     back_resid = upstream + norm_back(back_ln2, hat2, inverse2, gain2)
@@ -827,43 +920,38 @@
     attn_bias_sum = jnp.sum(back_qkv, axis=0, dtype=F32).reshape(3, head_width)[0::2]
     back_qkv_local = halves_swapped(back_qkv[:half], back_qkv[half:])
     back_part = sum_over_cores(lambda rows: dot_f32("te,de->td", rows, w_qkv), back_qkv_local)
-    qkv_part = dot_f32("td,te->de", to_local(ln1_low), back_qkv).astype(BF16)
-    proj_part = dot_f32("td,te->de", to_local(ga_low), mixed_low).astype(BF16)
+    qkv_part = dot_f32("td,te->de", ln1_low, back_qkv).astype(BF16)
+    proj_part = dot_f32("td,te->de", ga_low, mixed_low).astype(BF16)
     total_tile = jnp.broadcast_to(valid_total, (8, 128))
-    (qkv_raw, proj_raw), square, (back_taken, mlp_taken) = reduce_rows(
-        [qkv_part, proj_part], total_tile, [back_part, mlp_part], (4, 1), 1
-    )
-    back_ln1 = back_part.astype(F32) + back_taken.astype(F32)
-    mlp_out = mlp_part.astype(F32) + mlp_taken.astype(F32)
-    block_own = (residual + mlp_out + bias_d).astype(BF16)
-    hat1, inverse1 = norm_stats(x_own)
-    gain1_sum = jnp.sum(back_ln1 * hat1, axis=0)
-    shift1_sum = jnp.sum(back_ln1, axis=0)
-    whole_own = back_resid + norm_back(back_ln1, hat1, inverse1, gain1)
-
+    open_row = jnp.zeros_like(gain2_sum)
     norm_part = jnp.stack(
         [
-            gain1_sum,
-            shift1_sum,
+            open_row,
+            open_row,
             gain2_sum,
             shift2_sum,
             jnp.sum(back_resid, axis=0),
             jnp.sum(upstream, axis=0),
-            jnp.zeros_like(gain1_sum),
-            jnp.zeros_like(gain1_sum),
+            open_row,
+            open_row,
         ],
         axis=0,
     )
     norm_part = jnp.moveaxis(norm_part.reshape(8, dp_count, depth), 1, 0)
     bias_part = jnp.concatenate([attn_bias_sum.reshape(-1), fc_bias_sum]).reshape(-1, 128)
-    for reduced in (fc_reduced, down_reduced):
-        raw = reduced.astype(F32) / valid_total
-        square = square + jnp.sum(raw * raw)
-    norm_raw, bias_raw, square, whole_other = finish_sums(
-        norm_part, bias_part, square, total_tile, whole_own, 2
-    )
-    whole = merge_halves(side, whole_own, whole_other)
-    block_part = merge_halves(side, block_own, swap(block_own, "mp", 1))
+    (fc_raw, qkv_raw, proj_raw), square, norm_raw, bias_raw, whole, block_part = last_sums(
+        [fc_product, qkv_part, proj_part],
+        [back_part, mlp_part],
+        x_own,
+        back_resid,
+        residual,
+        total_tile,
+        gain1,
+        bias_d,
+        norm_part,
+        bias_part,
+    )
+    square = sum_everywhere(square, total_tile, [down_reduced], 3)
     grad_norm = jnp.sqrt(square[0, 0])
     bias_raw = bias_raw.reshape(-1)
     raw_grads = [
@@ -872,7 +960,7 @@
         bias_raw[2 * head_width :].reshape(1, -1),
         qkv_raw,
         proj_raw,
-        fc_reduced,
+        fc_raw,
         down_reduced,
     ]
     masters = (
@@ -918,12 +1006,17 @@
         values[3] = jnp.moveaxis(values[3], 0, 1)
         return [values[order.index(i)] for i in range(7)]
 
-    grads_out, momenta_out, averaged_out, updated_out, copies_out = [
-        returned(values)
-        for values in step_all(
-            square, total_tile, raw_grads, arranged(masters), arranged(moments), arranged(averages), 3
-        )
-    ]
+    steps = step_all(
+        square,
+        total_tile,
+        raw_grads,
+        arranged(masters),
+        arranged(moments),
+        arranged(averages),
+        3,
+        6,
+    )
+    grads_out, momenta_out, averaged_out, updated_out, copies_out = map(returned, steps)
     return (
         block_part,
         whole,

time: 756 us -> 728 us (0.963)
  other arithmetic: 76.8 us -> 35.6 us
  Pallas kernels: 396 us -> 429 us
  waiting for transfers between devices: 84.5 us -> 72 us
    pallas_call x5 -> x3, Pallas kernels: 192 us -> 226 us  [the longest x1 198 us: last_sums(): pl.pallas_call(functools.partial(last_kernel, dp_count, mp_count, depth,...]
    reduce_scatter x2 -> x1, waiting for transfers between devices: 11.8 us -> 0.01 us  [scatter_product(): return lax.psum_scatter(product, 'dp', scatter_dimension=0, tiled=True)]
    add x3 -> x2, other arithmetic: 12.1 us -> 3.3 us  [sum_across(): part = part.astype(F32) + swap(part, 'mp', flip).astype(F32)]
    reduce_sum x3 -> x0, other arithmetic: 8.76 us -> none  [the longest x2 6.04 us: local(): square = square + jnp.sum(raw * raw)]
    convert_element_type x3 -> x0, other arithmetic: 7.76 us -> none  [the longest x1 4.88 us: local(): block_own = (residual + mlp_out + bias_d).astype(BF16)]
    unnamed x118 -> x105, local copies, waits for them, and re-layouts: 25 us -> 20 us
    ppermute x9 -> x8, waiting for transfers between devices: 72.6 us -> 71.7 us  [swap(): return lax.ppermute(value, axis, [(i, i ^ flip) for i in range(size)])]
  transfers between devices with their start and end apart: 12 -> 10, of which waited for: 4 -> 6; matrix products, arithmetic and copies ran while one was open for 28% -> 20% of each run, Pallas kernels for 23% -> 31%
where the time goes in v3:
time: 728 us; the launch traced here: 723 us
  Pallas kernels  429 us (59%)
  matrix products  135 us (19%)
  waiting for transfers between devices  72 us (10%)
  other arithmetic  35.6 us (5%)
  local copies, waits for them, and re-layouts  27.7 us (4%)
  between operations  19.1 us (3%)
    pallas_call x1, Pallas kernels, last_sums(): pl.pallas_call(functools.partial(last_kernel, dp_count, mp_count, depth,...  198 us
    pallas_call x1, Pallas kernels, gather_rows(): pl.pallas_call(functools.partial(gather_kernel, outer, pieces, count), ou...  178 us
    dot_general x16, matrix products, dot_f32(): return jnp.einsum(eq, left, right, preferred_element_type=F32)  135 us
    ppermute x8, waiting for transfers between devices, swap(): return lax.ppermute(value, axis, [(i, i ^ flip) for i in range(size)])  71.7 us
    unnamed x105, local copies, waits for them, and re-layouts  20 us
    pallas_call x1, Pallas kernels, step_all(): pl.pallas_call(functools.partial(step_kernel, [len(raw) for raw in raws],...  19.9 us
    pallas_call x1, Pallas kernels, attend_back(): pl.pallas_call(functools.partial(attend_back_kernel, rows, 1.0 / math.sqr...  16.3 us
  transfers between devices with their start and end apart: 10, of which 6 were waited for; matrix products, arithmetic and copies ran while one was open for 20% of the time, Pallas kernels for 31%

profile of v3, /device:TPU:0, one launch (start us, length us, event | category | flops | bytes accessed | tf_op | source)
XLA Modules:
  0.0 723.3 jit_solution(14796149825089521750)
XLA Ops:
  8.7 2.7 convert_element_type.144.refs_4_
  11.5 2.4 bitcast_convert_fusion.refs_2_
  14.6 1.1 convert_element_type.160
  16.9 177.5 %shard_map.545 = (bf16[128,256]{1,0:T(8,128)(2,1)}, f32[64,128]{1,0:T(8,128)}, bf16[2048,1536]{1,0:T(8,128)(2,1)}, bf16[2048,512]{1,0:T(8,128)(2,1)}, bf16[2048,2048]{1,0:T(8,128)(2,1)}) custom-call(bf16[16,256]{1,0:T(8,128)(2,1)} %pad.8.refs_0_, f32[8,128]{1,0:T(8,128)} %broadcast_in_dim.63.refs_1_, bf16[3,256,512]{2,1,0:T(8,128)(2,1)} %bitcast_convert_fusion.refs_2_, ...), custom_call_target="tpu_custom_call" | custom-call | tf_op jit(solution)/shard_map/pallas_call | solution.py:189
  196.2 2.8 convert_reduce_fusion
  199.1 1.2 fusion.2
  200.4 10.8 %add_convert_fusion.query_ref.key_ref.value_ref = bf16[1024,1536]{1,0:T(8,128)(2,1)S(1)} fusion(bf16[2048,1536]{1,0:T(8,128)(2,1)} %get-tuple-element.100, f32[1536]{0:T(1024)S(1)} %pad_maximum_fusion.9, bf16[1024,2048]{1,0:T(8,128)(2,1)S(1)} %copy-done.8, f32[2048]{0:T(1024)S(1)} %bitcast.130, f32[2048]{0:T(1024)S(1)} %bitcast.128, ...), kind=kOutput, calls=%fused_computation.24 | convolution fusion | flops 6458179584 | bytes 13662208 | tf_op jit(solution)/shard_map/td,de->te/dot_general | solution.py:26
  211.2 9.7 %shard_map.546 = bf16[1024,512]{1,0:T(8,128)(2,1)S(1)} custom-call(bf16[1024,1536]{1,0:T(8,128)(2,1)S(1)} %add_convert_fusion.query_ref.key_ref.value_ref, bf16[1024,1536]{1,0:T(8,128)(2,1)S(1)} %add_convert_fusion.query_ref.key_ref.value_ref, bf16[1024,1536]{1,0:T(8,128)(2,1)S(1)} %add_convert_fusion.query_ref.key_ref.value_ref), custom_call_target="tpu_custom_call" | custom-call | tf_op jit(solution)/shard_map/pallas_call | solution.py:710
  221.3 1.6 copy-done.35
  222.9 1.3 convolution_convert_fusion.7
  224.3 4.1 collective-permute-done
  228.4 1.3 add_convert_fusion.5
  229.7 1.5 collective-permute-start.1
  233.9 1.3 fusion.38
  235.8 5.0 fusion.43
  241.3 36.2 %collective-permute-done.1 = bf16[512,2048]{1,0:T(8,128)(2,1)} collective-permute-done((bf16[512,2048]{1,0:T(8,128)(2,1)S(1)}, bf16[512,2048]{1,0:T(8,128)(2,1)}, u32[]{:S(2)}, u32[]{:S(2)}) %collective-permute-start.1) | collective-permute-done | bytes 2097184 | tf_op jit(solution)/shard_map/ppermute | solution.py:31
  277.5 2.5 convert_add_fusion.1
  280.1 2.1 fusion.47
  284.2 4.2 collective-permute-done.2
  288.3 15.1 %multiply_convert_fusion = (bf16[1024,2048]{1,0:T(8,128)(2,1)}, f32[1024,2048]{1,0:T(8,128)}) fusion(f32[2048]{0:T(1024)S(1)} %copy-done.26, bf16[2048,2048]{1,0:T(8,128)(2,1)S(1)} %bitcast.138, bf16[512,2048]{1,0:T(8,128)(2,1)S(1)} %collective-permute-done.2, bf16[512,2048]{1,0:T(8,128)(2,1)S(1)} %add_convert_fusion.4), kind=kOutput, calls=%fused_computation.19 | convolution fusion | flops 8619294720 | bytes 25174016 | tf_op jit(solution)/shard_map/td,df->tf/dot_general | solution.py:26
  303.4 13.5 %convolution_convert_fusion.2 = bf16[2048,2048]{1,0:T(8,128)(2,1)} fusion(bf16[1024,2048]{1,0:T(8,128)(2,1)S(1)} %pad_maximum_fusion, bf16[1024,2048]{1,0:T(8,128)(2,1)} %get-tuple-element.190), kind=kOutput, calls=%fused_computation.22 | convolution fusion | flops 8594128896 | bytes 16777216 | tf_op jit(solution)/shard_map/td,tf->df/dot_general | solution.py:26
  317.2 18.2 %convert_reduce_fusion.1 = (f32[2048]{0:T(1024)S(1)}, bf16[1024,2048]{1,0:T(8,128)(2,1)S(1)}) fusion(f32[1024,2048]{1,0:T(8,128)} %get-tuple-element.191, f32[2048]{0:T(1024)S(1)} %copy-done.26, bf16[1024,2048]{1,0:T(8,128)(2,1)} %copy-done.14, bf16[2048,2048]{1,0:T(8,128)(2,1)} %all-gather.2.cloned.1.call-done), kind=kOutput, calls=%fused_computation.18 | convolution fusion | flops 8636069888 | bytes 25182208 | tf_op jit(solution)/shard_map/td,df->tf/dot_general | solution.py:26
  335.5 10.6 %convolution_convert_fusion.5 = bf16[512,2048]{1,0:T(8,128)(2,1)} fusion(bf16[2048,2048]{1,0:T(8,128)(2,1)} %get-tuple-element.106, bf16[1024,2048]{1,0:T(8,128)(2,1)S(1)} %get-tuple-element.193), kind=kOutput, calls=%fused_computation.47 | convolution fusion | flops 4296015872 | bytes 12582912 | tf_op jit(solution)/shard_map/tf,df->td/dot_general | solution.py:26
  346.1 6.1 convolution_convert_fusion.6
  352.9 9.3 %add_convert_fusion.2 = bf16[512,2048]{1,0:T(8,128)(2,1)S(1)} fusion(bf16[512,2048]{1,0:T(8,128)(2,1)} %collective-permute-done.4, bf16[2048,2048]{1,0:T(8,128)(2,1)} %get-tuple-element.106, bf16[1024,2048]{1,0:T(8,128)(2,1)} %copy-done.39), kind=kOutput, calls=%fused_computation.33 | convolution fusion | flops 4298113024 | bytes 14680064 | tf_op jit(solution)/shard_map/tf,df->td/dot_general | solution.py:26
  362.2 1.5 collective-permute-start.5
  363.7 13.4 %convolution_convert_fusion.1 = bf16[2048,2048]{1,0:T(8,128)(2,1)} fusion(bf16[1024,2048]{1,0:T(8,128)(2,1)} %copy-done.39, bf16[512,2048]{1,0:T(8,128)(2,1)S(1)} %copy-done.37, bf16[512,2048]{1,0:T(8,128)(2,1)S(1)} %add_convert_fusion.4), kind=kOutput, calls=%fused_computation.21 | convolution fusion | flops 8602517504 | bytes 16777216 | tf_op jit(solution)/shard_map/td,tf->df/dot_general | solution.py:26
  377.1 7.7 %add_convert_fusion.3.refs_4_ = bf16[512,2048]{1,0:T(8,128)(2,1)} fusion(bf16[512,2048]{1,0:T(8,128)(2,1)} %collective-permute-done.3, bf16[2048,2048]{1,0:T(8,128)(2,1)S(1)} %bitcast.136, bf16[1024,2048]{1,0:T(8,128)(2,1)} %get-tuple-element.190), kind=kOutput, calls=%fused_computation.34 | convolution fusion | flops 4298113024 | bytes 14680064 | tf_op jit(solution)/shard_map/tf,df->td/dot_general | solution.py:26
  384.8 25.0 %collective-permute-done.5 = bf16[512,2048]{1,0:T(8,128)(2,1)S(1)} collective-permute-done((bf16[512,2048]{1,0:T(8,128)(2,1)S(1)}, bf16[512,2048]{1,0:T(8,128)(2,1)S(1)}, u32[]{:S(2)}, u32[]{:S(2)}) %collective-permute-start.5) | collective-permute-done | bytes 2097184 | tf_op jit(solution)/shard_map/ppermute | solution.py:31
  410.6 1.9 multiply_reduce_fusion
  412.8 2.3 fusion.46
  415.2 2.0 copy-done.7
  419.6 2.2 collective-permute-done.6
  421.8 4.6 fusion.31
  426.9 16.3 %shard_map.547 = (bf16[1024,512]{1,0:T(8,128)(2,1)S(1)}, bf16[1024,512]{1,0:T(8,128)(2,1)S(1)}, bf16[1024,512]{1,0:T(8,128)(2,1)S(1)}) custom-call(bf16[1024,1536]{1,0:T(8,128)(2,1)} %copy-done, bf16[1024,1536]{1,0:T(8,128)(2,1)} %copy-done, bf16[1024,1536]{1,0:T(8,128)(2,1)} %copy-done, bf16[1024,512]{1,0:T(8,128)(2,1)S(1)} %maximum_select_fusion.2.back_ref), custom_call_target="tpu_custom_call" | custom-call | tf_op jit(solution)/shard_map/pallas_call | solution.py:728
  446.9 3.9 convolution_convert_fusion.4
  451.6 5.5 convolution_convert_fusion.3
  457.1 9.5 %convolution_convert_fusion = bf16[2048,1536]{1,0:T(8,128)(2,1)} fusion(bf16[1024,1536]{1,0:T(8,128)(2,1)S(1)} %constant_dynamic-update-slice_fusion, bf16[1024,2048]{1,0:T(8,128)(2,1)S(1)} %copy-done.10, f32[2048]{0:T(1024)S(1)} %bitcast.131, f32[2048]{0:T(1024)S(1)} %bitcast.129, f32[1024]{0:T(1024)S(1)} %copy-done.32, f32[1024]{0:T(1024)S(1)} %copy-done.25), kind=kOutput, calls=%fused_computation.20 | convolution fusion | flops 6458179584 | bytes 13656064 | tf_op jit(solution)/shard_map/td,te->de/dot_general | solution.py:26
  466.7 4.6 add_convert_fusion.1.refs_3_
  471.3 1.2 broadcast_in_dim.68.refs_8_.total_ref
  472.5 197.8 %shard_map.548 = (f32[256,2048]{1,0:T(8,128)}, f32[256,1536]{1,0:T(8,128)}, f32[256,512]{1,0:T(8,128)}, f32[8,128]{1,0:T(8,128)}, f32[8,256]{1,0:T(8,128)}, /*in...) custom-call(bf16[2,2,2,256,2048]{4,3,2,1,0:T(8,128)(2,1)} %bitcast.96, ...), custom_call_target="tpu_custom_call" | custom-call | tf_op jit(solution)/shard_map/pallas_call | solution.py:469
  670.3 1.3 slice.131
  672.9 1.2 copy-done.1
  674.8 8.2 %shard_map.549.square_ref = f32[8,128]{1,0:T(8,128)S(1)} custom-call(f32[8,128]{1,0:T(8,128)S(1)} %copy-done.4, f32[8,128]{1,0:T(8,128)S(1)} %copy-done.2, bf16[256,2048]{1,0:T(8,128)(2,1)S(1)} %copy-done.1), custom_call_target="tpu_custom_call" | custom-call | tf_op jit(solution)/shard_map/pallas_call | solution.py:559
  684.3 19.9 %shard_map.550 = (f32[6,256]{1,0:T(8,128)}, f32[2,512]{1,0:T(2,128)}, f32[1,2048]{1,0:T(1,128)}, f32[3,256,512]{2,1,0:T(8,128)}, f32[256,512]{1,0:T(8,128)}, /*i...) custom-call(f32[8,128]{1,0:T(8,128)} %copy-done.3, ...), custom_call_target="tpu_custom_call" | custom-call | tf_op jit(solution)/shard_map/pallas_call | solution.py:641
  704.2 1.3 reduce.3
  705.5 5.1 copy.81
  711.6 3.4 copy.82
  (159 shorter events, 22.1 us)
Async XLA Ops:
  7.2 6.6 copy-start.17
  7.2 7.4 %copy-start.20 = (f32[256,6]{0,1:T(8,128)S(1)}, f32[256,6]{0,1:T(8,128)}, u32[]{:S(2)}) copy-start(f32[256,6]{0,1:T(8,128)} %param.31) | copy-start | bytes 18436
  7.2 7.3 %copy-start.12 = (f32[256,2048]{1,0:T(8,128)S(1)}, f32[256,2048]{1,0:T(8,128)}, u32[]{:S(2)}) copy-start(f32[256,2048]{1,0:T(8,128)} %refs_13_.1) | copy-start | bytes 6291460
  7.3 309.9 %all-gather.2.cloned.1.call-start = ((), (), s32[]{:S(2)}) async-start(), calls=%async_computation.1 | async-start | bytes 9437184 | tf_op jit(solution)/shard_map/all_gather | solution.py:841
  194.5 478.4 %reduce-scatter.2.cloned.1.call-start = ((), (), s32[]{:S(2)}) async-start(), calls=%async_computation.2 | async-start | bytes 9437184 | tf_op jit(solution)/shard_map/reduce_scatter | solution.py:897
  194.5 4.5 copy-start.8
  196.2 4.2 copy-start.27
  196.2 4.2 copy-start.29
  196.2 4.1 copy-start.23
  199.0 12.1 %copy-start.24 = (f32[1024]{0:T(1024)}, f32[1024]{0:T(1024)S(1)}, u32[]{:S(2)}) copy-start(f32[1024]{0:T(1024)S(1)} %broadcast_multiply_fusion) | copy-start | bytes 12292
  200.3 10.9 %copy-start.31 = (f32[1024]{0:T(1024)}, f32[1024]{0:T(1024)S(1)}, u32[]{:S(2)}) copy-start(f32[1024]{0:T(1024)S(1)} %add_rsqrt_fusion) | copy-start | bytes 12292
  211.2 9.7 %copy-start = (bf16[1024,1536]{1,0:T(8,128)(2,1)}, bf16[1024,1536]{1,0:T(8,128)(2,1)S(1)}, u32[]{:S(2)}) copy-start(bf16[1024,1536]{1,0:T(8,128)(2,1)S(1)} %add_convert_fusion.query_ref.key_ref.value_ref) | copy-start | bytes 9437188
  221.3 7.1 copy-start.18
  224.2 7.0 copy-start.33
  224.2 4.2 collective-permute-start
  229.7 47.8 %collective-permute-start.1 = (bf16[512,2048]{1,0:T(8,128)(2,1)S(1)}, bf16[512,2048]{1,0:T(8,128)(2,1)}, u32[]{:S(2)}, u32[]{:S(2)}) collective-permute-start(bf16[512,2048]{1,0:T(8,128)(2,1)S(1)} %add_convert_fusion.5), channel_id=1, source_target_pairs={{0,2},{1,3},{2,0},{3,1},{4,6},{5,7},{6,4},{7,5},{8,10},{9,11},{10,... | collective-permute-start | bytes 6291464 | tf_op jit(solution)/shard_map/ppermute | solution.py:31
  241.3 62.1 %copy-start.14 = (bf16[1024,2048]{1,0:T(8,128)(2,1)}, bf16[1024,2048]{1,0:T(8,128)(2,1)S(1)}, u32[]{:S(2)}) copy-start(bf16[1024,2048]{1,0:T(8,128)(2,1)S(1)} %pad_maximum_fusion) | copy-start | bytes 12582916
  241.3 38.7 %copy-start.9 = (bf16[1024,2048]{1,0:T(8,128)(2,1)S(1)}, bf16[1024,2048]{1,0:T(8,128)(2,1)}, u32[]{:S(2)}) copy-start(bf16[1024,2048]{1,0:T(8,128)(2,1)} %param.26) | copy-start | bytes 12582916
  277.5 10.8 %slice-start.2 = ((s8[8388608]{0:T(1024)(128)(4,1)}), s8[4194304]{0:T(1024)(128)(4,1)S(1)}, s32[]{:S(2)}) async-start(s8[8388608]{0:T(1024)(128)(4,1)} %bitcast.137), calls=%async_computation.5 | async-start | bytes 8388608
  280.1 8.3 %slice-start.3 = ((s8[8388608]{0:T(1024)(128)(4,1)}), s8[4194304]{0:T(1024)(128)(4,1)S(1)}, s32[]{:S(2)}) async-start(s8[8388608]{0:T(1024)(128)(4,1)} %bitcast.137), calls=%async_computation.6 | async-start | bytes 8388608
  282.8 5.5 copy-start.26
  284.2 4.2 collective-permute-start.2
  288.3 15.1 %copy-start.36 = (bf16[512,2048]{1,0:T(8,128)(2,1)}, bf16[512,2048]{1,0:T(8,128)(2,1)S(1)}, u32[]{:S(2)}) copy-start(bf16[512,2048]{1,0:T(8,128)(2,1)S(1)} %collective-permute-done.2) | copy-start | bytes 6291460
  335.4 10.7 %copy-start.39 = (bf16[1024,2048]{1,0:T(8,128)(2,1)}, bf16[1024,2048]{1,0:T(8,128)(2,1)S(1)}, u32[]{:S(2)}) copy-start(bf16[1024,2048]{1,0:T(8,128)(2,1)S(1)} %get-tuple-element.193) | copy-start | bytes 12582916
  335.4 10.7 %copy-start.34 = (bf16[2048,2048]{1,0:T(8,128)(2,1)S(1)}, bf16[2048,2048]{1,0:T(8,128)(2,1)}, u32[]{:S(2)}) copy-start(bf16[2048,2048]{1,0:T(8,128)(2,1)} %all-gather.2.cloned.1.call-done) | copy-start | bytes 25165828
  335.5 10.7 %copy-start.38 = (bf16[1024,2048]{1,0:T(8,128)(2,1)S(1)}, bf16[1024,2048]{1,0:T(8,128)(2,1)}, u32[]{:S(2)}) copy-start(bf16[1024,2048]{1,0:T(8,128)(2,1)} %get-tuple-element.190) | copy-start | bytes 12582916
  346.1 6.8 collective-permute-start.4
  352.3 24.8 %collective-permute-start.3 = (bf16[512,2048]{1,0:T(8,128)(2,1)}, bf16[512,2048]{1,0:T(8,128)(2,1)}, u32[]{:S(2)}, u32[]{:S(2)}) collective-permute-start(bf16[512,2048]{1,0:T(8,128)(2,1)} %convolution_convert_fusion.6), channel_id=1, source_target_pairs={{0,1},{1,0},{2,3},{3,2},{4,5},{5,4},{6,7},{7,6},{8,9},{9,8},{10,11... | collective-permute-start | bytes 6291464 | tf_op jit(solution)/shard_map/ppermute | solution.py:31
  352.9 10.8 %copy-start.37 = (bf16[512,2048]{1,0:T(8,128)(2,1)S(1)}, bf16[512,2048]{1,0:T(8,128)(2,1)}, u32[]{:S(2)}) copy-start(bf16[512,2048]{1,0:T(8,128)(2,1)} %copy-done.36) | copy-start | bytes 6291460
  352.9 24.2 %slice-start = ((s8[8388608]{0:T(1024)(128)(4,1)}), s8[4194304]{0:T(1024)(128)(4,1)S(1)}, s32[]{:S(2)}) async-start(s8[8388608]{0:T(1024)(128)(4,1)} %bitcast.135), calls=%async_computation.3 | async-start | bytes 8388608
  362.2 15.0 %slice-start.1 = ((s8[8388608]{0:T(1024)(128)(4,1)}), s8[4194304]{0:T(1024)(128)(4,1)S(1)}, s32[]{:S(2)}) async-start(s8[8388608]{0:T(1024)(128)(4,1)} %bitcast.135), calls=%async_computation.4 | async-start | bytes 8388608
  362.2 47.6 %collective-permute-start.5 = (bf16[512,2048]{1,0:T(8,128)(2,1)S(1)}, bf16[512,2048]{1,0:T(8,128)(2,1)S(1)}, u32[]{:S(2)}, u32[]{:S(2)}) collective-permute-start(bf16[512,2048]{1,0:T(8,128)(2,1)S(1)} %add_convert_fusion.2), channel_id=1, source_target_pairs={{0,2},{1,3},{2,0},{3,1},{4,6},{5,7},{6,4},{7,5},{8,10},{9,11},{10,... | collective-permute-start | bytes 6291464 | tf_op jit(solution)/shard_map/ppermute | solution.py:31
  384.8 25.8 %copy-start.6 = (f32[512,2048]{1,0:T(8,128)S(1)}, f32[512,2048]{1,0:T(8,128)}, u32[]{:S(2)}) copy-start(f32[512,2048]{1,0:T(8,128)} %copy-done.5) | copy-start | bytes 12582916
  415.1 2.4 copy-start.22
  415.1 3.1 copy-start.21
  417.5 9.0 %copy-start.15 = (bf16[512,2048]{1,0:T(8,128)(2,1)}, bf16[512,2048]{1,0:T(8,128)(2,1)S(1)}, u32[]{:S(2)}) copy-start(bf16[512,2048]{1,0:T(8,128)(2,1)S(1)} %convert_element_type.173) | copy-start | bytes 6291460
  417.5 4.4 collective-permute-start.6
  444.2 2.7 slice-start.5
  446.9 4.7 copy-start.16
  446.9 4.7 copy-start.19
  450.8 15.9 %collective-permute-start.7 = (bf16[512,2048]{1,0:T(8,128)(2,1)S(1)}, bf16[512,2048]{1,0:T(8,128)(2,1)S(1)}, u32[]{:S(2)}, u32[]{:S(2)}) collective-permute-start(bf16[512,2048]{1,0:T(8,128)(2,1)S(1)} %convolution_convert_fusion.4), channel_id=1, source_target_pairs={{0,1},{1,0},{2,3},{3,2},{4,5},{5,4},{6,7},{7,6},{8,9},{9,8},{10,11... | collective-permute-start | bytes 6291464 | tf_op jit(solution)/shard_map/ppermute | solution.py:31
  451.6 5.6 copy-start.10
  451.6 5.6 copy-start.25
  451.6 5.6 copy-start.28
  451.6 5.5 copy-start.30
  451.6 5.5 copy-start.32
  472.5 200.4 %copy-start.2 = (f32[8,128]{1,0:T(8,128)S(1)}, f32[8,128]{1,0:T(8,128)}, u32[]{:S(2)}) copy-start(f32[8,128]{1,0:T(8,128)} %broadcast_in_dim.68.refs_8_.total_ref) | copy-start | bytes 12292
  705.5 6.2 copy-start.13
  (8 other events, 13.5 us)
Sparse Core Ops, SparseCore 0:
  194.6 122.5 all-gather.1
  353.0 163.5 reduce-scatter.1

commit v4 on v3

--- a/solution.py
+++ b/solution.py
@@ -292,7 +292,7 @@
             local.at[p],
         )
 
-    lead, skew = 6, 2
+    lead, skew = 12, 4
     for p in range(min(lead, len(pieces))):
         trade(p, 0).start()
     for p in range(len(pieces)):

time: 728 us -> 726 us (level)
  no operation moved by 1% of the time
where the time goes in v4:
time: 726 us; the launch traced here: 721 us
  Pallas kernels  427 us (59%)
  matrix products  135 us (19%)
  waiting for transfers between devices  72 us (10%)
  other arithmetic  35.6 us (5%)
  local copies, waits for them, and re-layouts  27.7 us (4%)
  between operations  19.1 us (3%)
    pallas_call x1, Pallas kernels, last_sums(): pl.pallas_call(functools.partial(last_kernel, dp_count, mp_count, depth,...  194 us
    pallas_call x1, Pallas kernels, gather_rows(): pl.pallas_call(functools.partial(gather_kernel, outer, pieces, count), ou...  178 us
    dot_general x16, matrix products, dot_f32(): return jnp.einsum(eq, left, right, preferred_element_type=F32)  135 us
    ppermute x8, waiting for transfers between devices, swap(): return lax.ppermute(value, axis, [(i, i ^ flip) for i in range(size)])  71.7 us
    unnamed x105, local copies, waits for them, and re-layouts  20 us
    pallas_call x1, Pallas kernels, step_all(): pl.pallas_call(functools.partial(step_kernel, [len(raw) for raw in raws],...  19.9 us
    pallas_call x1, Pallas kernels, attend_back(): pl.pallas_call(functools.partial(attend_back_kernel, rows, 1.0 / math.sqr...  16.3 us
  transfers between devices with their start and end apart: 10, of which 6 were waited for; matrix products, arithmetic and copies ran while one was open for 20% of the time, Pallas kernels for 31%

profile of v4, /device:TPU:0, one launch (start us, length us, event | category | flops | bytes accessed | tf_op | source)
XLA Modules:
  0.0 720.9 jit_solution(16528766046347490426)
XLA Ops:
  8.7 2.7 convert_element_type.144.refs_4_
  11.5 2.4 bitcast_convert_fusion.refs_2_
  14.6 1.1 convert_element_type.160
  16.9 177.5 %shard_map.545 = (bf16[128,256]{1,0:T(8,128)(2,1)}, f32[64,128]{1,0:T(8,128)}, bf16[2048,1536]{1,0:T(8,128)(2,1)}, bf16[2048,512]{1,0:T(8,128)(2,1)}, bf16[2048,2048]{1,0:T(8,128)(2,1)}) custom-call(bf16[16,256]{1,0:T(8,128)(2,1)} %pad.8.refs_0_, f32[8,128]{1,0:T(8,128)} %broadcast_in_dim.63.refs_1_, bf16[3,256,512]{2,1,0:T(8,128)(2,1)} %bitcast_convert_fusion.refs_2_, ...), custom_call_target="tpu_custom_call" | custom-call | tf_op jit(solution)/shard_map/pallas_call | solution.py:189
  196.2 2.8 convert_reduce_fusion
  199.1 1.2 fusion.2
  200.4 10.8 %add_convert_fusion.query_ref.key_ref.value_ref = bf16[1024,1536]{1,0:T(8,128)(2,1)S(1)} fusion(bf16[2048,1536]{1,0:T(8,128)(2,1)} %get-tuple-element.100, f32[1536]{0:T(1024)S(1)} %pad_maximum_fusion.9, bf16[1024,2048]{1,0:T(8,128)(2,1)S(1)} %copy-done.8, f32[2048]{0:T(1024)S(1)} %bitcast.130, f32[2048]{0:T(1024)S(1)} %bitcast.128, ...), kind=kOutput, calls=%fused_computation.24 | convolution fusion | flops 6458179584 | bytes 13662208 | tf_op jit(solution)/shard_map/td,de->te/dot_general | solution.py:26
  211.2 9.7 %shard_map.546 = bf16[1024,512]{1,0:T(8,128)(2,1)S(1)} custom-call(bf16[1024,1536]{1,0:T(8,128)(2,1)S(1)} %add_convert_fusion.query_ref.key_ref.value_ref, bf16[1024,1536]{1,0:T(8,128)(2,1)S(1)} %add_convert_fusion.query_ref.key_ref.value_ref, bf16[1024,1536]{1,0:T(8,128)(2,1)S(1)} %add_convert_fusion.query_ref.key_ref.value_ref), custom_call_target="tpu_custom_call" | custom-call | tf_op jit(solution)/shard_map/pallas_call | solution.py:710
  221.3 1.6 copy-done.35
  222.9 1.3 convolution_convert_fusion.7
  224.3 4.1 collective-permute-done
  228.4 1.3 add_convert_fusion.5
  229.7 1.5 collective-permute-start.1
  233.9 1.3 fusion.38
  235.8 5.0 fusion.43
  241.3 36.2 %collective-permute-done.1 = bf16[512,2048]{1,0:T(8,128)(2,1)} collective-permute-done((bf16[512,2048]{1,0:T(8,128)(2,1)S(1)}, bf16[512,2048]{1,0:T(8,128)(2,1)}, u32[]{:S(2)}, u32[]{:S(2)}) %collective-permute-start.1) | collective-permute-done | bytes 2097184 | tf_op jit(solution)/shard_map/ppermute | solution.py:31
  277.5 2.5 convert_add_fusion.1
  280.1 2.1 fusion.47
  284.2 4.2 collective-permute-done.2
  288.3 15.1 %multiply_convert_fusion = (bf16[1024,2048]{1,0:T(8,128)(2,1)}, f32[1024,2048]{1,0:T(8,128)}) fusion(f32[2048]{0:T(1024)S(1)} %copy-done.26, bf16[2048,2048]{1,0:T(8,128)(2,1)S(1)} %bitcast.138, bf16[512,2048]{1,0:T(8,128)(2,1)S(1)} %collective-permute-done.2, bf16[512,2048]{1,0:T(8,128)(2,1)S(1)} %add_convert_fusion.4), kind=kOutput, calls=%fused_computation.19 | convolution fusion | flops 8619294720 | bytes 25174016 | tf_op jit(solution)/shard_map/td,df->tf/dot_general | solution.py:26
  303.4 13.5 %convolution_convert_fusion.2 = bf16[2048,2048]{1,0:T(8,128)(2,1)} fusion(bf16[1024,2048]{1,0:T(8,128)(2,1)S(1)} %pad_maximum_fusion, bf16[1024,2048]{1,0:T(8,128)(2,1)} %get-tuple-element.190), kind=kOutput, calls=%fused_computation.22 | convolution fusion | flops 8594128896 | bytes 16777216 | tf_op jit(solution)/shard_map/td,tf->df/dot_general | solution.py:26
  317.2 18.2 %convert_reduce_fusion.1 = (f32[2048]{0:T(1024)S(1)}, bf16[1024,2048]{1,0:T(8,128)(2,1)S(1)}) fusion(f32[1024,2048]{1,0:T(8,128)} %get-tuple-element.191, f32[2048]{0:T(1024)S(1)} %copy-done.26, bf16[1024,2048]{1,0:T(8,128)(2,1)} %copy-done.14, bf16[2048,2048]{1,0:T(8,128)(2,1)} %all-gather.2.cloned.1.call-done), kind=kOutput, calls=%fused_computation.18 | convolution fusion | flops 8636069888 | bytes 25182208 | tf_op jit(solution)/shard_map/td,df->tf/dot_general | solution.py:26
  335.5 10.6 %convolution_convert_fusion.5 = bf16[512,2048]{1,0:T(8,128)(2,1)} fusion(bf16[2048,2048]{1,0:T(8,128)(2,1)} %get-tuple-element.106, bf16[1024,2048]{1,0:T(8,128)(2,1)S(1)} %get-tuple-element.193), kind=kOutput, calls=%fused_computation.47 | convolution fusion | flops 4296015872 | bytes 12582912 | tf_op jit(solution)/shard_map/tf,df->td/dot_general | solution.py:26
  346.1 6.1 convolution_convert_fusion.6
  352.9 9.3 %add_convert_fusion.2 = bf16[512,2048]{1,0:T(8,128)(2,1)S(1)} fusion(bf16[512,2048]{1,0:T(8,128)(2,1)} %collective-permute-done.4, bf16[2048,2048]{1,0:T(8,128)(2,1)} %get-tuple-element.106, bf16[1024,2048]{1,0:T(8,128)(2,1)} %copy-done.39), kind=kOutput, calls=%fused_computation.33 | convolution fusion | flops 4298113024 | bytes 14680064 | tf_op jit(solution)/shard_map/tf,df->td/dot_general | solution.py:26
  362.2 1.5 collective-permute-start.5
  363.7 13.4 %convolution_convert_fusion.1 = bf16[2048,2048]{1,0:T(8,128)(2,1)} fusion(bf16[1024,2048]{1,0:T(8,128)(2,1)} %copy-done.39, bf16[512,2048]{1,0:T(8,128)(2,1)S(1)} %copy-done.37, bf16[512,2048]{1,0:T(8,128)(2,1)S(1)} %add_convert_fusion.4), kind=kOutput, calls=%fused_computation.21 | convolution fusion | flops 8602517504 | bytes 16777216 | tf_op jit(solution)/shard_map/td,tf->df/dot_general | solution.py:26
  377.1 7.7 %add_convert_fusion.3.refs_4_ = bf16[512,2048]{1,0:T(8,128)(2,1)} fusion(bf16[512,2048]{1,0:T(8,128)(2,1)} %collective-permute-done.3, bf16[2048,2048]{1,0:T(8,128)(2,1)S(1)} %bitcast.136, bf16[1024,2048]{1,0:T(8,128)(2,1)} %get-tuple-element.190), kind=kOutput, calls=%fused_computation.34 | convolution fusion | flops 4298113024 | bytes 14680064 | tf_op jit(solution)/shard_map/tf,df->td/dot_general | solution.py:26
  384.8 25.0 %collective-permute-done.5 = bf16[512,2048]{1,0:T(8,128)(2,1)S(1)} collective-permute-done((bf16[512,2048]{1,0:T(8,128)(2,1)S(1)}, bf16[512,2048]{1,0:T(8,128)(2,1)S(1)}, u32[]{:S(2)}, u32[]{:S(2)}) %collective-permute-start.5) | collective-permute-done | bytes 2097184 | tf_op jit(solution)/shard_map/ppermute | solution.py:31
  410.6 1.9 multiply_reduce_fusion
  412.8 2.3 fusion.46
  415.2 2.0 copy-done.7
  419.6 2.2 collective-permute-done.6
  421.8 4.6 fusion.31
  426.9 16.3 %shard_map.547 = (bf16[1024,512]{1,0:T(8,128)(2,1)S(1)}, bf16[1024,512]{1,0:T(8,128)(2,1)S(1)}, bf16[1024,512]{1,0:T(8,128)(2,1)S(1)}) custom-call(bf16[1024,1536]{1,0:T(8,128)(2,1)} %copy-done, bf16[1024,1536]{1,0:T(8,128)(2,1)} %copy-done, bf16[1024,1536]{1,0:T(8,128)(2,1)} %copy-done, bf16[1024,512]{1,0:T(8,128)(2,1)S(1)} %maximum_select_fusion.2.back_ref), custom_call_target="tpu_custom_call" | custom-call | tf_op jit(solution)/shard_map/pallas_call | solution.py:728
  446.9 3.9 convolution_convert_fusion.4
  451.6 5.5 convolution_convert_fusion.3
  457.1 9.5 %convolution_convert_fusion = bf16[2048,1536]{1,0:T(8,128)(2,1)} fusion(bf16[1024,1536]{1,0:T(8,128)(2,1)S(1)} %constant_dynamic-update-slice_fusion, bf16[1024,2048]{1,0:T(8,128)(2,1)S(1)} %copy-done.10, f32[2048]{0:T(1024)S(1)} %bitcast.131, f32[2048]{0:T(1024)S(1)} %bitcast.129, f32[1024]{0:T(1024)S(1)} %copy-done.32, f32[1024]{0:T(1024)S(1)} %copy-done.25), kind=kOutput, calls=%fused_computation.20 | convolution fusion | flops 6458179584 | bytes 13656064 | tf_op jit(solution)/shard_map/td,te->de/dot_general | solution.py:26
  466.7 4.6 add_convert_fusion.1.refs_3_
  471.3 1.2 broadcast_in_dim.68.refs_8_.total_ref
  472.5 194.0 %shard_map.548 = (f32[256,2048]{1,0:T(8,128)}, f32[256,1536]{1,0:T(8,128)}, f32[256,512]{1,0:T(8,128)}, f32[8,128]{1,0:T(8,128)}, f32[8,256]{1,0:T(8,128)}, /*in...) custom-call(bf16[2,2,2,256,2048]{4,3,2,1,0:T(8,128)(2,1)} %bitcast.96, ...), custom_call_target="tpu_custom_call" | custom-call | tf_op jit(solution)/shard_map/pallas_call | solution.py:469
  666.5 1.3 slice.131
  669.1 1.2 copy-done.1
  671.0 9.6 %shard_map.549.square_ref = f32[8,128]{1,0:T(8,128)S(1)} custom-call(f32[8,128]{1,0:T(8,128)S(1)} %copy-done.4, f32[8,128]{1,0:T(8,128)S(1)} %copy-done.2, bf16[256,2048]{1,0:T(8,128)(2,1)S(1)} %copy-done.1), custom_call_target="tpu_custom_call" | custom-call | tf_op jit(solution)/shard_map/pallas_call | solution.py:559
  681.9 19.9 %shard_map.550 = (f32[6,256]{1,0:T(8,128)}, f32[2,512]{1,0:T(2,128)}, f32[1,2048]{1,0:T(1,128)}, f32[3,256,512]{2,1,0:T(8,128)}, f32[256,512]{1,0:T(8,128)}, /*i...) custom-call(f32[8,128]{1,0:T(8,128)} %copy-done.3, ...), custom_call_target="tpu_custom_call" | custom-call | tf_op jit(solution)/shard_map/pallas_call | solution.py:641
  701.8 1.3 reduce.3
  703.1 5.1 copy.81
  709.2 3.4 copy.82
  (159 shorter events, 22.1 us)
Async XLA Ops:
  7.2 6.6 copy-start.17
  7.2 7.4 %copy-start.20 = (f32[256,6]{0,1:T(8,128)S(1)}, f32[256,6]{0,1:T(8,128)}, u32[]{:S(2)}) copy-start(f32[256,6]{0,1:T(8,128)} %param.31) | copy-start | bytes 18436
  7.2 7.3 %copy-start.12 = (f32[256,2048]{1,0:T(8,128)S(1)}, f32[256,2048]{1,0:T(8,128)}, u32[]{:S(2)}) copy-start(f32[256,2048]{1,0:T(8,128)} %refs_13_.1) | copy-start | bytes 6291460
  7.3 309.9 %all-gather.2.cloned.1.call-start = ((), (), s32[]{:S(2)}) async-start(), calls=%async_computation.1 | async-start | bytes 9437184 | tf_op jit(solution)/shard_map/all_gather | solution.py:841
  194.5 474.6 %reduce-scatter.2.cloned.1.call-start = ((), (), s32[]{:S(2)}) async-start(), calls=%async_computation.2 | async-start | bytes 9437184 | tf_op jit(solution)/shard_map/reduce_scatter | solution.py:897
  194.5 4.5 copy-start.8
  196.2 4.2 copy-start.27
  196.2 4.2 copy-start.29
  196.2 4.1 copy-start.23
  199.0 12.1 %copy-start.24 = (f32[1024]{0:T(1024)}, f32[1024]{0:T(1024)S(1)}, u32[]{:S(2)}) copy-start(f32[1024]{0:T(1024)S(1)} %broadcast_multiply_fusion) | copy-start | bytes 12292
  200.3 10.9 %copy-start.31 = (f32[1024]{0:T(1024)}, f32[1024]{0:T(1024)S(1)}, u32[]{:S(2)}) copy-start(f32[1024]{0:T(1024)S(1)} %add_rsqrt_fusion) | copy-start | bytes 12292
  211.2 9.7 %copy-start = (bf16[1024,1536]{1,0:T(8,128)(2,1)}, bf16[1024,1536]{1,0:T(8,128)(2,1)S(1)}, u32[]{:S(2)}) copy-start(bf16[1024,1536]{1,0:T(8,128)(2,1)S(1)} %add_convert_fusion.query_ref.key_ref.value_ref) | copy-start | bytes 9437188
  221.3 7.1 copy-start.18
  224.2 7.0 copy-start.33
  224.2 4.2 collective-permute-start
  229.7 47.8 %collective-permute-start.1 = (bf16[512,2048]{1,0:T(8,128)(2,1)S(1)}, bf16[512,2048]{1,0:T(8,128)(2,1)}, u32[]{:S(2)}, u32[]{:S(2)}) collective-permute-start(bf16[512,2048]{1,0:T(8,128)(2,1)S(1)} %add_convert_fusion.5), channel_id=1, source_target_pairs={{0,2},{1,3},{2,0},{3,1},{4,6},{5,7},{6,4},{7,5},{8,10},{9,11},{10,... | collective-permute-start | bytes 6291464 | tf_op jit(solution)/shard_map/ppermute | solution.py:31
  241.3 62.1 %copy-start.14 = (bf16[1024,2048]{1,0:T(8,128)(2,1)}, bf16[1024,2048]{1,0:T(8,128)(2,1)S(1)}, u32[]{:S(2)}) copy-start(bf16[1024,2048]{1,0:T(8,128)(2,1)S(1)} %pad_maximum_fusion) | copy-start | bytes 12582916
  241.3 38.7 %copy-start.9 = (bf16[1024,2048]{1,0:T(8,128)(2,1)S(1)}, bf16[1024,2048]{1,0:T(8,128)(2,1)}, u32[]{:S(2)}) copy-start(bf16[1024,2048]{1,0:T(8,128)(2,1)} %param.26) | copy-start | bytes 12582916
  277.5 10.8 %slice-start.2 = ((s8[8388608]{0:T(1024)(128)(4,1)}), s8[4194304]{0:T(1024)(128)(4,1)S(1)}, s32[]{:S(2)}) async-start(s8[8388608]{0:T(1024)(128)(4,1)} %bitcast.137), calls=%async_computation.5 | async-start | bytes 8388608
  280.1 8.3 %slice-start.3 = ((s8[8388608]{0:T(1024)(128)(4,1)}), s8[4194304]{0:T(1024)(128)(4,1)S(1)}, s32[]{:S(2)}) async-start(s8[8388608]{0:T(1024)(128)(4,1)} %bitcast.137), calls=%async_computation.6 | async-start | bytes 8388608
  282.8 5.5 copy-start.26
  284.2 4.2 collective-permute-start.2
  288.3 15.1 %copy-start.36 = (bf16[512,2048]{1,0:T(8,128)(2,1)}, bf16[512,2048]{1,0:T(8,128)(2,1)S(1)}, u32[]{:S(2)}) copy-start(bf16[512,2048]{1,0:T(8,128)(2,1)S(1)} %collective-permute-done.2) | copy-start | bytes 6291460
  335.4 10.7 %copy-start.39 = (bf16[1024,2048]{1,0:T(8,128)(2,1)}, bf16[1024,2048]{1,0:T(8,128)(2,1)S(1)}, u32[]{:S(2)}) copy-start(bf16[1024,2048]{1,0:T(8,128)(2,1)S(1)} %get-tuple-element.193) | copy-start | bytes 12582916
  335.4 10.7 %copy-start.34 = (bf16[2048,2048]{1,0:T(8,128)(2,1)S(1)}, bf16[2048,2048]{1,0:T(8,128)(2,1)}, u32[]{:S(2)}) copy-start(bf16[2048,2048]{1,0:T(8,128)(2,1)} %all-gather.2.cloned.1.call-done) | copy-start | bytes 25165828
  335.5 10.7 %copy-start.38 = (bf16[1024,2048]{1,0:T(8,128)(2,1)S(1)}, bf16[1024,2048]{1,0:T(8,128)(2,1)}, u32[]{:S(2)}) copy-start(bf16[1024,2048]{1,0:T(8,128)(2,1)} %get-tuple-element.190) | copy-start | bytes 12582916
  346.1 6.8 collective-permute-start.4
  352.3 24.8 %collective-permute-start.3 = (bf16[512,2048]{1,0:T(8,128)(2,1)}, bf16[512,2048]{1,0:T(8,128)(2,1)}, u32[]{:S(2)}, u32[]{:S(2)}) collective-permute-start(bf16[512,2048]{1,0:T(8,128)(2,1)} %convolution_convert_fusion.6), channel_id=1, source_target_pairs={{0,1},{1,0},{2,3},{3,2},{4,5},{5,4},{6,7},{7,6},{8,9},{9,8},{10,11... | collective-permute-start | bytes 6291464 | tf_op jit(solution)/shard_map/ppermute | solution.py:31
  352.9 10.8 %copy-start.37 = (bf16[512,2048]{1,0:T(8,128)(2,1)S(1)}, bf16[512,2048]{1,0:T(8,128)(2,1)}, u32[]{:S(2)}) copy-start(bf16[512,2048]{1,0:T(8,128)(2,1)} %copy-done.36) | copy-start | bytes 6291460
  352.9 24.2 %slice-start = ((s8[8388608]{0:T(1024)(128)(4,1)}), s8[4194304]{0:T(1024)(128)(4,1)S(1)}, s32[]{:S(2)}) async-start(s8[8388608]{0:T(1024)(128)(4,1)} %bitcast.135), calls=%async_computation.3 | async-start | bytes 8388608
  362.2 15.0 %slice-start.1 = ((s8[8388608]{0:T(1024)(128)(4,1)}), s8[4194304]{0:T(1024)(128)(4,1)S(1)}, s32[]{:S(2)}) async-start(s8[8388608]{0:T(1024)(128)(4,1)} %bitcast.135), calls=%async_computation.4 | async-start | bytes 8388608
  362.2 47.6 %collective-permute-start.5 = (bf16[512,2048]{1,0:T(8,128)(2,1)S(1)}, bf16[512,2048]{1,0:T(8,128)(2,1)S(1)}, u32[]{:S(2)}, u32[]{:S(2)}) collective-permute-start(bf16[512,2048]{1,0:T(8,128)(2,1)S(1)} %add_convert_fusion.2), channel_id=1, source_target_pairs={{0,2},{1,3},{2,0},{3,1},{4,6},{5,7},{6,4},{7,5},{8,10},{9,11},{10,... | collective-permute-start | bytes 6291464 | tf_op jit(solution)/shard_map/ppermute | solution.py:31
  384.8 25.8 %copy-start.6 = (f32[512,2048]{1,0:T(8,128)S(1)}, f32[512,2048]{1,0:T(8,128)}, u32[]{:S(2)}) copy-start(f32[512,2048]{1,0:T(8,128)} %copy-done.5) | copy-start | bytes 12582916
  415.1 2.4 copy-start.22
  415.1 3.1 copy-start.21
  417.5 9.0 %copy-start.15 = (bf16[512,2048]{1,0:T(8,128)(2,1)}, bf16[512,2048]{1,0:T(8,128)(2,1)S(1)}, u32[]{:S(2)}) copy-start(bf16[512,2048]{1,0:T(8,128)(2,1)S(1)} %convert_element_type.173) | copy-start | bytes 6291460
  417.5 4.4 collective-permute-start.6
  444.2 2.7 slice-start.5
  446.9 4.7 copy-start.16
  446.9 4.7 copy-start.19
  450.8 15.9 %collective-permute-start.7 = (bf16[512,2048]{1,0:T(8,128)(2,1)S(1)}, bf16[512,2048]{1,0:T(8,128)(2,1)S(1)}, u32[]{:S(2)}, u32[]{:S(2)}) collective-permute-start(bf16[512,2048]{1,0:T(8,128)(2,1)S(1)} %convolution_convert_fusion.4), channel_id=1, source_target_pairs={{0,1},{1,0},{2,3},{3,2},{4,5},{5,4},{6,7},{7,6},{8,9},{9,8},{10,11... | collective-permute-start | bytes 6291464 | tf_op jit(solution)/shard_map/ppermute | solution.py:31
  451.6 5.6 copy-start.10
  451.6 5.6 copy-start.25
  451.6 5.6 copy-start.28
  451.6 5.5 copy-start.30
  451.6 5.5 copy-start.32
  472.5 196.6 %copy-start.2 = (f32[8,128]{1,0:T(8,128)S(1)}, f32[8,128]{1,0:T(8,128)}, u32[]{:S(2)}) copy-start(f32[8,128]{1,0:T(8,128)} %broadcast_in_dim.68.refs_8_.total_ref) | copy-start | bytes 12292
  703.1 6.2 copy-start.13
  (8 other events, 13.5 us)
Sparse Core Ops, SparseCore 0:
  194.6 122.5 all-gather.1
  353.0 163.8 reduce-scatter.1
